TPU v7x, 32 devices: a whole 2x2x4 slice. The times are simulated.
32 devices in a mesh: dp: 16 (over z, x, core), mp: 2 (over y).
Axes of the slice: x: 2, y: 2, z: 4, core: 2. Of those that a mesh axis runs over, the one named last changes fastest.
Arguments:
- lang: bfloat16 [15360, 768], P(('dp', 'mp')), may hold values from -6 to 6
- vision: bfloat16 [27648, 768], P(('dp', 'mp')), may hold values from -6 to 6
- region_count: int32 [768], P('dp'), may hold values from 10 to 36, as said below
- att_in: bfloat16 [3, 3, 768, 768], P(None, None, None, 'mp'), may hold values from -0.3125 to 0.3125
- att_in_bias: bfloat16 [3, 2, 768], P(None, None, 'mp'), may hold values from -3 to 3
- att_out: bfloat16 [3, 768, 768], P(None, 'mp'), may hold values from -0.5 to 0.5
- att_row_bias: bfloat16 [3, 2, 768], replicated, may hold values from -3 to 3
- att_gain: bfloat16 [3, 768], replicated, may hold values from 0.25 to 1.75
- ffn_up: bfloat16 [2, 768, 3072], P(None, None, 'mp'), may hold values from -0.21875 to 0.21875
- ffn_up_bias: bfloat16 [2, 3072], P(None, 'mp'), may hold values from -3 to 3
- ffn_down: bfloat16 [2, 3072, 768], P(None, 'mp'), may hold values from -0.15625 to 0.15625
- ffn_row_bias: bfloat16 [2, 2, 768], replicated, may hold values from -3 to 3
- ffn_gain: bfloat16 [2, 768], replicated, may hold values from 0.25 to 1.75
- cot_lang: bfloat16 [15360, 768], P(('dp', 'mp')), may hold values from -6 to 6
- cot_vision: bfloat16 [27648, 768], P(('dp', 'mp')), may hold values from -6 to 6
Outputs:
- out_lang: float32 [15360, 768], P(('dp', 'mp'))
- out_vision: float32 [27648, 768], P(('dp', 'mp'))
- grad_lang: float32 [15360, 768], P(('dp', 'mp'))
- grad_vision: float32 [27648, 768], P(('dp', 'mp'))
- grad_att_in: float32 [3, 3, 768, 768], P(None, None, 'dp', 'mp')
- grad_att_in_bias: float32 [3, 2, 768], replicated
- grad_att_out: float32 [3, 768, 768], P(None, 'mp', 'dp')
- grad_att_row_bias: float32 [3, 2, 768], replicated
- grad_att_gain: float32 [3, 768], replicated
- grad_ffn_up: float32 [2, 768, 3072], P(None, 'dp', 'mp')
- grad_ffn_up_bias: float32 [2, 3072], replicated
- grad_ffn_down: float32 [2, 3072, 768], P(None, 'mp', 'dp')
- grad_ffn_row_bias: float32 [2, 2, 768], replicated
- grad_ffn_gain: float32 [2, 768], replicated
Inputs may be any that keep to these rules, and one draw needn't show every extreme that they name: `region_count`: real regions of each item; its slots from that count up to 36 are padding. Some item has 36 and some has 10.
All inputs are finite; a program needn't handle non-finite values.
Results may differ from a plain program's by a relative error of at most 0.029.
The roundings to bfloat16 on the way count: a program that leaves them out, or rounds other values in their place, can miss the bound.
Values may be sent and summed in bfloat16 or wider, within the bound.
No kernel may reach another device: no remote copies, remote signals or barrier semaphores. Data moves between devices by JAX's collectives and lax.ppermute only.
A program may use at most 320 MiB of HBM per device.

v0:
```python
from functools import partial

import jax
import jax.numpy as jnp
from jax import lax
from jax.sharding import PartitionSpec as P

D = 768
FF = 3072
WORDS = 20
REGIONS = 36
HEAD_DIM = 64


NORM_EPSILON = 1e-06
MASK_FILL = -1000000000.0


def shortened(value):

    def short(part):
        return part.astype(jnp.bfloat16) if part.dtype == jnp.float32 else part

    return jax.tree.map(short, value)


def gather_rows(stream_pair):
    return jax.tree.map(
        lambda part, own: part.astype(own.dtype),
        lax.all_gather(shortened(stream_pair), "mp", axis=0, tiled=True),
        stream_pair,
    )


def sum_rows(partials):
    return lax.psum_scatter(partials, "mp", scatter_dimension=0, tiled=True)


def gather_grads(grad_pair):
    return jax.tree.map(
        lambda part, own: part.astype(own.dtype),
        lax.all_gather(shortened(grad_pair), "mp", axis=0, tiled=True),
        grad_pair,
    )


def sum_inputs(partials):
    return lax.psum_scatter(partials, "mp", scatter_dimension=0, tiled=True)


def norm_forward(summed, gain, shift):
    row_mean = jnp.mean(summed, axis=-1, keepdims=True)
    centred = summed - row_mean
    spread = jnp.mean(centred * centred, axis=-1, keepdims=True)
    inv_scale = lax.rsqrt(spread + NORM_EPSILON)
    normed = centred * inv_scale
    return (normed * gain.astype(jnp.float32) + shift, (normed, inv_scale))


def norm_backward(grad_out, saved, gain):
    normed, inv_scale = saved
    grad_normed = grad_out * gain.astype(jnp.float32)
    mean_first = jnp.mean(grad_normed, axis=-1, keepdims=True)
    mean_second = jnp.mean(grad_normed * normed, axis=-1, keepdims=True)
    grad_total = inv_scale * (grad_normed - mean_first - normed * mean_second)
    return (grad_total, jnp.sum(grad_out * normed, axis=0), jnp.sum(grad_out, axis=0))


def project(row_data, weight, in_bias):
    projected = jnp.einsum("rd,kde->rke", row_data, weight, preferred_element_type=jnp.float32)
    queries = (projected[:, 0] + in_bias[0].astype(jnp.float32)).astype(jnp.bfloat16)
    key_rows = projected[:, 1].astype(jnp.bfloat16)
    values = (projected[:, 2] + in_bias[1].astype(jnp.float32)).astype(jnp.bfloat16)
    return (queries, key_rows, values)


def split_heads(matrix, item_count):
    return matrix.reshape(
        item_count, matrix.shape[0] // item_count, matrix.shape[1] // HEAD_DIM, HEAD_DIM
    )


def score_block(queries, key_rows, key_ok):
    item_count = key_ok.shape[0]
    scores = jnp.einsum(
        "nahd,nchd->nhac",
        split_heads(queries, item_count),
        split_heads(key_rows, item_count),
        preferred_element_type=jnp.float32,
    )
    scores = scores * HEAD_DIM ** (-0.5)
    return jnp.where(key_ok[:, None, None, :], scores, MASK_FILL)


def attend_forward(queries, key_rows, values, key_ok):
    item_count = key_ok.shape[0]
    scores = score_block(queries, key_rows, key_ok)
    row_max = jnp.max(scores, axis=-1, keepdims=True)
    exp_total = jnp.sum(jnp.exp(scores - row_max), axis=-1, keepdims=True)
    log_total = row_max + jnp.log(exp_total)
    probability = jnp.exp(scores - log_total).astype(jnp.bfloat16)
    mixed_rows = jnp.einsum(
        "nhac,nchd->nahd",
        probability,
        split_heads(values, item_count),
        preferred_element_type=jnp.float32,
    )
    return (mixed_rows.reshape(queries.shape).astype(jnp.bfloat16), log_total)


def attend_backward(queries, key_rows, values, log_total, key_ok, grad_mixed):
    item_count = key_ok.shape[0]
    scores = score_block(queries, key_rows, key_ok)
    probability = jnp.exp(scores - log_total)
    grad_heads = split_heads(grad_mixed, item_count)
    grad_probs = jnp.einsum(
        "nahd,nchd->nhac",
        grad_heads,
        split_heads(values, item_count),
        preferred_element_type=jnp.float32,
    )
    grad_values = jnp.einsum(
        "nhac,nahd->nchd",
        probability.astype(jnp.bfloat16),
        grad_heads,
        preferred_element_type=jnp.float32,
    )
    centre = jnp.sum(grad_probs * probability, axis=-1, keepdims=True)
    grad_scores = (probability * (grad_probs - centre)).astype(jnp.bfloat16)
    grad_queries = jnp.einsum(
        "nhac,nchd->nahd",
        grad_scores,
        split_heads(key_rows, item_count),
        preferred_element_type=jnp.float32,
    ) * HEAD_DIM ** (-0.5)
    grad_keys = jnp.einsum(
        "nhac,nahd->nchd",
        grad_scores,
        split_heads(queries, item_count),
        preferred_element_type=jnp.float32,
    ) * HEAD_DIM ** (-0.5)
    return (
        grad_queries.reshape(queries.shape).astype(jnp.bfloat16),
        grad_keys.reshape(key_rows.shape).astype(jnp.bfloat16),
        grad_values.reshape(values.shape).astype(jnp.bfloat16),
    )


def pick_context(lang_proj, vision_proj, is_cross, word_ok, region_ok):
    if is_cross:
        return (vision_proj, lang_proj, region_ok, word_ok)
    return (lang_proj, vision_proj, word_ok, region_ok)


def attention_forward(low_pair, in_pair, bias_pair, out_pair, is_cross, word_ok, region_ok):
    lang_rows, vision_rows = gather_rows(low_pair)
    lang_proj = project(lang_rows, in_pair[0], bias_pair[0])
    vision_proj = project(vision_rows, in_pair[1], bias_pair[1])
    lang_ctx, vision_ctx, lang_ok, vision_ok = pick_context(
        lang_proj, vision_proj, is_cross, word_ok, region_ok
    )
    lang_mixed, lang_log = attend_forward(lang_proj[0], lang_ctx[1], lang_ctx[2], lang_ok)
    vision_mixed, vision_log = attend_forward(
        vision_proj[0], vision_ctx[1], vision_ctx[2], vision_ok
    )
    partials = (
        jnp.dot(lang_mixed, out_pair[0], preferred_element_type=jnp.float32),
        jnp.dot(vision_mixed, out_pair[1], preferred_element_type=jnp.float32),
    )
    kept = (
        lang_rows,
        vision_rows,
        lang_proj,
        vision_proj,
        lang_mixed,
        vision_mixed,
        lang_log,
        vision_log,
    )
    return (sum_rows(partials), kept)


def attention_backward(grad_pair, kept, in_pair, out_pair, is_cross, word_ok, region_ok):
    (
        lang_rows,
        vision_rows,
        lang_proj,
        vision_proj,
        lang_mixed,
        vision_mixed,
        lang_log,
        vision_log,
    ) = kept
    lang_grad, vision_grad = gather_grads(
        (grad_pair[0].astype(jnp.bfloat16), grad_pair[1].astype(jnp.bfloat16))
    )
    out_grads = (
        jnp.einsum("re,rd->ed", lang_mixed, lang_grad, preferred_element_type=jnp.float32),
        jnp.einsum("re,rd->ed", vision_mixed, vision_grad, preferred_element_type=jnp.float32),
    )
    lang_dmix = jnp.einsum(
        "rd,ed->re", lang_grad, out_pair[0], preferred_element_type=jnp.float32
    ).astype(jnp.bfloat16)
    vision_dmix = jnp.einsum(
        "rd,ed->re", vision_grad, out_pair[1], preferred_element_type=jnp.float32
    ).astype(jnp.bfloat16)
    lang_ctx, vision_ctx, lang_ok, vision_ok = pick_context(
        lang_proj, vision_proj, is_cross, word_ok, region_ok
    )
    lang_back = attend_backward(
        lang_proj[0], lang_ctx[1], lang_ctx[2], lang_log, lang_ok, lang_dmix
    )
    vision_back = attend_backward(
        vision_proj[0], vision_ctx[1], vision_ctx[2], vision_log, vision_ok, vision_dmix
    )
    if is_cross:
        lang_stack = jnp.stack((lang_back[0], vision_back[1], vision_back[2]), axis=1)
        vision_stack = jnp.stack((vision_back[0], lang_back[1], lang_back[2]), axis=1)
    else:
        lang_stack = jnp.stack(lang_back, axis=1)
        vision_stack = jnp.stack(vision_back, axis=1)
    in_grads = (
        jnp.einsum("rd,rke->kde", lang_rows, lang_stack, preferred_element_type=jnp.float32),
        jnp.einsum("rd,rke->kde", vision_rows, vision_stack, preferred_element_type=jnp.float32),
    )
    bias_grads = (
        jnp.sum(lang_stack[:, 0::2], axis=0, dtype=jnp.float32),
        jnp.sum(vision_stack[:, 0::2], axis=0, dtype=jnp.float32),
    )
    partials = (
        jnp.einsum("rke,kde->rd", lang_stack, in_pair[0], preferred_element_type=jnp.float32),
        jnp.einsum("rke,kde->rd", vision_stack, in_pair[1], preferred_element_type=jnp.float32),
    )
    return (sum_inputs(partials), in_grads, out_grads, bias_grads)


def ffn_forward(low_pair, up_pair, up_bias_pair, down_pair):
    row_pair = gather_rows(low_pair)
    hidden_pair = tuple(
        (
            jnp.dot(row_data, weight, preferred_element_type=jnp.float32)
            + in_bias.astype(jnp.float32)
            for row_data, weight, in_bias in zip(row_pair, up_pair, up_bias_pair)
        )
    )
    act_pair = tuple(
        (jax.nn.gelu(hidden, approximate=False).astype(jnp.bfloat16) for hidden in hidden_pair)
    )
    partials = tuple(
        (
            jnp.dot(activated, weight, preferred_element_type=jnp.float32)
            for activated, weight in zip(act_pair, down_pair)
        )
    )
    return (sum_rows(partials), (row_pair, hidden_pair, act_pair))


def gelu_back(hidden, grad_full, weight):
    act_grad = jnp.einsum("rd,fd->rf", grad_full, weight, preferred_element_type=jnp.float32)
    pull_back = jax.vjp(partial(jax.nn.gelu, approximate=False), hidden)[1]
    return pull_back(act_grad)[0].astype(jnp.bfloat16)


def ffn_backward(grad_pair, kept, up_pair, down_pair):
    row_pair, hidden_pair, act_pair = kept
    grad_full_pair = gather_grads(
        (grad_pair[0].astype(jnp.bfloat16), grad_pair[1].astype(jnp.bfloat16))
    )
    down_grads = tuple(
        (
            jnp.einsum("rf,rd->fd", activated, grad_full, preferred_element_type=jnp.float32)
            for activated, grad_full in zip(act_pair, grad_full_pair)
        )
    )
    hidden_grads = tuple(
        (
            gelu_back(hidden, grad_full, weight)
            for hidden, grad_full, weight in zip(hidden_pair, grad_full_pair, down_pair)
        )
    )
    up_grads = tuple(
        (
            jnp.einsum("rd,rf->df", row_data, hidden_grad, preferred_element_type=jnp.float32)
            for row_data, hidden_grad in zip(row_pair, hidden_grads)
        )
    )
    up_bias_grads = tuple(
        (jnp.sum(hidden_grad, axis=0, dtype=jnp.float32) for hidden_grad in hidden_grads)
    )
    partials = tuple(
        (
            jnp.einsum("rf,df->rd", hidden_grad, weight, preferred_element_type=jnp.float32)
            for hidden_grad, weight in zip(hidden_grads, up_pair)
        )
    )
    return (sum_inputs(partials), up_grads, down_grads, up_bias_grads)


def per_device(
    lang,
    vision,
    region_count,
    att_in,
    att_in_bias,
    att_out,
    att_row_bias,
    att_gain,
    ffn_up,
    ffn_up_bias,
    ffn_down,
    ffn_row_bias,
    ffn_gain,
    cot_lang,
    cot_vision,
):
    item_count = region_count.shape[0]
    mp_rank = lax.axis_index("mp")
    slot_index = jnp.arange(REGIONS, dtype=jnp.int32)
    region_ok = slot_index[None, :] < region_count[:, None]
    word_ok = jnp.ones((item_count, WORDS), dtype=bool)
    vision_count = vision.shape[0]
    row_ok = lax.dynamic_slice_in_dim(region_ok.reshape(-1), mp_rank * vision_count, vision_count)
    row_bias = att_row_bias.astype(jnp.float32)
    ffn_bias = ffn_row_bias.astype(jnp.float32)
    cross_in = (att_in[0], att_in[0])
    cross_out = (att_out[0], att_out[0])
    branches, cross_kept = attention_forward(
        (lang, vision),
        cross_in,
        (att_in_bias[0], att_in_bias[0]),
        cross_out,
        True,
        word_ok,
        region_ok,
    )
    lang_one, lang_norm_a = norm_forward(
        lang.astype(jnp.float32) + branches[0] + row_bias[0, 0], att_gain[0], row_bias[0, 1]
    )
    vision_one, vision_norm_a = norm_forward(
        vision.astype(jnp.float32) + branches[1] + row_bias[0, 0], att_gain[0], row_bias[0, 1]
    )
    self_in = (att_in[1], att_in[2])
    self_out = (att_out[1], att_out[2])
    branches, self_kept = attention_forward(
        (lang_one.astype(jnp.bfloat16), vision_one.astype(jnp.bfloat16)),
        self_in,
        (att_in_bias[1], att_in_bias[2]),
        self_out,
        False,
        word_ok,
        region_ok,
    )
    lang_two, lang_norm_b = norm_forward(
        lang_one + branches[0] + row_bias[1, 0], att_gain[1], row_bias[1, 1]
    )
    vision_two, vision_norm_b = norm_forward(
        vision_one + branches[1] + row_bias[2, 0], att_gain[2], row_bias[2, 1]
    )
    up_pair = (ffn_up[0], ffn_up[1])
    down_pair = (ffn_down[0], ffn_down[1])
    branches, ffn_kept = ffn_forward(
        (lang_two.astype(jnp.bfloat16), vision_two.astype(jnp.bfloat16)),
        up_pair,
        (ffn_up_bias[0], ffn_up_bias[1]),
        down_pair,
    )
    out_lang, lang_norm_c = norm_forward(
        lang_two + branches[0] + ffn_bias[0, 0], ffn_gain[0], ffn_bias[0, 1]
    )
    out_vision, vision_norm_c = norm_forward(
        vision_two + branches[1] + ffn_bias[1, 0], ffn_gain[1], ffn_bias[1, 1]
    )
    lang_total, lang_gain_c, lang_shift_c = norm_backward(
        cot_lang.astype(jnp.float32), lang_norm_c, ffn_gain[0]
    )
    vision_total, vision_gain_c, vision_shift_c = norm_backward(
        cot_vision.astype(jnp.float32) * row_ok[:, None].astype(jnp.float32),
        vision_norm_c,
        ffn_gain[1],
    )
    ffn_rows_grad = jnp.stack(
        (
            jnp.stack((jnp.sum(lang_total, axis=0), lang_shift_c)),
            jnp.stack((jnp.sum(vision_total, axis=0), vision_shift_c)),
        )
    )
    ffn_gain_grad = jnp.stack((lang_gain_c, vision_gain_c))
    input_pair, up_grads, down_grads, up_bias_grads = ffn_backward(
        (lang_total, vision_total), ffn_kept, up_pair, down_pair
    )
    up_stack = jnp.stack(up_grads)
    down_stack = jnp.stack(down_grads)
    lang_back = lang_total + input_pair[0]
    vision_back = vision_total + input_pair[1]
    lang_total, lang_gain_b, lang_shift_b = norm_backward(lang_back, lang_norm_b, att_gain[1])
    vision_total, vision_gain_b, vision_shift_b = norm_backward(
        vision_back, vision_norm_b, att_gain[2]
    )
    lang_rows_b = jnp.stack((jnp.sum(lang_total, axis=0), lang_shift_b))
    vision_rows_b = jnp.stack((jnp.sum(vision_total, axis=0), vision_shift_b))
    input_pair, in_grads, out_grads, self_bias_grads = attention_backward(
        (lang_total, vision_total), self_kept, self_in, self_out, False, word_ok, region_ok
    )
    self_in_stack = jnp.stack(in_grads)
    self_out_stack = jnp.stack(out_grads)
    lang_back = lang_total + input_pair[0]
    vision_back = vision_total + input_pair[1]
    lang_total, lang_gain_a, lang_shift_a = norm_backward(lang_back, lang_norm_a, att_gain[0])
    vision_total, vision_gain_a, vision_shift_a = norm_backward(
        vision_back, vision_norm_a, att_gain[0]
    )
    cross_rows = jnp.stack(
        (jnp.sum(lang_total, axis=0) + jnp.sum(vision_total, axis=0), lang_shift_a + vision_shift_a)
    )
    input_pair, in_grads, out_grads, cross_bias_grads = attention_backward(
        (lang_total, vision_total), cross_kept, cross_in, cross_out, True, word_ok, region_ok
    )
    cross_in_sum = in_grads[0] + in_grads[1]
    cross_out_sum = out_grads[0] + out_grads[1]
    grad_lang = lang_total + input_pair[0]
    grad_vision = vision_total + input_pair[1]
    att_in_grad = jnp.concatenate((cross_in_sum[None], self_in_stack), axis=0)
    att_out_grad = jnp.concatenate((cross_out_sum[None], self_out_stack), axis=0)
    att_in_grad, att_out_grad, up_stack, down_stack = (
        lax.psum_scatter(att_in_grad, "dp", scatter_dimension=2, tiled=True),
        lax.psum_scatter(att_out_grad, "dp", scatter_dimension=2, tiled=True),
        lax.psum_scatter(up_stack, "dp", scatter_dimension=1, tiled=True),
        lax.psum_scatter(down_stack, "dp", scatter_dimension=2, tiled=True),
    )
    head_width = att_in_bias.shape[-1]
    in_bias_local = jnp.stack(
        (cross_bias_grads[0] + cross_bias_grads[1], self_bias_grads[0], self_bias_grads[1])
    )
    in_bias_full = lax.dynamic_update_slice(
        jnp.zeros((3, 2, D), jnp.float32), in_bias_local, (0, 0, mp_rank * head_width)
    )
    unit_width = ffn_up_bias.shape[-1]
    up_bias_full = lax.dynamic_update_slice(
        jnp.zeros((2, FF), jnp.float32), jnp.stack(up_bias_grads), (0, mp_rank * unit_width)
    )
    att_rows_grad = jnp.stack((cross_rows, lang_rows_b, vision_rows_b))
    att_gain_grad = jnp.stack((lang_gain_a + vision_gain_a, lang_gain_b, vision_gain_b))
    summed = lax.psum(
        (in_bias_full, up_bias_full, att_rows_grad, att_gain_grad, ffn_rows_grad, ffn_gain_grad),
        ("dp", "mp"),
    )
    return (
        out_lang,
        out_vision,
        grad_lang,
        grad_vision,
        att_in_grad,
        summed[0],
        att_out_grad,
        summed[2],
        summed[3],
        up_stack,
        summed[1],
        down_stack,
        summed[4],
        summed[5],
    )


def solution(mesh):
    return jax.shard_map(
        per_device,
        mesh=mesh,
        in_specs=(
            P(("dp", "mp"), None),
            P(("dp", "mp"), None),
            P("dp"),
            P(None, None, None, "mp"),
            P(None, None, "mp"),
            P(None, "mp", None),
            P(),
            P(),
            P(None, None, "mp"),
            P(None, "mp"),
            P(None, "mp", None),
            P(),
            P(),
            P(("dp", "mp"), None),
            P(("dp", "mp"), None),
        ),
        out_specs=(
            P(("dp", "mp"), None),
            P(("dp", "mp"), None),
            P(("dp", "mp"), None),
            P(("dp", "mp"), None),
            P(None, None, "dp", "mp"),
            P(),
            P(None, "mp", "dp"),
            P(),
            P(),
            P(None, "dp", "mp"),
            P(),
            P(None, "mp", "dp"),
            P(),
            P(),
        ),
        check_vma=False,
    )
```

profile of v0, /device:TPU:0, one launch (start us, length us, event | category | flops | bytes accessed | tf_op | source)
XLA Modules:
  0.0 1964.4 jit_solution(10092145185197159594)
XLA Ops:
  11.0 27.4 %all-gather.15.cloned.1.call-done = bf16[960,768]{1,0:T(8,128)(2,1)} async-done(((bf16[480,768]{1,0:T(8,128)(2,1)}), bf16[960,768]{1,0:T(8,128)(2,1)}) %all-gather.15.cloned.1.call-update) | async-done | bytes 1474576 | tf_op jit(solution)/shard_map/all_gather | solution.py:30
  52.2 27.1 %all-gather.13.cloned.1.call-done = bf16[1728,768]{1,0:T(8,128)(2,1)} async-done(((bf16[864,768]{1,0:T(8,128)(2,1)}), bf16[1728,768]{1,0:T(8,128)(2,1)}) %all-gather.13.cloned.1.call-update) | async-done | bytes 2654224 | tf_op jit(solution)/shard_map/all_gather | solution.py:30
  79.3 5.9 fusion.25
  91.4 4.3 fusion.18
  98.7 5.6 squeeze.37
  134.3 22.5 %reduce-scatter.14.cloned.1.call-done = f32[480,768]{1,0:T(8,128)} async-done(((f32[960,768]{1,0:T(8,128)}), f32[480,768]{1,0:T(8,128)}) %reduce-scatter.14.cloned.1.call-update) | async-done | bytes 1474576 | tf_op jit(solution)/shard_map/reduce_scatter | solution.py:36
  172.9 5.3 fusion.168
  179.0 8.2 all-gather.17.cloned.1.call-done
  195.9 60.0 %reduce-scatter.20.cloned.1.call-done = f32[864,768]{1,0:T(8,128)} async-done(((f32[1728,768]{1,0:T(8,128)}), f32[864,768]{1,0:T(8,128)}) %reduce-scatter.20.cloned.1.call-update) | async-done | bytes 2654224 | tf_op jit(solution)/shard_map/reduce_scatter | solution.py:36
  290.1 9.9 all-gather.21.cloned.1.call-done
  300.0 5.9 fusion.21
  310.8 5.2 convert_element_type.536
  316.0 5.3 fusion.207
  321.3 5.6 squeeze.100
  326.9 5.6 squeeze.49
  352.2 8.0 convert_bitcast_fusion.2
  362.7 5.5 convert_element_type.540
  368.2 5.3 fusion.161
  374.5 18.6 multiply_convert_fusion.6
  394.8 5.7 fusion.39
  401.0 42.3 %reduce-scatter.22.cloned.1.call-done = f32[864,768]{1,0:T(8,128)} async-done(((f32[1728,768]{1,0:T(8,128)}), f32[864,768]{1,0:T(8,128)}) %reduce-scatter.22.cloned.1.call-update) | async-done | bytes 2654224 | tf_op jit(solution)/shard_map/reduce_scatter | solution.py:36
  449.3 37.5 %reduce-scatter.18.cloned.1.call-done = f32[480,768]{1,0:T(8,128)} async-done(((f32[960,768]{1,0:T(8,128)}), f32[480,768]{1,0:T(8,128)}) %reduce-scatter.18.cloned.1.call-update) | async-done | bytes 1474576 | tf_op jit(solution)/shard_map/reduce_scatter | solution.py:36
  494.8 33.5 %all-gather.23.cloned.1.call-done = bf16[1728,768]{1,0:T(8,128)(2,1)} async-done(((bf16[864,768]{1,0:T(8,128)(2,1)}), bf16[1728,768]{1,0:T(8,128)(2,1)}) %all-gather.23.cloned.1.call-update) | async-done | bytes 2654224 | tf_op jit(solution)/shard_map/all_gather | solution.py:30
  528.3 29.7 %multiply_convert_fusion = (bf16[1728,1536]{1,0:T(8,128)(2,1)S(1)}, f32[1728,1536]{1,0:T(8,128)}, f32[1728,1536]{1,0:T(8,128)}) fusion(f32[1536]{0:T(1024)S(1)} %get-tuple-element.90, bf16[1728,768]{1,0:T(8,128)(2,1)} %all-gather.23.cloned.1.call-done, bf16[2,768,1536]{2,1,0:T(8,128)(2,1)} %param.23), kind=kOutput, calls=%fused_computation.5 | convolution fusion | flops 4252041216 | bytes 31561728 | tf_op jit(solution)/shard_map/dot_general | solution.py:241
  560.3 5.9 fusion.31
  566.5 10.5 convert_reduce_fusion.1
  583.6 49.3 %reduce-scatter.24.cloned.1.call-done = f32[864,768]{1,0:T(8,128)} async-done(((f32[1728,768]{1,0:T(8,128)}), f32[864,768]{1,0:T(8,128)}) %reduce-scatter.24.cloned.1.call-update) | async-done | bytes 2654224 | tf_op jit(solution)/shard_map/reduce_scatter | solution.py:36
  644.5 31.8 %reduce-scatter.26.cloned.1.call-done = f32[480,768]{1,0:T(8,128)} async-done(((f32[960,768]{1,0:T(8,128)}), f32[480,768]{1,0:T(8,128)}) %reduce-scatter.26.cloned.1.call-update) | async-done | bytes 1474576 | tf_op jit(solution)/shard_map/reduce_scatter | solution.py:48
  683.4 33.6 %all-gather.31.cloned.1.call-done = bf16[1728,768]{1,0:T(8,128)(2,1)} async-done(((bf16[864,768]{1,0:T(8,128)(2,1)}), bf16[1728,768]{1,0:T(8,128)(2,1)}) %all-gather.31.cloned.1.call-update) | async-done | bytes 2654224 | tf_op jit(solution)/shard_map/all_gather | solution.py:42
  717.1 15.1 convert_reduce_fusion
  734.5 7.7 fusion.33
  749.1 64.2 %reduce-scatter.30.cloned.1.call-done = f32[864,768]{1,0:T(8,128)} async-done(((f32[1728,768]{1,0:T(8,128)}), f32[864,768]{1,0:T(8,128)}) %reduce-scatter.30.cloned.1.call-update) | async-done | bytes 2654224 | tf_op jit(solution)/shard_map/reduce_scatter | solution.py:48
  813.3 4.5 multiply_reduce_fusion.7
  851.7 5.3 convolution_bitcast_fusion.8
  857.2 4.3 all-gather.33.cloned.1.call-done
  868.4 9.1 multiply_reduce_fusion
  884.2 5.6 convert_element_type.573
  896.0 5.8 convert_element_type.576
  901.9 4.4 convert_bitcast_fusion.1
  914.3 6.8 convolution_bitcast_fusion.5
  930.5 57.3 %reduce-scatter.32.cloned.1.call-done = f32[864,768]{1,0:T(8,128)} async-done(((f32[1728,768]{1,0:T(8,128)}), f32[864,768]{1,0:T(8,128)}) %reduce-scatter.32.cloned.1.call-update) | async-done | bytes 2654224 | tf_op jit(solution)/shard_map/reduce_scatter | solution.py:48
  987.8 4.5 multiply_reduce_fusion.8
  996.7 18.8 all-gather.29.cloned.1.call-done
  1022.7 4.8 multiply_reduce_fusion.2
  1033.5 22.9 %all-gather.35.cloned.1.call-done = bf16[1728,768]{1,0:T(8,128)(2,1)} async-done(((bf16[864,768]{1,0:T(8,128)(2,1)}), bf16[1728,768]{1,0:T(8,128)(2,1)}) %all-gather.35.cloned.1.call-update) | async-done | bytes 2654224 | tf_op jit(solution)/shard_map/all_gather | solution.py:42
  1056.4 4.5 convolution_convert_fusion
  1060.9 5.4 reshape.582
  1066.3 4.5 convert_bitcast_fusion.4
  1082.6 5.9 convolution_bitcast_fusion.7
  1096.0 5.6 convert_element_type.594
  1101.6 4.6 convert_bitcast_fusion
  1108.7 5.6 convert_element_type.597
  1125.7 6.8 convolution_bitcast_fusion.4
  1133.9 4.7 convolution_bitcast_fusion.1
  1145.3 7.0 convolution_bitcast_fusion
  1156.6 15.2 copy.169
  1175.6 5.4 fusion.94
  1196.2 5.0 pad_maximum_fusion
  1201.2 16.4 copy.167
  1223.6 6.8 convolution_bitcast_fusion.2
  1230.5 4.4 pad_maximum_fusion.1
  1252.0 449.2 %all-reduce.10.cloned.1.call-done = (f32[3,3,768,384]{3,1,0,2:T(4,128)}, f32[3,384,768]{1,0,2:T(4,128)}, f32[2,1536,768]{1,0,2:T(2,128)}) async-done(((f32[3,3,768,384]{3,1,0,2:T(4,128)}, f32[3,384,768]{1,0,2:T(4,128)}, f32[2,1536,768]{1,0,2:T(2,128)}), (f32[3,3,768,384]{3,1,0,2:T(4,128)}, f32[3,384,768]{1,0,2:T(4,128)}, f32[2,1536,768]{1,0,2:T(2,128)})) %all-reduce.10.cloned.1.call-update) | async-done | bytes 23592976
  1707.2 109.8 %reduce-scatter.38.cloned.1.call-done = f32[2,48,1536]{2,1,0:T(8,128)} async-done(((f32[2,768,1536]{2,1,0:T(8,128)}), f32[2,48,1536]{2,1,0:T(8,128)}) %reduce-scatter.38.cloned.1.call-update) | async-done | bytes 589840 | tf_op jit(solution)/shard_map/reduce_scatter | solution.py:427
  1817.0 132.4 %all-reduce.8.cloned.1.call-done = (f32[3,2,768]{2,1,0:T(2,128)}, f32[3,2,768]{2,1,0:T(2,128)}, f32[3,768]{1,0:T(4,128)}, f32[2,3072]{1,0:T(2,128)}, f32[2,2,768]{2,1,0:T(2,128)}, /*index=5*/f32[2,768]{1,0:T(2,128)}) async-done(((f32[3,2,768]{2,1,0:T(2,128)}, f32[3,2,768]{2,1,0:T(2,128)}, f32[3,768]{1,0:T(4,128)}, f32[2,3072]{1,0:T(2,128)}, f32[2,2,768]{2,1,0:T(2,128)}, /*index=5*/f32[2,768]{1,0:T(2,128)}), ...) | async-done | bytes 89104 | tf_op jit(solution)/shard_map/psum | solution.py:443
  (631 shorter events, 385.5 us)
Async XLA Ops:
  7.2 31.2 %all-gather.15.cloned.1.call-start = ((), (), s32[]{:S(2)}) async-start(), calls=%async_computation.14 | async-start | bytes 2211840 | tf_op jit(solution)/shard_map/all_gather | solution.py:30
  7.9 71.4 %all-gather.13.cloned.1.call-start = ((), (), s32[]{:S(2)}) async-start(), calls=%async_computation.13 | async-start | bytes 3981312 | tf_op jit(solution)/shard_map/all_gather | solution.py:30
  8.7 148.1 %reduce-scatter.14.cloned.1.call-start = ((), (), s32[]{:S(2)}) async-start(), calls=%async_computation.15 | async-start | bytes 4423680 | tf_op jit(solution)/shard_map/reduce_scatter | solution.py:36
  10.2 38.0 %copy-start.109 = (f32[6,64]{1,0:T(8,128)}, f32[6,64]{1,0:T(8,128)S(1)}, u32[]{:S(2)}) copy-start(f32[6,64]{1,0:T(8,128)S(1)} %reshape.584) | copy-start | bytes 4612
  10.2 94.1 %copy-start.110 = (f32[6,64]{1,0:T(8,128)}, f32[6,64]{1,0:T(8,128)S(1)}, u32[]{:S(2)}) copy-start(f32[6,64]{1,0:T(8,128)S(1)} %reshape.583) | copy-start | bytes 4612
  11.0 341.2 %copy-start.90 = (pred[48,36]{1,0:T(8,128)(4,1)}, pred[48,36]{1,0:T(8,128)(4,1)S(1)}, u32[]{:S(2)}) copy-start(pred[48,36]{1,0:T(8,128)(4,1)S(1)} %iota_compare_fusion) | copy-start | bytes 5188
  95.8 12.3 copy-start.9
  115.4 71.8 %all-gather.17.cloned.1.call-start = ((), (), s32[]{:S(2)}) async-start(), calls=%async_computation.16 | async-start | bytes 2211840 | tf_op jit(solution)/shard_map/all_gather | solution.py:30
  116.1 327.3 %copy-start.92 = (f32[768]{0:T(1024)}, f32[768]{0:T(1024)S(1)}, u32[]{:S(2)}) copy-start(f32[768]{0:T(1024)S(1)} %get-tuple-element.93) | copy-start | bytes 9220
  134.3 26.7 %copy-start.19 = (bf16[48,36,6,64]{3,2,1,0:T(8,128)(2,1)}, bf16[48,36,6,64]{3,2,1,0:T(8,128)(2,1)S(1)}, u32[]{:S(2)}) copy-start(bf16[48,36,6,64]{3,2,1,0:T(8,128)(2,1)S(1)} %add_convert_fusion.3) | copy-start | bytes 3981316
  161.0 94.9 %reduce-scatter.20.cloned.1.call-start = ((), (), s32[]{:S(2)}) async-start(), calls=%async_computation.20 | async-start | bytes 7962624 | tf_op jit(solution)/shard_map/reduce_scatter | solution.py:36
  178.2 121.8 %all-gather.21.cloned.1.call-start = ((), (), s32[]{:S(2)}) async-start(), calls=%async_computation.21 | async-start | bytes 3981312 | tf_op jit(solution)/shard_map/all_gather | solution.py:30
  193.3 62.6 %copy-start.114 = (f32[768]{0:T(1024)S(1)}, f32[768]{0:T(1024)}, u32[]{:S(2)}) copy-start(f32[768]{0:T(1024)} %get-tuple-element.85) | copy-start | bytes 9220
  195.9 63.0 %copy-start.100 = (f32[768]{0:T(1024)S(1)}, f32[768]{0:T(1024)}, u32[]{:S(2)}) copy-start(f32[768]{0:T(1024)} %get-tuple-element.84) | copy-start | bytes 9220
  258.4 184.9 %copy-start.5 = (f32[864,768]{1,0:T(8,128)}, f32[864,768]{1,0:T(8,128)S(1)}, u32[]{:S(2)}) copy-start(f32[864,768]{1,0:T(8,128)S(1)} %get-tuple-element.135) | copy-start | bytes 7962628
  258.4 184.9 %copy-start.94 = (f32[864]{0:T(1024)}, f32[864]{0:T(1024)S(1)}, u32[]{:S(2)}) copy-start(f32[864]{0:T(1024)S(1)} %broadcast_multiply_fusion.8) | copy-start | bytes 10372
  258.9 184.4 %copy-start.96 = (f32[864]{0:T(1024)}, f32[864]{0:T(1024)S(1)}, u32[]{:S(2)}) copy-start(f32[864]{0:T(1024)S(1)} %add_rsqrt_fusion.2) | copy-start | bytes 10372
  260.5 83.1 %reduce-scatter.16.cloned.1.call-start = ((), (), s32[]{:S(2)}) async-start(), calls=%async_computation.17 | async-start | bytes 4423680 | tf_op jit(solution)/shard_map/reduce_scatter | solution.py:36
  289.7 84.8 %all-gather.19.cloned.1.call-start = ((), (), s32[]{:S(2)}) async-start(), calls=%async_computation.18 | async-start | bytes 2211840 | tf_op jit(solution)/shard_map/all_gather | solution.py:30
  341.9 10.3 copy-start.59
  348.3 95.1 %reduce-scatter.22.cloned.1.call-start = ((), (), s32[]{:S(2)}) async-start(), calls=%async_computation.22 | async-start | bytes 7962624 | tf_op jit(solution)/shard_map/reduce_scatter | solution.py:36
  352.2 8.0 copy-start.21
  373.5 113.2 %reduce-scatter.18.cloned.1.call-start = ((), (), s32[]{:S(2)}) async-start(), calls=%async_computation.19 | async-start | bytes 4423680 | tf_op jit(solution)/shard_map/reduce_scatter | solution.py:36
  400.6 42.8 %copy-start.129 = (f32[768]{0:T(1024)S(1)}, f32[768]{0:T(1024)}, u32[]{:S(2)}) copy-start(f32[768]{0:T(1024)} %get-tuple-element.81) | copy-start | bytes 9220
  400.6 127.7 %all-gather.23.cloned.1.call-start = ((), (), s32[]{:S(2)}) async-start(), calls=%async_computation.23 | async-start | bytes 3981312 | tf_op jit(solution)/shard_map/all_gather | solution.py:30
  446.5 40.2 %copy-start.15 = (f32[480,768]{1,0:T(8,128)S(1)}, f32[480,768]{1,0:T(8,128)}, u32[]{:S(2)}) copy-start(f32[480,768]{1,0:T(8,128)} %copy-done.14) | copy-start | bytes 4423684
  449.1 117.4 %all-gather.25.cloned.1.call-start = ((), (), s32[]{:S(2)}) async-start(), calls=%async_computation.25 | async-start | bytes 2211840 | tf_op jit(solution)/shard_map/all_gather | solution.py:42
  490.4 69.9 %slice-start.2 = ((s8[4718592]{0:T(1024)(128)(4,1)}), s8[524288]{0:T(1024)(128)(4,1)S(1)}, s32[]{:S(2)}) async-start(s8[4718592]{0:T(1024)(128)(4,1)} %bitcast.249), calls=%async_computation.42 | async-start | bytes 1048576
  494.7 138.1 %reduce-scatter.24.cloned.1.call-start = ((), (), s32[]{:S(2)}) async-start(), calls=%async_computation.24 | async-start | bytes 7962624 | tf_op jit(solution)/shard_map/reduce_scatter | solution.py:36
  528.3 32.0 %slice-start.3 = ((s8[4718592]{0:T(1024)(128)(4,1)}), s8[4194304]{0:T(1024)(128)(4,1)S(1)}, s32[]{:S(2)}) async-start(s8[4718592]{0:T(1024)(128)(4,1)} %bitcast.249), calls=%async_computation.43 | async-start | bytes 8388608
  566.2 12.4 slice-start.4
  566.2 110.0 %reduce-scatter.26.cloned.1.call-start = ((), (), s32[]{:S(2)}) async-start(), calls=%async_computation.26 | async-start | bytes 4423680 | tf_op jit(solution)/shard_map/reduce_scatter | solution.py:48
  566.5 12.1 slice-start.5
  582.7 50.2 %copy-start.8 = (f32[864,768]{1,0:T(8,128)S(1)}, f32[864,768]{1,0:T(8,128)}, u32[]{:S(2)}) copy-start(f32[864,768]{1,0:T(8,128)} %copy-done.7) | copy-start | bytes 7962628
  582.7 134.4 %all-gather.31.cloned.1.call-start = ((), (), s32[]{:S(2)}) async-start(), calls=%async_computation.30 | async-start | bytes 3981312 | tf_op jit(solution)/shard_map/all_gather | solution.py:42
  644.5 100.1 %all-gather.27.cloned.1.call-start = ((), (), s32[]{:S(2)}) async-start(), calls=%async_computation.27 | async-start | bytes 2211840 | tf_op jit(solution)/shard_map/all_gather | solution.py:42
  683.2 130.1 %reduce-scatter.30.cloned.1.call-start = ((), (), s32[]{:S(2)}) async-start(), calls=%async_computation.31 | async-start | bytes 7962624 | tf_op jit(solution)/shard_map/reduce_scatter | solution.py:48
  742.2 119.4 %all-gather.33.cloned.1.call-start = ((), (), s32[]{:S(2)}) async-start(), calls=%async_computation.32 | async-start | bytes 3981312 | tf_op jit(solution)/shard_map/all_gather | solution.py:42
  822.0 99.2 %reduce-scatter.28.cloned.1.call-start = ((), (), s32[]{:S(2)}) async-start(), calls=%async_computation.28 | async-start | bytes 4423680 | tf_op jit(solution)/shard_map/reduce_scatter | solution.py:48
  857.0 130.8 %reduce-scatter.32.cloned.1.call-start = ((), (), s32[]{:S(2)}) async-start(), calls=%async_computation.33 | async-start | bytes 7962624 | tf_op jit(solution)/shard_map/reduce_scatter | solution.py:48
  865.0 12.5 slice-start
  868.4 9.2 slice-start.1
  896.0 5.8 copy-start.22
  921.2 94.3 %all-gather.29.cloned.1.call-start = ((), (), s32[]{:S(2)}) async-start(), calls=%async_computation.29 | async-start | bytes 2211840 | tf_op jit(solution)/shard_map/all_gather | solution.py:42
  925.7 62.1 %copy-start.6 = (f32[864,768]{1,0:T(8,128)S(1)}, f32[864,768]{1,0:T(8,128)}, u32[]{:S(2)}) copy-start(f32[864,768]{1,0:T(8,128)} %copy-done.5) | copy-start | bytes 7962628
  925.7 62.1 %copy-start.95 = (f32[864]{0:T(1024)S(1)}, f32[864]{0:T(1024)}, u32[]{:S(2)}) copy-start(f32[864]{0:T(1024)} %copy-done.94) | copy-start | bytes 10372
  925.7 62.1 %copy-start.97 = (f32[864]{0:T(1024)S(1)}, f32[864]{0:T(1024)}, u32[]{:S(2)}) copy-start(f32[864]{0:T(1024)} %copy-done.96) | copy-start | bytes 10372
  930.5 125.9 %all-gather.35.cloned.1.call-start = ((), (), s32[]{:S(2)}) async-start(), calls=%async_computation.34 | async-start | bytes 3981312 | tf_op jit(solution)/shard_map/all_gather | solution.py:42
  996.6 26.0 %copy-start.10 = (f32[48,6,20,36]{3,2,1,0:T(8,128)S(1)}, f32[48,6,20,36]{3,2,1,0:T(8,128)}, u32[]{:S(2)}) copy-start(f32[48,6,20,36]{3,2,1,0:T(8,128)} %copy-done.9) | copy-start | bytes 2488324
  996.7 248.5 %reduce-scatter.34.cloned.1.call-start = ((), (), s32[]{:S(2)}) async-start(), calls=%async_computation.35 | async-start | bytes 4423680 | tf_op jit(solution)/shard_map/reduce_scatter | solution.py:48
  1088.6 159.9 %reduce-scatter.36.cloned.1.call-start = ((), (), s32[]{:S(2)}) async-start(), calls=%async_computation.36 | async-start | bytes 7962624 | tf_op jit(solution)/shard_map/reduce_scatter | solution.py:48
  1132.6 6.0 copy-start.82
  1132.6 568.6 %all-reduce.10.cloned.1.call-start = ((), (), s32[]{:S(2)}) async-start(), calls=%async_computation.39 | async-start | bytes 56623104
  1156.6 15.2 copy-start.51
  1217.6 599.4 %reduce-scatter.38.cloned.1.call-start = ((), (), s32[]{:S(2)}) async-start(), calls=%async_computation.37 | async-start | bytes 10027008 | tf_op jit(solution)/shard_map/reduce_scatter | solution.py:427
  1234.9 8.8 copy-start.86
  1235.0 7.4 copy-start.117
  1235.0 7.4 copy-start.120
  1235.0 7.4 copy-start.116
  1235.0 7.4 copy-start.118
  1235.0 7.4 copy-start.119
  1235.0 7.4 copy-start.130
  1235.0 714.4 %all-reduce.8.cloned.1.call-start = ((), (), s32[]{:S(2)}) async-start(), calls=%async_computation.38 | async-start | bytes 184320 | tf_op jit(solution)/shard_map/psum | solution.py:443
  1236.9 7.1 copy-start.69
  (128 other events, 354.8 us)
Sparse Core Ops, SparseCore 0:
  9.5 28.7 all-gather.14
  39.9 39.3 all-gather.12
  115.5 41.2 reduce-scatter.13
  161.1 26.0 all-gather.16
  189.3 66.4 reduce-scatter.19
  260.6 39.3 all-gather.20
  302.3 41.2 reduce-scatter.15
  348.4 26.0 all-gather.18
  376.8 66.4 reduce-scatter.21
  445.4 41.2 reduce-scatter.17
  488.8 39.3 all-gather.22
  529.7 26.0 all-gather.24
  566.4 66.4 reduce-scatter.23
  635.0 41.2 reduce-scatter.25
  677.6 39.3 all-gather.30
  718.5 26.0 all-gather.26
  746.7 66.4 reduce-scatter.29
  822.2 39.3 all-gather.32
  863.8 41.2 reduce-scatter.27
  921.3 66.4 reduce-scatter.31
  989.4 26.0 all-gather.28
  1017.0 39.3 all-gather.34
  1088.7 41.2 reduce-scatter.33
  1132.7 66.5 reduce-scatter.35
  1217.7 483.4 all-reduce.9
  1705.8 111.2 reduce-scatter.37
  1824.5 124.9 all-reduce.7
where the time goes:
time: 1980 us; the launch traced here: 1960 us
  waiting for transfers between devices  1250 us (63%)
  matrix products  300 us (15%)
  local copies, waits for them, and re-layouts  266 us (13%)
  other arithmetic  130 us (7%)
    unnamed x28, waiting for transfers between devices  451 us
    reduce_scatter x6, waiting for transfers between devices, sum_rows(): return lax.psum_scatter(partials, 'mp', scatter_dimension=0, tiled=True)  213 us
    reduce_scatter x6, waiting for transfers between devices, sum_inputs(): return lax.psum_scatter(partials, 'mp', scatter_dimension=0, tiled=True)  153 us
    psum x1, waiting for transfers between devices, per_device(): lax.psum((in_bias_full, up_bias_full, att_rows_grad, att_gain_grad, ffn_r...  132 us
    reduce_scatter x1, waiting for transfers between devices, per_device(): lax.psum_scatter(up_stack, 'dp', scatter_dimension=1, tiled=True)  110 us
    all_gather x6, waiting for transfers between devices, gather_rows(): lax.all_gather(shortened(stream_pair), 'mp', axis=0, tiled=True)  106 us
    all_gather x6, waiting for transfers between devices, gather_grads(): lax.all_gather(shortened(grad_pair), 'mp', axis=0, tiled=True)  81.9 us
    unnamed x351, local copies, waits for them, and re-layouts  72.9 us
  transfers between devices with their start and end apart: 27, of which 23 were waited for; matrix products, arithmetic and copies ran while one was open for 28% of the time, Pallas kernels for 0%

commit v1 on v0

v1 whole, which is shorter than its diff:
```python
from functools import partial

import jax
import jax.numpy as jnp
from jax import lax
from jax.experimental import pallas as pl
from jax.experimental.pallas import tpu as pltpu
from jax.sharding import PartitionSpec as P

D = 768
FF = 3072
WORDS = 20
REGIONS = 36
HEAD_DIM = 64
GROUP = 4
PIECES = 4

NORM_EPSILON = 1e-06
MASK_FILL = -1000000000.0
F32 = jnp.float32
BF16 = jnp.bfloat16


def dot32(left, right, left_dim, right_dim):
    return lax.dot_general(
        left, right, (((left_dim,), (right_dim,)), ((), ())), preferred_element_type=F32
    )


def item_rows(rows, per_item):
    row = lax.broadcasted_iota(jnp.int32, (rows, 1), 0)
    item = jnp.zeros((rows, 1), jnp.int32)
    for bound in range(per_item, rows, per_item):
        item = item + (row >= bound).astype(jnp.int32)
    return item


def two_heads(block):
    lane = lax.broadcasted_iota(jnp.int32, block.shape, 1)
    zero = jnp.zeros_like(block)
    return jnp.concatenate(
        (jnp.where(lane < HEAD_DIM, block, zero), jnp.where(lane < HEAD_DIM, zero, block)), axis=0
    )


def join_heads(stacked):
    rows = stacked.shape[0] // 2
    lane = lax.broadcasted_iota(jnp.int32, (rows, stacked.shape[1]), 1)
    return jnp.where(lane < HEAD_DIM, stacked[:rows], stacked[rows:])


def probabilities(query_stack, keys, ok_stack):
    scores = dot32(query_stack, keys, 1, 1) * HEAD_DIM ** (-0.5)
    scores = jnp.where(ok_stack, scores, MASK_FILL)
    raised = jnp.exp(scores - jnp.max(scores, axis=-1, keepdims=True))
    return raised * (1.0 / jnp.sum(raised, axis=-1, keepdims=True))


def attend_pairs_forward(q_ref, k_ref, v_ref, ok, o_ref):
    ok_stack = jnp.concatenate((ok, ok), axis=0)
    for start in range(0, q_ref.shape[1], 2 * HEAD_DIM):
        span = slice(start, start + 2 * HEAD_DIM)
        probs = probabilities(two_heads(q_ref[:, span]), k_ref[:, span], ok_stack)
        mixed = dot32(probs.astype(BF16), v_ref[:, span], 1, 0)
        o_ref[:, span] = join_heads(mixed).astype(BF16)


def attend_pairs_backward(q_ref, k_ref, v_ref, d_ref, ok, dq_ref, dk_ref, dv_ref):
    ok_stack = jnp.concatenate((ok, ok), axis=0)
    scale = HEAD_DIM ** (-0.5)
    for start in range(0, q_ref.shape[1], 2 * HEAD_DIM):
        span = slice(start, start + 2 * HEAD_DIM)
        query_stack = two_heads(q_ref[:, span])
        keys = k_ref[:, span]
        probs = probabilities(query_stack, keys, ok_stack)
        grad_stack = two_heads(d_ref[:, span])
        grad_probs = dot32(grad_stack, v_ref[:, span], 1, 1)
        centre = jnp.sum(grad_probs * probs, axis=-1, keepdims=True)
        grad_scores = (probs * (grad_probs - centre)).astype(BF16)
        dq_ref[:, span] = (join_heads(dot32(grad_scores, keys, 1, 0)) * scale).astype(BF16)
        dk_ref[:, span] = (dot32(grad_scores, query_stack, 0, 0) * scale).astype(BF16)
        dv_ref[:, span] = dot32(probs.astype(BF16), grad_stack, 0, 0).astype(BF16)


def group_masks(region_key, cross, words, regions):
    lang_item = item_rows(words, WORDS)
    vision_item = item_rows(regions, REGIONS)
    lane = lax.broadcasted_iota(jnp.int32, (1, words), 1)
    word_key = jnp.zeros((1, words), jnp.int32)
    for bound in range(WORDS, words, WORDS):
        word_key = word_key + (lane >= bound).astype(jnp.int32)
    if cross:
        return lang_item == region_key, vision_item == word_key
    return lang_item == word_key, vision_item == region_key


def attention_forward_kernel(cross, key_ref, ql, kl, vl, qv, kv, vv, ol, ov):
    lang_ok, vision_ok = group_masks(key_ref[0], cross, ql.shape[0], qv.shape[0])
    if cross:
        attend_pairs_forward(ql, kv, vv, lang_ok, ol)
        attend_pairs_forward(qv, kl, vl, vision_ok, ov)
    else:
        attend_pairs_forward(ql, kl, vl, lang_ok, ol)
        attend_pairs_forward(qv, kv, vv, vision_ok, ov)


def attention_backward_kernel(
    cross, key_ref, ql, kl, vl, qv, kv, vv, dol, dov, dql, dkl, dvl, dqv, dkv, dvv
):
    lang_ok, vision_ok = group_masks(key_ref[0], cross, ql.shape[0], qv.shape[0])
    if cross:
        attend_pairs_backward(ql, kv, vv, dol, lang_ok, dql, dkv, dvv)
        attend_pairs_backward(qv, kl, vl, dov, vision_ok, dqv, dkl, dvl)
    else:
        attend_pairs_backward(ql, kl, vl, dol, lang_ok, dql, dkl, dvl)
        attend_pairs_backward(qv, kv, vv, dov, vision_ok, dqv, dkv, dvv)


def attention_call(kernel, cross, region_key, arrays, out_streams):
    groups = region_key.shape[0]
    width = arrays[0].shape[1]
    rows = {"l": GROUP * WORDS, "v": GROUP * REGIONS}

    def spec(stream):
        return pl.BlockSpec((rows[stream], width), lambda g: (g, 0))

    streams = "lllvvv" + ("lv" if len(arrays) == 8 else "")
    flops = 24 * 64 * 2 * 8 * groups * GROUP * 100
    return pl.pallas_call(
        partial(kernel, cross),
        grid=(groups,),
        in_specs=[pl.BlockSpec((1, 1, rows["v"]), lambda g: (g, 0, 0))]
        + [spec(stream) for stream in streams],
        out_specs=[spec(stream) for stream in out_streams],
        out_shape=[
            jax.ShapeDtypeStruct((groups * rows[stream], width), BF16) for stream in out_streams
        ],
        cost_estimate=pl.CostEstimate(
            flops=flops * 100, bytes_accessed=30_000_000, transcendentals=1_000_000
        ),
    )(region_key, *arrays)


def norm_forward(summed, gain, shift):
    row_mean = jnp.mean(summed, axis=-1, keepdims=True)
    centred = summed - row_mean
    spread = jnp.mean(centred * centred, axis=-1, keepdims=True)
    inv_scale = lax.rsqrt(spread + NORM_EPSILON)
    normed = centred * inv_scale
    return (normed * gain.astype(F32) + shift, (normed, inv_scale))


def norm_backward(grad_out, saved, gain):
    normed, inv_scale = saved
    grad_normed = grad_out * gain.astype(F32)
    mean_first = jnp.mean(grad_normed, axis=-1, keepdims=True)
    mean_second = jnp.mean(grad_normed * normed, axis=-1, keepdims=True)
    grad_total = inv_scale * (grad_normed - mean_first - normed * mean_second)
    return (grad_total, jnp.sum(grad_out * normed, axis=0), jnp.sum(grad_out, axis=0))


class Links:
    def __init__(self):
        self.ndp = lax.axis_size("dp")
        self.dp = lax.axis_index("dp")
        self.mp = lax.axis_index("mp")
        self.piece = self.dp % PIECES

    def across(self, value):
        pairs = [(2 * d + m, 2 * d + 1 - m) for d in range(self.ndp) for m in range(2)]
        return lax.ppermute(value, ("dp", "mp"), pairs)

    def flip(self, value, bit):
        pairs = [
            (2 * d + m, 2 * (d ^ (1 << bit)) + m) for d in range(self.ndp) for m in range(2)
        ]
        return lax.ppermute(value, ("dp", "mp"), pairs)

    def other_pieces(self, own_piece):
        first = self.across(own_piece)
        third = self.flip(first, 1)
        second = self.flip(first, 0)
        fourth = self.flip(third, 0)
        return [first, second, third, fourth]

    def place(self, pieces, axis):
        size = pieces[0].shape[axis]
        shape = list(pieces[0].shape)
        shape[axis] = size * PIECES
        whole = jnp.zeros(shape, pieces[0].dtype)
        for step, part in enumerate(pieces):
            whole = lax.dynamic_update_slice_in_dim(
                whole, part, (self.piece ^ step) * size, axis
            )
        return whole

    def own_pieces(self, value, axis):
        size = value.shape[axis] // PIECES
        return [
            lax.dynamic_slice_in_dim(value, (self.piece ^ step) * size, size, axis)
            for step in range(PIECES)
        ]

    def own_piece(self, value, axis):
        size = value.shape[axis] // PIECES
        return lax.dynamic_slice_in_dim(value, self.piece * size, size, axis)

    def reduce(self, own, other, moved):
        rows, columns = own.shape
        low = rows // self.ndp
        side = self.dp % 2

        def halves(value, side, count):
            split = value.reshape(count // 2, 2, low, value.shape[-1])
            keep = lax.dynamic_index_in_dim(split, side, 1, keepdims=False)
            send = lax.dynamic_index_in_dim(split, 1 - side, 1, keepdims=False)
            return keep, send.astype(BF16)

        def swapped(value, bit):
            if not moved or bit > 1:
                return value
            split = value.reshape(*value.shape[:-1], 2, 2, columns // 4)
            flipped = split[..., ::-1, :] if bit == 0 else split[..., ::-1, :, :]
            return flipped.reshape(value.shape)

        keep_own, send_own = halves(own, side, self.ndp)
        keep_other, send_other = halves(other, side, self.ndp)
        got_other = self.flip(send_other, 0)
        got_own = self.flip(send_own, 0)
        other_sum = keep_other + swapped(got_other, 0).astype(F32)
        total = keep_own + swapped(got_own, 0).astype(F32)
        total = total + self.across(other_sum.astype(BF16)).astype(F32)
        bit, count = 1, self.ndp // 2
        while count > 1:
            side = (self.dp >> bit) % 2
            keep, send = halves(total, side, count)
            total = keep + swapped(self.flip(send, bit), bit).astype(F32)
            bit, count = bit + 1, count // 2
        return total.reshape(low, columns)

    def settle(self, value):
        size = value.shape[-1] // PIECES
        return jnp.concatenate(
            [
                lax.dynamic_slice_in_dim(value, (self.piece ^ step) * size, size, -1)
                for step in range(PIECES)
            ],
            axis=-1,
        )

    def total(self, value):
        value = value + self.across(value)
        for bit in range(self.ndp.bit_length() - 1):
            value = value + self.flip(value, bit)
        return value


def project(rows, weight, bias):
    queries = (dot32(rows, weight[0], 1, 0) + bias[0].astype(F32)).astype(BF16)
    keys = dot32(rows, weight[1], 1, 0).astype(BF16)
    values = (dot32(rows, weight[2], 1, 0) + bias[1].astype(F32)).astype(BF16)
    return queries, keys, values


def attention_block(low_pair, halves_pair, cross, region_key):
    kept, branch_lang, branch_vision = [], 0.0, 0.0
    for lang_half, vision_half in zip(*halves_pair):
        lang_proj = project(low_pair[0], lang_half[0], lang_half[2])
        vision_proj = project(low_pair[1], vision_half[0], vision_half[2])
        mixed = attention_call(
            attention_forward_kernel, cross, region_key, (*lang_proj, *vision_proj), "lv"
        )
        branch_lang = branch_lang + dot32(mixed[0], lang_half[1], 1, 0)
        branch_vision = branch_vision + dot32(mixed[1], vision_half[1], 1, 0)
        kept.append((lang_proj, vision_proj, mixed))
    return (branch_lang, branch_vision), kept


def attention_block_backward(grad_pair, low_pair, halves_pair, kept, cross, region_key):
    grads = tuple(g.astype(BF16) for g in grad_pair)
    back_lang, back_vision = 0.0, 0.0
    per_half = []
    for (lang_half, vision_half), (lang_proj, vision_proj, mixed) in zip(
        zip(*halves_pair), kept
    ):
        out_grads = [dot32(g, m, 0, 0) for g, m in zip(grads, mixed)]
        dmix = [
            dot32(g, half[1], 1, 1).astype(BF16)
            for g, half in zip(grads, (lang_half, vision_half))
        ]
        back = attention_call(
            attention_backward_kernel,
            cross,
            region_key,
            (*lang_proj, *vision_proj, *dmix),
            "lllvvv",
        )
        lang_d, vision_d = back[:3], back[3:]
        in_grads = [
            [dot32(low, d, 0, 0) for d in ds] for low, ds in zip(low_pair, (lang_d, vision_d))
        ]
        bias_grads = [
            jnp.stack([jnp.sum(ds[k].astype(F32), axis=0) for k in (0, 2)])
            for ds in (lang_d, vision_d)
        ]
        for k in range(3):
            back_lang = back_lang + dot32(lang_d[k], lang_half[0][k], 1, 1)
            back_vision = back_vision + dot32(vision_d[k], vision_half[0][k], 1, 1)
        per_half.append((in_grads, out_grads, bias_grads))
    return (back_lang, back_vision), per_half


def gelu_back(hidden, act_grad):
    pull_back = jax.vjp(partial(jax.nn.gelu, approximate=False), hidden)[1]
    return pull_back(act_grad)[0].astype(BF16)


def per_device(
    lang,
    vision,
    region_count,
    att_in,
    att_in_bias,
    att_out,
    att_row_bias,
    att_gain,
    ffn_up,
    ffn_up_bias,
    ffn_down,
    ffn_row_bias,
    ffn_gain,
    cot_lang,
    cot_vision,
):
    links = Links()
    items = region_count.shape[0] // 2
    groups = items // GROUP
    counts = lax.dynamic_slice_in_dim(region_count, links.mp * items, items)
    slot = jnp.arange(REGIONS, dtype=jnp.int32)
    region_ok = slot[None, :] < counts[:, None]
    item_index = (jnp.arange(items, dtype=jnp.int32) % GROUP)[:, None]
    region_key = jnp.where(region_ok, item_index, -1).reshape(groups, 1, GROUP * REGIONS)
    row_ok = region_ok.reshape(-1, 1).astype(F32)

    heads = att_in.shape[-1]
    units = ffn_up.shape[-1]
    small_own = jnp.concatenate((att_in_bias.reshape(-1), ffn_up_bias.reshape(-1)))
    small_other = links.across(small_own)
    bias_other = small_other[: 6 * heads].reshape(3, 2, heads)
    up_bias_other = small_other[6 * heads :].reshape(2, units)
    att_halves = []
    for block in range(3):
        in_other = links.place(links.other_pieces(links.own_piece(att_in[block], 1)), 1)
        out_other = links.place(links.other_pieces(links.own_piece(att_out[block], 0)), 0)
        att_halves.append(
            (
                (att_in[block], att_out[block], att_in_bias[block]),
                (in_other, out_other, bias_other[block]),
            )
        )
    up_own = links.own_pieces(ffn_up, 2)
    down_own = links.own_pieces(ffn_down, 1)
    up_other = links.other_pieces(up_own[0])
    down_other = links.other_pieces(down_own[0])
    ups = [jnp.concatenate(part, axis=2) for part in (up_own, up_other)]
    downs = [jnp.concatenate(part, axis=1) for part in (down_own, down_other)]
    up_biases = [
        jnp.concatenate(links.own_pieces(bias, 1), axis=1)
        for bias in (ffn_up_bias, up_bias_other)
    ]

    row_bias = att_row_bias.astype(F32)
    ffn_bias = ffn_row_bias.astype(F32)
    cross_halves = (att_halves[0], att_halves[0])
    self_halves = (att_halves[1], att_halves[2])

    branches, cross_kept = attention_block((lang, vision), cross_halves, True, region_key)
    lang_one, lang_norm_a = norm_forward(
        lang.astype(F32) + branches[0] + row_bias[0, 0], att_gain[0], row_bias[0, 1]
    )
    vision_one, vision_norm_a = norm_forward(
        vision.astype(F32) + branches[1] + row_bias[0, 0], att_gain[0], row_bias[0, 1]
    )
    low_one = (lang_one.astype(BF16), vision_one.astype(BF16))
    branches, self_kept = attention_block(low_one, self_halves, False, region_key)
    lang_two, lang_norm_b = norm_forward(
        lang_one + branches[0] + row_bias[1, 0], att_gain[1], row_bias[1, 1]
    )
    vision_two, vision_norm_b = norm_forward(
        vision_one + branches[1] + row_bias[2, 0], att_gain[2], row_bias[2, 1]
    )
    low_two = (lang_two.astype(BF16), vision_two.astype(BF16))

    outs, ffn_grads, streams = [], [], []
    cots = (cot_lang.astype(F32), cot_vision.astype(F32) * row_ok)
    for stream, (low, full, cot) in enumerate(zip(low_two, (lang_two, vision_two), cots)):
        hidden = [
            dot32(low, up[stream], 1, 0) + bias[stream].astype(F32)
            for up, bias in zip(ups, up_biases)
        ]
        act = [jax.nn.gelu(h, approximate=False).astype(BF16) for h in hidden]
        branch = sum(dot32(a, down[stream], 1, 0) for a, down in zip(act, downs))
        out, saved = norm_forward(
            full + branch + ffn_bias[stream, 0], ffn_gain[stream], ffn_bias[stream, 1]
        )
        outs.append(out)
        total, gain_grad, shift_grad = norm_backward(cot, saved, ffn_gain[stream])
        low_grad = total.astype(BF16)
        back = total
        down_grads, up_grads, up_bias_grads = [], [], []
        for part in range(2):
            dhidden = gelu_back(hidden[part], dot32(low_grad, downs[part][stream], 1, 1))
            down_grads.append(dot32(low_grad, act[part], 0, 0))
            up_grads.append(dot32(low, dhidden, 0, 0))
            up_bias_grads.append(jnp.sum(dhidden.astype(F32), axis=0))
            back = back + dot32(dhidden, ups[part][stream], 1, 1)
        ffn_grads.append(
            (
                links.reduce(down_grads[0], down_grads[1], True),
                links.reduce(up_grads[0], up_grads[1], True),
                up_bias_grads,
                jnp.stack((jnp.sum(total, axis=0), shift_grad)),
                gain_grad,
            )
        )
        streams.append(back)

    lang_total, lang_gain_b, lang_shift_b = norm_backward(streams[0], lang_norm_b, att_gain[1])
    vision_total, vision_gain_b, vision_shift_b = norm_backward(
        streams[1], vision_norm_b, att_gain[2]
    )
    lang_rows_b = jnp.stack((jnp.sum(lang_total, axis=0), lang_shift_b))
    vision_rows_b = jnp.stack((jnp.sum(vision_total, axis=0), vision_shift_b))
    back, self_grads = attention_block_backward(
        (lang_total, vision_total), low_one, self_halves, self_kept, False, region_key
    )
    in_reduced, out_reduced, bias_parts = [None] * 3, [None] * 3, [None] * 3
    for stream in range(2):
        own, other = self_grads
        own_in = jnp.concatenate(own[0][stream], axis=1)
        other_in = jnp.concatenate(other[0][stream], axis=1)
        in_reduced[1 + stream] = links.reduce(own_in, other_in, False)
        out_reduced[1 + stream] = links.reduce(own[1][stream], other[1][stream], False)
        bias_parts[1 + stream] = (own[2][stream], other[2][stream])
    lang_back = lang_total + back[0]
    vision_back = vision_total + back[1]
    lang_total, lang_gain_a, lang_shift_a = norm_backward(lang_back, lang_norm_a, att_gain[0])
    vision_total, vision_gain_a, vision_shift_a = norm_backward(
        vision_back, vision_norm_a, att_gain[0]
    )
    cross_rows = jnp.stack(
        (jnp.sum(lang_total, axis=0) + jnp.sum(vision_total, axis=0), lang_shift_a + vision_shift_a)
    )
    back, cross_grads = attention_block_backward(
        (lang_total, vision_total), (lang, vision), cross_halves, cross_kept, True, region_key
    )
    grad_lang = lang_total + back[0]
    grad_vision = vision_total + back[1]
    own, other = cross_grads
    in_reduced[0] = links.reduce(
        jnp.concatenate([a + b for a, b in zip(*own[0])], axis=1),
        jnp.concatenate([a + b for a, b in zip(*other[0])], axis=1),
        False,
    )
    out_reduced[0] = links.reduce(own[1][0] + own[1][1], other[1][0] + other[1][1], False)
    bias_parts[0] = (own[2][0] + own[2][1], other[2][0] + other[2][1])

    low_rows = D // links.ndp
    att_in_grad = jnp.stack(
        [part.reshape(low_rows, 3, heads).transpose(1, 0, 2) for part in in_reduced]
    )
    att_out_grad = jnp.stack([part.T for part in out_reduced])
    down_grad = jnp.stack([links.settle(part[0]).T for part in ffn_grads])
    up_grad = jnp.stack([links.settle(part[1]) for part in ffn_grads])

    def whole(own, other, width):
        lead = own.shape[:-1]
        result = jnp.zeros((*lead, 2 * width), F32)
        zeros = (0,) * len(lead)
        result = lax.dynamic_update_slice(result, own, (*zeros, links.mp * width))
        return lax.dynamic_update_slice(result, other, (*zeros, (1 - links.mp) * width))

    in_bias = whole(
        jnp.stack([part[0] for part in bias_parts]),
        jnp.stack([part[1] for part in bias_parts]),
        heads,
    )
    up_bias = whole(
        *(links.settle(jnp.stack([part[2][h] for part in ffn_grads])) for h in range(2)), units
    )
    parts = (
        in_bias,
        up_bias,
        jnp.stack((cross_rows, lang_rows_b, vision_rows_b)),
        jnp.stack((lang_gain_a + vision_gain_a, lang_gain_b, vision_gain_b)),
        jnp.stack([part[3] for part in ffn_grads]),
        jnp.stack([part[4] for part in ffn_grads]),
    )
    flat = links.total(jnp.concatenate([part.reshape(-1) for part in parts]))
    summed, at = [], 0
    for part in parts:
        summed.append(flat[at : at + part.size].reshape(part.shape))
        at += part.size
    return (
        outs[0],
        outs[1],
        grad_lang,
        grad_vision,
        att_in_grad,
        summed[0],
        att_out_grad,
        summed[2],
        summed[3],
        up_grad,
        summed[1],
        down_grad,
        summed[4],
        summed[5],
    )


def solution(mesh):
    rows = P(("dp", "mp"), None)
    return jax.shard_map(
        per_device,
        mesh=mesh,
        in_specs=(
            rows,
            rows,
            P("dp"),
            P(None, None, None, "mp"),
            P(None, None, "mp"),
            P(None, "mp", None),
            P(),
            P(),
            P(None, None, "mp"),
            P(None, "mp"),
            P(None, "mp", None),
            P(),
            P(),
            rows,
            rows,
        ),
        out_specs=(
            rows,
            rows,
            rows,
            rows,
            P(None, None, "dp", "mp"),
            P(),
            P(None, "mp", "dp"),
            P(),
            P(),
            P(None, "dp", "mp"),
            P(),
            P(None, "mp", "dp"),
            P(),
            P(),
        ),
        check_vma=False,
    )
```

time: 1980 us -> 1150 us (0.58)
  waiting for transfers between devices: 1250 us -> 218 us
  Pallas kernels: 0 us -> 123 us
  starting transfers between devices: 3.29 us -> 88.9 us
  other arithmetic: 130 us -> 108 us
    reduce_scatter x13 -> x0, waiting for transfers between devices: 476 us -> none  [the longest x6 213 us: sum_rows(): return lax.psum_scatter(partials, 'mp', scatter_dimension=0, tiled=True)]
    unnamed x28 -> x0, waiting for transfers between devices: 451 us -> none
    ppermute x0 -> x98, waiting for transfers between devices: none -> 218 us  [the longest x78 119 us: flip(): return lax.ppermute(value, ('dp', 'mp'), pairs)]
    all_gather x12 -> x0, waiting for transfers between devices: 188 us -> none  [the longest x6 106 us: gather_rows(): lax.all_gather(shortened(stream_pair), 'mp', axis=0, tiled=True)]
    psum x1 -> x0, waiting for transfers between devices: 132 us -> none  [per_device(): lax.psum((in_bias_full, up_bias_full, att_rows_grad, att_gain_grad, ffn_r...]
    pallas_call x0 -> x8, Pallas kernels: none -> 123 us  [attention_call(): pl.pallas_call(partial(kernel, cross), grid=(groups,), in_specs=[pl.Block...]
    ppermute x0 -> x98, starting transfers between devices: none -> 88.9 us  [the longest x78 66.8 us: flip(): return lax.ppermute(value, ('dp', 'mp'), pairs)]
    rev x0 -> x8, local copies, waits for them, and re-layouts: none -> 55.4 us  [swapped(): flipped = split[..., ::-1, :] if bit == 0 else split[..., ::-1, :, :]]
  transfers between devices with their start and end apart: 27 -> 98, of which waited for: 23 -> 38; matrix products, arithmetic and copies ran while one was open for 28% -> 42% of each run, Pallas kernels for 0% -> 3%
where the time goes in v1:
time: 1150 us; the launch traced here: 1140 us
  matrix products  315 us (27%)
  local copies, waits for them, and re-layouts  284 us (25%)
  waiting for transfers between devices  218 us (19%)
  Pallas kernels  123 us (11%)
  other arithmetic  108 us (9%)
  starting transfers between devices  88.9 us (8%)
    dot_general x120, matrix products, dot32(): lax.dot_general(left, right, (((left_dim,), (right_dim,)), ((), ())), pre...  315 us
    pallas_call x8, Pallas kernels, attention_call(): pl.pallas_call(partial(kernel, cross), grid=(groups,), in_specs=[pl.Block...  123 us
    ppermute x78, waiting for transfers between devices, flip(): return lax.ppermute(value, ('dp', 'mp'), pairs)  119 us
    ppermute x20, waiting for transfers between devices, across(): return lax.ppermute(value, ('dp', 'mp'), pairs)  98.8 us
    ppermute x78, starting transfers between devices, flip(): return lax.ppermute(value, ('dp', 'mp'), pairs)  66.8 us
    rev x8, local copies, waits for them, and re-layouts, swapped(): flipped = split[..., ::-1, :] if bit == 0 else split[..., ::-1, :, :]  55.4 us
    convert_element_type x50, local copies, waits for them, and re-layouts, halves(): return (keep, send.astype(BF16))  52.8 us
    reshape x12, local copies, waits for them, and re-layouts, swapped(): split = value.reshape(*value.shape[:-1], 2, 2, columns // 4)  33 us
  transfers between devices with their start and end apart: 98, of which 38 were waited for; matrix products, arithmetic and copies ran while one was open for 42% of the time, Pallas kernels for 3%

profile of v1, /device:TPU:0, one launch (start us, length us, event | category | flops | bytes accessed | tf_op | source)
XLA Modules:
  0.0 1141.8 jit_solution(3057016815055958184)
XLA Ops:
  11.3 5.0 fusion.259
  39.8 8.5 shard_map.254
  82.9 4.1 collective-permute-done.19
  103.0 6.1 collective-permute-done.11
  112.5 9.8 collective-permute-done.2
  122.4 7.8 collective-permute-done.15
  136.0 16.5 %collective-permute-done.25 = bf16[2,384,768]{2,1,0:T(8,128)(2,1)} collective-permute-done((bf16[2,384,768]{2,1,0:T(8,128)(2,1)S(1)}, bf16[2,384,768]{2,1,0:T(8,128)(2,1)}, u32[]{:S(2)}, u32[]{:S(2)}) %collective-permute-start.25) | collective-permute-done | bytes 1179680 | tf_op jit(solution)/shard_map/ppermute | solution.py:171
  164.5 8.5 shard_map.255
  201.6 10.5 shard_map.256
  214.9 10.9 shard_map.257
  234.1 14.6 %multiply_convert_fusion.1 = (bf16[864,1536]{1,0:T(8,128)(2,1)S(1)}, f32[864,1536]{1,0:T(8,128)}, f32[864,1536]{1,0:T(8,128)}) fusion(f32[1536]{0:T(1024)S(1)} %copy-done.200, bf16[864,768]{1,0:T(8,128)(2,1)S(1)} %fusion.36, bf16[2,768,1536]{2,1,0:T(8,128)(2,1)S(1)} %bitcast.864), kind=kOutput, calls=%fused_computation.21 | convolution fusion | flops 2126020608 | bytes 16965632 | tf_op jit(solution)/shard_map/dot_general | solution.py:25
  248.7 9.1 multiply_convert_fusion.3
  259.6 3.7 fusion.46
  269.7 9.3 multiply_convert_fusion.2
  284.6 4.2 convert_reduce_fusion.3
  290.6 4.3 convert_reduce_fusion.2
  319.5 15.0 %multiply_convert_fusion = (bf16[864,1536]{1,0:T(8,128)(2,1)S(1)}, f32[864,1536]{1,0:T(8,128)}, f32[864,1536]{1,0:T(8,128)}) fusion(f32[1536]{0:T(1024)S(1)} %copy-done.203, bf16[864,768]{1,0:T(8,128)(2,1)S(1)} %fusion.36, bf16[2,768,1536]{2,1,0:T(8,128)(2,1)S(1)} %constant_dynamic-update-slice_fusion.28), kind=kOutput, calls=%fused_computation.8 | convolution fusion | flops 2126020608 | bytes 16965632 | tf_op jit(solution)/shard_map/dot_general | solution.py:25
  344.6 7.0 convert_reduce_fusion.1
  353.9 7.9 convert_reduce_fusion
  361.7 3.6 multiply_reduce_fusion.1
  375.1 21.5 %shard_map.258 = (bf16[480,384]{1,0:T(8,128)(2,1)}, bf16[480,384]{1,0:T(8,128)(2,1)}, bf16[480,384]{1,0:T(8,128)(2,1)}, bf16[864,384]{1,0:T(8,128)(2,1)}, bf16[8...) custom-call(s32[6,1,144]{2,1,0:T(1,128)} %compare_select_fusion.key_ref, bf16[480,384]{1,0:T(8,128)(2,1)} %fusion.85.ql, ...), custom_call_target="tpu_custom_call" | custom-call | flops 5898240000 | bytes 30000000 | tf_op jit(solution)/shard_map/pallas_call | solution.py:129
  417.5 21.7 %shard_map.259 = (bf16[480,384]{1,0:T(8,128)(2,1)}, bf16[480,384]{1,0:T(8,128)(2,1)}, bf16[480,384]{1,0:T(8,128)(2,1)}, bf16[864,384]{1,0:T(8,128)(2,1)}, bf16[8...) custom-call(s32[6,1,144]{2,1,0:T(1,128)} %compare_select_fusion.key_ref, bf16[480,384]{1,0:T(8,128)(2,1)} %fusion.87.ql, ...), custom_call_target="tpu_custom_call" | custom-call | flops 5898240000 | bytes 30000000 | tf_op jit(solution)/shard_map/pallas_call | solution.py:129
  483.1 20.6 %shard_map.261 = (bf16[480,384]{1,0:T(8,128)(2,1)}, bf16[480,384]{1,0:T(8,128)(2,1)}, bf16[480,384]{1,0:T(8,128)(2,1)}, bf16[864,384]{1,0:T(8,128)(2,1)}, bf16[8...) custom-call(s32[6,1,144]{2,1,0:T(1,128)} %compare_select_fusion.key_ref, bf16[480,384]{1,0:T(8,128)(2,1)} %fusion.92.ql, ...), custom_call_target="tpu_custom_call" | custom-call | flops 5898240000 | bytes 30000000 | tf_op jit(solution)/shard_map/pallas_call | solution.py:129
  509.1 20.7 %shard_map.260 = (bf16[480,384]{1,0:T(8,128)(2,1)}, bf16[480,384]{1,0:T(8,128)(2,1)}, bf16[480,384]{1,0:T(8,128)(2,1)}, bf16[864,384]{1,0:T(8,128)(2,1)}, bf16[8...) custom-call(s32[6,1,144]{2,1,0:T(1,128)} %compare_select_fusion.key_ref, bf16[480,384]{1,0:T(8,128)(2,1)} %fusion.83.ql, ...), custom_call_target="tpu_custom_call" | custom-call | flops 5898240000 | bytes 30000000 | tf_op jit(solution)/shard_map/pallas_call | solution.py:129
  562.9 4.4 fusion.299
  567.4 4.4 fusion.298
  571.7 4.4 fusion.295
  576.2 4.6 fusion.294
  606.5 5.3 copy.61
  614.3 3.7 pad_maximum_fusion.6
  618.0 5.3 copy.66
  625.8 3.7 pad_maximum_fusion.5
  629.5 5.3 copy.62
  637.2 3.7 pad_maximum_fusion.7
  640.9 5.4 copy.67
  649.0 3.7 convolution_add_fusion.10
  678.1 5.5 copy.57
  691.9 5.3 copy.56
  711.9 3.6 add_add_fusion.6
  749.3 6.8 collective-permute-done.70
  757.9 4.0 collective-permute-done.58
  768.9 3.6 collective-permute-done.71
  814.3 6.2 rev.37
  827.5 6.4 rev.43
  840.8 6.2 rev.46
  851.9 6.2 rev.40
  859.5 3.7 fusion.27
  870.7 6.2 rev.36
  881.7 6.2 rev.42
  892.6 6.2 rev.45
  900.8 3.6 reshape.945
  904.4 11.6 %rev.39 = bf16[8,48,2,2,384]{4,3,2,1,0:T(2,128)(2,1)} reverse(bf16[8,48,2,2,384]{4,3,2,1,0:T(2,128)(2,1)} %reshape.945), dimensions={3} | reverse | bytes 2359296 | tf_op jit(solution)/shard_map/rev | solution.py:223
  916.0 4.1 reshape.983
  928.6 14.3 %collective-permute-done.35 = bf16[8,48,1152]{2,1,0:T(8,128)(2,1)S(1)} collective-permute-done((bf16[8,48,1152]{2,1,0:T(8,128)(2,1)}, bf16[8,48,1152]{2,1,0:T(8,128)(2,1)S(1)}, u32[]{:S(2)}, u32[]{:S(2)}) %collective-permute-start.35) | collective-permute-done | bytes 884768 | tf_op jit(solution)/shard_map/ppermute | solution.py:171
  946.0 7.9 collective-permute-done.42
  955.4 8.7 collective-permute-done.48
  965.8 7.6 collective-permute-done.36
  977.8 15.6 %collective-permute-done.88 = bf16[8,48,1536]{2,1,0:T(8,128)(2,1)S(1)} collective-permute-done((bf16[8,48,1536]{2,1,0:T(8,128)(2,1)S(1)}, bf16[8,48,1536]{2,1,0:T(8,128)(2,1)S(1)}, u32[]{:S(2)}, u32[]{:S(2)}) %collective-permute-start.88) | collective-permute-done | bytes 1179680 | tf_op jit(solution)/shard_map/ppermute | solution.py:171
  996.6 22.1 %collective-permute-done.94 = bf16[8,48,1536]{2,1,0:T(8,128)(2,1)S(1)} collective-permute-done((bf16[8,48,1536]{2,1,0:T(8,128)(2,1)S(1)}, bf16[8,48,1536]{2,1,0:T(8,128)(2,1)S(1)}, u32[]{:S(2)}, u32[]{:S(2)}) %collective-permute-start.94) | collective-permute-done | bytes 1179680 | tf_op jit(solution)/shard_map/ppermute | solution.py:171
  1023.9 19.5 %collective-permute-done.82 = bf16[8,48,1536]{2,1,0:T(8,128)(2,1)S(1)} collective-permute-done((bf16[8,48,1536]{2,1,0:T(8,128)(2,1)S(1)}, bf16[8,48,1536]{2,1,0:T(8,128)(2,1)S(1)}, u32[]{:S(2)}, u32[]{:S(2)}) %collective-permute-start.82) | collective-permute-done | bytes 1179680 | tf_op jit(solution)/shard_map/ppermute | solution.py:171
  1052.5 4.5 collective-permute-done.44
  1058.1 7.1 collective-permute-done.50
  1124.8 3.8 collective-permute-done.84
  1128.8 8.4 collective-permute-done.91
  (1175 shorter events, 616.5 us)
Async XLA Ops:
  2.7 65.0 %collective-permute-start.4 = (bf16[5376]{0:T(1024)(128)(2,1)}, bf16[5376]{0:T(1024)(128)(2,1)}, u32[]{:S(2)}, u32[]{:S(2)}) collective-permute-start(bf16[5376]{0:T(1024)(128)(2,1)} %pad_maximum_fusion.13), channel_id=1, source_target_pairs={{0,1},{1,0},{2,3},{3,2},{4,5},{5,4},{6,7},{7,6},{8,9},{9,8},{10,11... | collective-permute-start | bytes 32264 | tf_op jit(solution)/shard_map/ppermute | solution.py:171
  7.9 65.2 %collective-permute-start.17 = (bf16[96,768]{1,0:T(8,128)(2,1)}, bf16[96,768]{1,0:T(8,128)(2,1)}, u32[]{:S(2)}, u32[]{:S(2)}) collective-permute-start(bf16[96,768]{1,0:T(8,128)(2,1)} %dynamic-slice_bitcast_fusion.4), channel_id=1, source_target_pairs={{0,1},{1,0},{2,3},{3,2},{4,5},{5,4},{6,7},{7,6},{8,9},{9,8},{10,11... | collective-permute-start | bytes 442376 | tf_op jit(solution)/shard_map/ppermute | solution.py:171
  8.6 67.5 %collective-permute-start.5 = (bf16[96,768]{1,0:T(8,128)(2,1)}, bf16[96,768]{1,0:T(8,128)(2,1)}, u32[]{:S(2)}, u32[]{:S(2)}) collective-permute-start(bf16[96,768]{1,0:T(8,128)(2,1)} %dynamic-slice_bitcast_fusion.5), channel_id=1, source_target_pairs={{0,1},{1,0},{2,3},{3,2},{4,5},{5,4},{6,7},{7,6},{8,9},{9,8},{10,11... | collective-permute-start | bytes 442376 | tf_op jit(solution)/shard_map/ppermute | solution.py:171
  11.3 67.3 %collective-permute-start.29 = (bf16[96,768]{1,0:T(8,128)(2,1)}, bf16[96,768]{1,0:T(8,128)(2,1)}, u32[]{:S(2)}, u32[]{:S(2)}) collective-permute-start(bf16[96,768]{1,0:T(8,128)(2,1)} %dynamic-slice_bitcast_fusion.3), channel_id=1, source_target_pairs={{0,1},{1,0},{2,3},{3,2},{4,5},{5,4},{6,7},{7,6},{8,9},{9,8},{10,11... | collective-permute-start | bytes 442376 | tf_op jit(solution)/shard_map/ppermute | solution.py:171
  17.1 77.5 %collective-permute-start.9 = (bf16[3,192,384]{2,1,0:T(8,128)(2,1)}, bf16[3,192,384]{2,1,0:T(8,128)(2,1)}, u32[]{:S(2)}, u32[]{:S(2)}) collective-permute-start(bf16[3,192,384]{2,1,0:T(8,128)(2,1)} %dynamic-slice_bitcast_fusion.1), channel_id=1, source_target_pairs={{0,1},{1,0},{2,3},{3,2},{4,5},{5,4},{6,7},{7,6},{8,9},{9,8},{10,11... | collective-permute-start | bytes 1327112 | tf_op jit(solution)/shard_map/ppermute | solution.py:171
  67.7 28.8 %collective-permute-start = (bf16[3,192,384]{2,1,0:T(8,128)(2,1)}, bf16[3,192,384]{2,1,0:T(8,128)(2,1)}, u32[]{:S(2)}, u32[]{:S(2)}) collective-permute-start(bf16[3,192,384]{2,1,0:T(8,128)(2,1)} %dynamic-slice_bitcast_fusion.2), channel_id=1, source_target_pairs={{0,1},{1,0},{2,3},{3,2},{4,5},{5,4},{6,7},{7,6},{8,9},{9,8},{10,11... | collective-permute-start | bytes 1327112 | tf_op jit(solution)/shard_map/ppermute | solution.py:171
  73.0 27.4 %collective-permute-start.13 = (bf16[3,192,384]{2,1,0:T(8,128)(2,1)}, bf16[3,192,384]{2,1,0:T(8,128)(2,1)S(1)}, u32[]{:S(2)}, u32[]{:S(2)}) collective-permute-start(bf16[3,192,384]{2,1,0:T(8,128)(2,1)} %dynamic-slice_bitcast_fusion), channel_id=1, source_target_pairs={{0,1},{1,0},{2,3},{3,2},{4,5},{5,4},{6,7},{7,6},{8,9},{9,8},{10,11... | collective-permute-start | bytes 1327112 | tf_op jit(solution)/shard_map/ppermute | solution.py:171
  96.5 12.6 %collective-permute-start.11 = (bf16[3,192,384]{2,1,0:T(8,128)(2,1)}, bf16[3,192,384]{2,1,0:T(8,128)(2,1)}, u32[]{:S(2)}, u32[]{:S(2)}) collective-permute-start(bf16[3,192,384]{2,1,0:T(8,128)(2,1)} %collective-permute-done.9), channel_id=1, source_target_pairs={{0,4},{1,5},{2,6},{3,7},{4,0},{5,1},{6,2},{7,3},{8,12},{9,13},{10,... | collective-permute-start | bytes 1327112 | tf_op jit(solution)/shard_map/ppermute | solution.py:177
  99.3 32.7 %collective-permute-start.21 = (bf16[2,768,384]{2,1,0:T(8,128)(2,1)S(1)}, bf16[2,768,384]{2,1,0:T(8,128)(2,1)}, u32[]{:S(2)}, u32[]{:S(2)}) collective-permute-start(bf16[2,768,384]{2,1,0:T(8,128)(2,1)S(1)} %copy-done.72), channel_id=1, source_target_pairs={{0,1},{1,0},{2,3},{3,2},{4,5},{5,4},{6,7},{7,6},{8,9},{9,8},{10,11... | collective-permute-start | bytes 3538952 | tf_op jit(solution)/shard_map/ppermute | solution.py:171
  100.5 52.1 %collective-permute-start.25 = (bf16[2,384,768]{2,1,0:T(8,128)(2,1)S(1)}, bf16[2,384,768]{2,1,0:T(8,128)(2,1)}, u32[]{:S(2)}, u32[]{:S(2)}) collective-permute-start(bf16[2,384,768]{2,1,0:T(8,128)(2,1)S(1)} %copy-done.70), channel_id=1, source_target_pairs={{0,1},{1,0},{2,3},{3,2},{4,5},{5,4},{6,7},{7,6},{8,9},{9,8},{10,11... | collective-permute-start | bytes 3538952 | tf_op jit(solution)/shard_map/ppermute | solution.py:171
  109.1 13.2 %collective-permute-start.2 = (bf16[3,192,384]{2,1,0:T(8,128)(2,1)}, bf16[3,192,384]{2,1,0:T(8,128)(2,1)S(1)}, u32[]{:S(2)}, u32[]{:S(2)}) collective-permute-start(bf16[3,192,384]{2,1,0:T(8,128)(2,1)} %collective-permute-done), channel_id=1, source_target_pairs={{0,4},{1,5},{2,6},{3,7},{4,0},{5,1},{6,2},{7,3},{8,12},{9,13},{10,... | collective-permute-start | bytes 1327112 | tf_op jit(solution)/shard_map/ppermute | solution.py:177
  110.6 19.6 %collective-permute-start.15 = (bf16[3,192,384]{2,1,0:T(8,128)(2,1)S(1)}, bf16[3,192,384]{2,1,0:T(8,128)(2,1)}, u32[]{:S(2)}, u32[]{:S(2)}) collective-permute-start(bf16[3,192,384]{2,1,0:T(8,128)(2,1)S(1)} %collective-permute-done.13), channel_id=1, source_target_pairs={{0,4},{1,5},{2,6},{3,7},{4,0},{5,1},{6,2},{7,3},{8,12},{9,13},{10,... | collective-permute-start | bytes 1327112 | tf_op jit(solution)/shard_map/ppermute | solution.py:177
  111.2 19.0 %collective-permute-start.14 = (bf16[3,192,384]{2,1,0:T(8,128)(2,1)S(1)}, bf16[3,192,384]{2,1,0:T(8,128)(2,1)S(1)}, u32[]{:S(2)}, u32[]{:S(2)}) collective-permute-start(bf16[3,192,384]{2,1,0:T(8,128)(2,1)S(1)} %collective-permute-done.13), channel_id=1, source_target_pairs={{0,2},{1,3},{2,0},{3,1},{4,6},{5,7},{6,4},{7,5},{8,10},{9,11},{10,... | collective-permute-start | bytes 1327112 | tf_op jit(solution)/shard_map/ppermute | solution.py:177
  122.4 56.8 %collective-permute-start.12 = (bf16[3,192,384]{2,1,0:T(8,128)(2,1)}, bf16[3,192,384]{2,1,0:T(8,128)(2,1)}, u32[]{:S(2)}, u32[]{:S(2)}) collective-permute-start(bf16[3,192,384]{2,1,0:T(8,128)(2,1)} %collective-permute-done.11), channel_id=1, source_target_pairs={{0,2},{1,3},{2,0},{3,1},{4,6},{5,7},{6,4},{7,5},{8,10},{9,11},{10,... | collective-permute-start | bytes 1327112 | tf_op jit(solution)/shard_map/ppermute | solution.py:177
  130.3 24.6 %collective-permute-start.3 = (bf16[3,192,384]{2,1,0:T(8,128)(2,1)S(1)}, bf16[3,192,384]{2,1,0:T(8,128)(2,1)S(1)}, u32[]{:S(2)}, u32[]{:S(2)}) collective-permute-start(bf16[3,192,384]{2,1,0:T(8,128)(2,1)S(1)} %collective-permute-done.2), channel_id=1, source_target_pairs={{0,2},{1,3},{2,0},{3,1},{4,6},{5,7},{6,4},{7,5},{8,10},{9,11},{10,... | collective-permute-start | bytes 1327112 | tf_op jit(solution)/shard_map/ppermute | solution.py:177
  130.3 61.6 %collective-permute-start.16 = (bf16[3,192,384]{2,1,0:T(8,128)(2,1)}, bf16[3,192,384]{2,1,0:T(8,128)(2,1)}, u32[]{:S(2)}, u32[]{:S(2)}) collective-permute-start(bf16[3,192,384]{2,1,0:T(8,128)(2,1)} %collective-permute-done.15), channel_id=1, source_target_pairs={{0,2},{1,3},{2,0},{3,1},{4,6},{5,7},{6,4},{7,5},{8,10},{9,11},{10,... | collective-permute-start | bytes 1327112 | tf_op jit(solution)/shard_map/ppermute | solution.py:177
  132.0 125.9 %collective-permute-start.23 = (bf16[2,768,384]{2,1,0:T(8,128)(2,1)}, bf16[2,768,384]{2,1,0:T(8,128)(2,1)}, u32[]{:S(2)}, u32[]{:S(2)}) collective-permute-start(bf16[2,768,384]{2,1,0:T(8,128)(2,1)} %collective-permute-done.21), channel_id=1, source_target_pairs={{0,4},{1,5},{2,6},{3,7},{4,0},{5,1},{6,2},{7,3},{8,12},{9,13},{10,... | collective-permute-start | bytes 3538952 | tf_op jit(solution)/shard_map/ppermute | solution.py:177
  152.5 111.1 %collective-permute-start.22 = (bf16[2,768,384]{2,1,0:T(8,128)(2,1)}, bf16[2,768,384]{2,1,0:T(8,128)(2,1)}, u32[]{:S(2)}, u32[]{:S(2)}) collective-permute-start(bf16[2,768,384]{2,1,0:T(8,128)(2,1)} %collective-permute-done.21), channel_id=1, source_target_pairs={{0,2},{1,3},{2,0},{3,1},{4,6},{5,7},{6,4},{7,5},{8,10},{9,11},{10,... | collective-permute-start | bytes 3538952 | tf_op jit(solution)/shard_map/ppermute | solution.py:177
  154.9 108.4 %collective-permute-start.27 = (bf16[2,384,768]{2,1,0:T(8,128)(2,1)}, bf16[2,384,768]{2,1,0:T(8,128)(2,1)}, u32[]{:S(2)}, u32[]{:S(2)}) collective-permute-start(bf16[2,384,768]{2,1,0:T(8,128)(2,1)} %collective-permute-done.25), channel_id=1, source_target_pairs={{0,4},{1,5},{2,6},{3,7},{4,0},{5,1},{6,2},{7,3},{8,12},{9,13},{10,... | collective-permute-start | bytes 3538952 | tf_op jit(solution)/shard_map/ppermute | solution.py:177
  179.1 87.5 %collective-permute-start.26 = (bf16[2,384,768]{2,1,0:T(8,128)(2,1)}, bf16[2,384,768]{2,1,0:T(8,128)(2,1)}, u32[]{:S(2)}, u32[]{:S(2)}) collective-permute-start(bf16[2,384,768]{2,1,0:T(8,128)(2,1)} %collective-permute-done.25), channel_id=1, source_target_pairs={{0,2},{1,3},{2,0},{3,1},{4,6},{5,7},{6,4},{7,5},{8,10},{9,11},{10,... | collective-permute-start | bytes 3538952 | tf_op jit(solution)/shard_map/ppermute | solution.py:177
  257.9 11.5 %collective-permute-start.24 = (bf16[2,768,384]{2,1,0:T(8,128)(2,1)}, bf16[2,768,384]{2,1,0:T(8,128)(2,1)S(1)}, u32[]{:S(2)}, u32[]{:S(2)}) collective-permute-start(bf16[2,768,384]{2,1,0:T(8,128)(2,1)} %collective-permute-done.23), channel_id=1, source_target_pairs={{0,2},{1,3},{2,0},{3,1},{4,6},{5,7},{6,4},{7,5},{8,10},{9,11},{10,... | collective-permute-start | bytes 3538952 | tf_op jit(solution)/shard_map/ppermute | solution.py:177
  263.3 15.7 %collective-permute-start.28 = (bf16[2,384,768]{2,1,0:T(8,128)(2,1)}, bf16[2,384,768]{2,1,0:T(8,128)(2,1)S(1)}, u32[]{:S(2)}, u32[]{:S(2)}) collective-permute-start(bf16[2,384,768]{2,1,0:T(8,128)(2,1)} %collective-permute-done.27), channel_id=1, source_target_pairs={{0,2},{1,3},{2,0},{3,1},{4,6},{5,7},{6,4},{7,5},{8,10},{9,11},{10,... | collective-permute-start | bytes 3538952 | tf_op jit(solution)/shard_map/ppermute | solution.py:177
  585.6 142.5 %collective-permute-start.63 = (bf16[8,48,384]{2,1,0:T(8,128)(2,1)}, bf16[8,48,384]{2,1,0:T(8,128)(2,1)}, u32[]{:S(2)}, u32[]{:S(2)}) collective-permute-start(bf16[8,48,384]{2,1,0:T(8,128)(2,1)} %fusion.210), channel_id=1, source_target_pairs={{0,2},{1,3},{2,0},{3,1},{4,6},{5,7},{6,4},{7,5},{8,10},{9,11},{10,... | collective-permute-start | bytes 884744 | tf_op jit(solution)/shard_map/ppermute | solution.py:177
  585.8 160.2 %collective-permute-start.62 = (bf16[8,48,384]{2,1,0:T(8,128)(2,1)S(1)}, bf16[8,48,384]{2,1,0:T(8,128)(2,1)}, u32[]{:S(2)}, u32[]{:S(2)}) collective-permute-start(bf16[8,48,384]{2,1,0:T(8,128)(2,1)S(1)} %fusion.209), channel_id=1, source_target_pairs={{0,2},{1,3},{2,0},{3,1},{4,6},{5,7},{6,4},{7,5},{8,10},{9,11},{10,... | collective-permute-start | bytes 884744 | tf_op jit(solution)/shard_map/ppermute | solution.py:177
  588.9 222.3 %collective-permute-start.75 = (bf16[8,48,1536]{2,1,0:T(8,128)(2,1)}, bf16[8,48,1536]{2,1,0:T(8,128)(2,1)}, u32[]{:S(2)}, u32[]{:S(2)}) collective-permute-start(bf16[8,48,1536]{2,1,0:T(8,128)(2,1)} %fusion.95), channel_id=1, source_target_pairs={{0,2},{1,3},{2,0},{3,1},{4,6},{5,7},{6,4},{7,5},{8,10},{9,11},{10,... | collective-permute-start | bytes 3538952 | tf_op jit(solution)/shard_map/ppermute | solution.py:177
  600.3 130.1 %collective-permute-start.69 = (bf16[8,48,384]{2,1,0:T(8,128)(2,1)}, bf16[8,48,384]{2,1,0:T(8,128)(2,1)}, u32[]{:S(2)}, u32[]{:S(2)}) collective-permute-start(bf16[8,48,384]{2,1,0:T(8,128)(2,1)} %fusion.212), channel_id=1, source_target_pairs={{0,2},{1,3},{2,0},{3,1},{4,6},{5,7},{6,4},{7,5},{8,10},{9,11},{10,... | collective-permute-start | bytes 884744 | tf_op jit(solution)/shard_map/ppermute | solution.py:177
  663.5 57.5 %collective-permute-start.51 = (f32[22272]{0:T(1024)}, f32[22272]{0:T(1024)}, u32[]{:S(2)}, u32[]{:S(2)}) collective-permute-start(f32[22272]{0:T(1024)} %constant_dynamic-update-slice_fusion.37), channel_id=1, source_target_pairs={{0,1},{1,0},{2,3},{3,2},{4,5},{5,4},{6,7},{7,6},{8,9},{9,8},{10,11... | collective-permute-start | bytes 267272 | tf_op jit(solution)/shard_map/ppermute | solution.py:171
  728.1 21.1 %collective-permute-start.68 = (bf16[8,48,384]{2,1,0:T(8,128)(2,1)S(1)}, bf16[8,48,384]{2,1,0:T(8,128)(2,1)}, u32[]{:S(2)}, u32[]{:S(2)}) collective-permute-start(bf16[8,48,384]{2,1,0:T(8,128)(2,1)S(1)} %fusion.211), channel_id=1, source_target_pairs={{0,2},{1,3},{2,0},{3,1},{4,6},{5,7},{6,4},{7,5},{8,10},{9,11},{10,... | collective-permute-start | bytes 884744 | tf_op jit(solution)/shard_map/ppermute | solution.py:177
  742.2 15.1 %collective-permute-start.56 = (bf16[8,48,384]{2,1,0:T(8,128)(2,1)}, bf16[8,48,384]{2,1,0:T(8,128)(2,1)}, u32[]{:S(2)}, u32[]{:S(2)}) collective-permute-start(bf16[8,48,384]{2,1,0:T(8,128)(2,1)} %fusion.213), channel_id=1, source_target_pairs={{0,2},{1,3},{2,0},{3,1},{4,6},{5,7},{6,4},{7,5},{8,10},{9,11},{10,... | collective-permute-start | bytes 884744 | tf_op jit(solution)/shard_map/ppermute | solution.py:177
  746.4 15.5 %collective-permute-start.58 = (bf16[8,48,384]{2,1,0:T(8,128)(2,1)}, bf16[8,48,384]{2,1,0:T(8,128)(2,1)S(1)}, u32[]{:S(2)}, u32[]{:S(2)}) collective-permute-start(bf16[8,48,384]{2,1,0:T(8,128)(2,1)} %fusion.116), channel_id=1, source_target_pairs={{0,1},{1,0},{2,3},{3,2},{4,5},{5,4},{6,7},{7,6},{8,9},{9,8},{10,11... | collective-permute-start | bytes 884744 | tf_op jit(solution)/shard_map/ppermute | solution.py:171
  749.2 109.7 %collective-permute-start.74 = (bf16[8,48,1536]{2,1,0:T(8,128)(2,1)}, bf16[8,48,1536]{2,1,0:T(8,128)(2,1)}, u32[]{:S(2)}, u32[]{:S(2)}) collective-permute-start(bf16[8,48,1536]{2,1,0:T(8,128)(2,1)} %fusion.94), channel_id=1, source_target_pairs={{0,2},{1,3},{2,0},{3,1},{4,6},{5,7},{6,4},{7,5},{8,10},{9,11},{10,... | collective-permute-start | bytes 3538952 | tf_op jit(solution)/shard_map/ppermute | solution.py:177
  756.1 50.1 %collective-permute-start.40 = (bf16[8,48,1152]{2,1,0:T(8,128)(2,1)}, bf16[8,48,1152]{2,1,0:T(8,128)(2,1)S(1)}, u32[]{:S(2)}, u32[]{:S(2)}) collective-permute-start(bf16[8,48,1152]{2,1,0:T(8,128)(2,1)} %fusion.106), channel_id=1, source_target_pairs={{0,2},{1,3},{2,0},{3,1},{4,6},{5,7},{6,4},{7,5},{8,10},{9,11},{10,... | collective-permute-start | bytes 2654216 | tf_op jit(solution)/shard_map/ppermute | solution.py:177
  757.3 50.4 %collective-permute-start.46 = (bf16[8,48,1152]{2,1,0:T(8,128)(2,1)}, bf16[8,48,1152]{2,1,0:T(8,128)(2,1)S(1)}, u32[]{:S(2)}, u32[]{:S(2)}) collective-permute-start(bf16[8,48,1152]{2,1,0:T(8,128)(2,1)} %fusion.107), channel_id=1, source_target_pairs={{0,2},{1,3},{2,0},{3,1},{4,6},{5,7},{6,4},{7,5},{8,10},{9,11},{10,... | collective-permute-start | bytes 2654216 | tf_op jit(solution)/shard_map/ppermute | solution.py:177
  805.4 15.8 %collective-permute-start.87 = (bf16[8,48,1536]{2,1,0:T(8,128)(2,1)}, bf16[8,48,1536]{2,1,0:T(8,128)(2,1)}, u32[]{:S(2)}, u32[]{:S(2)}) collective-permute-start(bf16[8,48,1536]{2,1,0:T(8,128)(2,1)} %fusion.99), channel_id=1, source_target_pairs={{0,2},{1,3},{2,0},{3,1},{4,6},{5,7},{6,4},{7,5},{8,10},{9,11},{10,... | collective-permute-start | bytes 3538952 | tf_op jit(solution)/shard_map/ppermute | solution.py:177
  807.8 26.8 %collective-permute-start.93 = (bf16[8,48,1536]{2,1,0:T(8,128)(2,1)}, bf16[8,48,1536]{2,1,0:T(8,128)(2,1)}, u32[]{:S(2)}, u32[]{:S(2)}) collective-permute-start(bf16[8,48,1536]{2,1,0:T(8,128)(2,1)} %fusion.101), channel_id=1, source_target_pairs={{0,2},{1,3},{2,0},{3,1},{4,6},{5,7},{6,4},{7,5},{8,10},{9,11},{10,... | collective-permute-start | bytes 3538952 | tf_op jit(solution)/shard_map/ppermute | solution.py:177
  809.7 39.0 %collective-permute-start.81 = (bf16[8,48,1536]{2,1,0:T(8,128)(2,1)}, bf16[8,48,1536]{2,1,0:T(8,128)(2,1)}, u32[]{:S(2)}, u32[]{:S(2)}) collective-permute-start(bf16[8,48,1536]{2,1,0:T(8,128)(2,1)} %fusion.97), channel_id=1, source_target_pairs={{0,2},{1,3},{2,0},{3,1},{4,6},{5,7},{6,4},{7,5},{8,10},{9,11},{10,... | collective-permute-start | bytes 3538952 | tf_op jit(solution)/shard_map/ppermute | solution.py:177
  811.2 52.0 %collective-permute-start.86 = (bf16[8,48,1536]{2,1,0:T(8,128)(2,1)}, bf16[8,48,1536]{2,1,0:T(8,128)(2,1)}, u32[]{:S(2)}, u32[]{:S(2)}) collective-permute-start(bf16[8,48,1536]{2,1,0:T(8,128)(2,1)} %fusion.98), channel_id=1, source_target_pairs={{0,2},{1,3},{2,0},{3,1},{4,6},{5,7},{6,4},{7,5},{8,10},{9,11},{10,... | collective-permute-start | bytes 3538952 | tf_op jit(solution)/shard_map/ppermute | solution.py:177
  821.3 41.9 %collective-permute-start.92 = (bf16[8,48,1536]{2,1,0:T(8,128)(2,1)}, bf16[8,48,1536]{2,1,0:T(8,128)(2,1)}, u32[]{:S(2)}, u32[]{:S(2)}) collective-permute-start(bf16[8,48,1536]{2,1,0:T(8,128)(2,1)} %fusion.100), channel_id=1, source_target_pairs={{0,2},{1,3},{2,0},{3,1},{4,6},{5,7},{6,4},{7,5},{8,10},{9,11},{10,... | collective-permute-start | bytes 3538952 | tf_op jit(solution)/shard_map/ppermute | solution.py:177
  834.6 66.0 %collective-permute-start.80 = (bf16[8,48,1536]{2,1,0:T(8,128)(2,1)}, bf16[8,48,1536]{2,1,0:T(8,128)(2,1)}, u32[]{:S(2)}, u32[]{:S(2)}) collective-permute-start(bf16[8,48,1536]{2,1,0:T(8,128)(2,1)} %fusion.96), channel_id=1, source_target_pairs={{0,2},{1,3},{2,0},{3,1},{4,6},{5,7},{6,4},{7,5},{8,10},{9,11},{10,... | collective-permute-start | bytes 3538952 | tf_op jit(solution)/shard_map/ppermute | solution.py:177
  848.7 71.3 %collective-permute-start.39 = (bf16[8,48,1152]{2,1,0:T(8,128)(2,1)}, bf16[8,48,1152]{2,1,0:T(8,128)(2,1)}, u32[]{:S(2)}, u32[]{:S(2)}) collective-permute-start(bf16[8,48,1152]{2,1,0:T(8,128)(2,1)} %fusion.103), channel_id=1, source_target_pairs={{0,2},{1,3},{2,0},{3,1},{4,6},{5,7},{6,4},{7,5},{8,10},{9,11},{10,... | collective-permute-start | bytes 2654216 | tf_op jit(solution)/shard_map/ppermute | solution.py:177
  858.9 61.7 %collective-permute-start.41 = (bf16[8,48,1152]{2,1,0:T(8,128)(2,1)}, bf16[8,48,1152]{2,1,0:T(8,128)(2,1)}, u32[]{:S(2)}, u32[]{:S(2)}) collective-permute-start(bf16[8,48,1152]{2,1,0:T(8,128)(2,1)} %fusion.56), channel_id=1, source_target_pairs={{0,1},{1,0},{2,3},{3,2},{4,5},{5,4},{6,7},{7,6},{8,9},{9,8},{10,11... | collective-permute-start | bytes 2654216 | tf_op jit(solution)/shard_map/ppermute | solution.py:171
  863.2 60.7 %collective-permute-start.45 = (bf16[8,48,1152]{2,1,0:T(8,128)(2,1)}, bf16[8,48,1152]{2,1,0:T(8,128)(2,1)}, u32[]{:S(2)}, u32[]{:S(2)}) collective-permute-start(bf16[8,48,1152]{2,1,0:T(8,128)(2,1)} %fusion.104), channel_id=1, source_target_pairs={{0,2},{1,3},{2,0},{3,1},{4,6},{5,7},{6,4},{7,5},{8,10},{9,11},{10,... | collective-permute-start | bytes 2654216 | tf_op jit(solution)/shard_map/ppermute | solution.py:177
  863.2 61.3 %collective-permute-start.47 = (bf16[8,48,1152]{2,1,0:T(8,128)(2,1)}, bf16[8,48,1152]{2,1,0:T(8,128)(2,1)}, u32[]{:S(2)}, u32[]{:S(2)}) collective-permute-start(bf16[8,48,1152]{2,1,0:T(8,128)(2,1)} %fusion.54), channel_id=1, source_target_pairs={{0,1},{1,0},{2,3},{3,2},{4,5},{5,4},{6,7},{7,6},{8,9},{9,8},{10,11... | collective-permute-start | bytes 2654216 | tf_op jit(solution)/shard_map/ppermute | solution.py:171
  900.6 27.4 %collective-permute-start.33 = (bf16[8,48,1152]{2,1,0:T(8,128)(2,1)}, bf16[8,48,1152]{2,1,0:T(8,128)(2,1)}, u32[]{:S(2)}, u32[]{:S(2)}) collective-permute-start(bf16[8,48,1152]{2,1,0:T(8,128)(2,1)} %fusion.102), channel_id=1, source_target_pairs={{0,2},{1,3},{2,0},{3,1},{4,6},{5,7},{6,4},{7,5},{8,10},{9,11},{10,... | collective-permute-start | bytes 2654216 | tf_op jit(solution)/shard_map/ppermute | solution.py:177
  920.1 22.8 %collective-permute-start.35 = (bf16[8,48,1152]{2,1,0:T(8,128)(2,1)}, bf16[8,48,1152]{2,1,0:T(8,128)(2,1)S(1)}, u32[]{:S(2)}, u32[]{:S(2)}) collective-permute-start(bf16[8,48,1152]{2,1,0:T(8,128)(2,1)} %fusion.58), channel_id=1, source_target_pairs={{0,1},{1,0},{2,3},{3,2},{4,5},{5,4},{6,7},{7,6},{8,9},{9,8},{10,11... | collective-permute-start | bytes 2654216 | tf_op jit(solution)/shard_map/ppermute | solution.py:171
  920.6 55.5 %collective-permute-start.76 = (bf16[8,48,1536]{2,1,0:T(8,128)(2,1)}, bf16[8,48,1536]{2,1,0:T(8,128)(2,1)S(1)}, u32[]{:S(2)}, u32[]{:S(2)}) collective-permute-start(bf16[8,48,1536]{2,1,0:T(8,128)(2,1)} %fusion.33), channel_id=1, source_target_pairs={{0,1},{1,0},{2,3},{3,2},{4,5},{5,4},{6,7},{7,6},{8,9},{9,8},{10,11... | collective-permute-start | bytes 3538952 | tf_op jit(solution)/shard_map/ppermute | solution.py:171
  923.9 69.5 %collective-permute-start.88 = (bf16[8,48,1536]{2,1,0:T(8,128)(2,1)S(1)}, bf16[8,48,1536]{2,1,0:T(8,128)(2,1)S(1)}, u32[]{:S(2)}, u32[]{:S(2)}) collective-permute-start(bf16[8,48,1536]{2,1,0:T(8,128)(2,1)S(1)} %copy-done.136), channel_id=1, source_target_pairs={{0,1},{1,0},{2,3},{3,2},{4,5},{5,4},{6,7},{7,6},{8,9},{9,8},{10,11... | collective-permute-start | bytes 3538952 | tf_op jit(solution)/shard_map/ppermute | solution.py:171
  924.5 94.2 %collective-permute-start.94 = (bf16[8,48,1536]{2,1,0:T(8,128)(2,1)S(1)}, bf16[8,48,1536]{2,1,0:T(8,128)(2,1)S(1)}, u32[]{:S(2)}, u32[]{:S(2)}) collective-permute-start(bf16[8,48,1536]{2,1,0:T(8,128)(2,1)S(1)} %copy-done.138), channel_id=1, source_target_pairs={{0,1},{1,0},{2,3},{3,2},{4,5},{5,4},{6,7},{7,6},{8,9},{9,8},{10,11... | collective-permute-start | bytes 3538952 | tf_op jit(solution)/shard_map/ppermute | solution.py:171
  928.0 115.4 %collective-permute-start.82 = (bf16[8,48,1536]{2,1,0:T(8,128)(2,1)S(1)}, bf16[8,48,1536]{2,1,0:T(8,128)(2,1)S(1)}, u32[]{:S(2)}, u32[]{:S(2)}) collective-permute-start(bf16[8,48,1536]{2,1,0:T(8,128)(2,1)S(1)} %copy-done.137), channel_id=1, source_target_pairs={{0,1},{1,0},{2,3},{3,2},{4,5},{5,4},{6,7},{7,6},{8,9},{9,8},{10,11... | collective-permute-start | bytes 3538952 | tf_op jit(solution)/shard_map/ppermute | solution.py:171
  973.4 73.1 %collective-permute-start.43 = (bf16[2,48,1152]{2,1,0:T(8,128)(2,1)S(1)}, bf16[2,48,1152]{2,1,0:T(8,128)(2,1)S(1)}, u32[]{:S(2)}, u32[]{:S(2)}) collective-permute-start(bf16[2,48,1152]{2,1,0:T(8,128)(2,1)S(1)} %fusion.216), channel_id=1, source_target_pairs={{0,8},{1,9},{2,10},{3,11},{4,12},{5,13},{6,14},{7,15},{8,0},{9,1},... | collective-permute-start | bytes 663560 | tf_op jit(solution)/shard_map/ppermute | solution.py:177
  976.2 70.9 %collective-permute-start.49 = (bf16[2,48,1152]{2,1,0:T(8,128)(2,1)S(1)}, bf16[2,48,1152]{2,1,0:T(8,128)(2,1)S(1)}, u32[]{:S(2)}, u32[]{:S(2)}) collective-permute-start(bf16[2,48,1152]{2,1,0:T(8,128)(2,1)S(1)} %fusion.217), channel_id=1, source_target_pairs={{0,8},{1,9},{2,10},{3,11},{4,12},{5,13},{6,14},{7,15},{8,0},{9,1},... | collective-permute-start | bytes 663560 | tf_op jit(solution)/shard_map/ppermute | solution.py:177
  993.4 55.3 %collective-permute-start.37 = (bf16[2,48,1152]{2,1,0:T(8,128)(2,1)S(1)}, bf16[2,48,1152]{2,1,0:T(8,128)(2,1)S(1)}, u32[]{:S(2)}, u32[]{:S(2)}) collective-permute-start(bf16[2,48,1152]{2,1,0:T(8,128)(2,1)S(1)} %fusion.215), channel_id=1, source_target_pairs={{0,8},{1,9},{2,10},{3,11},{4,12},{5,13},{6,14},{7,15},{8,0},{9,1},... | collective-permute-start | bytes 663560 | tf_op jit(solution)/shard_map/ppermute | solution.py:177
  1018.7 58.7 %collective-permute-start.77 = (bf16[4,48,1536]{2,1,0:T(8,128)(2,1)}, bf16[4,48,1536]{2,1,0:T(8,128)(2,1)}, u32[]{:S(2)}, u32[]{:S(2)}) collective-permute-start(bf16[4,48,1536]{2,1,0:T(8,128)(2,1)} %fusion.108), channel_id=1, source_target_pairs={{0,4},{1,5},{2,6},{3,7},{4,0},{5,1},{6,2},{7,3},{8,12},{9,13},{10,... | collective-permute-start | bytes 1769480 | tf_op jit(solution)/shard_map/ppermute | solution.py:177
  1043.4 46.5 %collective-permute-start.89 = (bf16[4,48,1536]{2,1,0:T(8,128)(2,1)}, bf16[4,48,1536]{2,1,0:T(8,128)(2,1)}, u32[]{:S(2)}, u32[]{:S(2)}) collective-permute-start(bf16[4,48,1536]{2,1,0:T(8,128)(2,1)} %fusion.110), channel_id=1, source_target_pairs={{0,4},{1,5},{2,6},{3,7},{4,0},{5,1},{6,2},{7,3},{8,12},{9,13},{10,... | collective-permute-start | bytes 1769480 | tf_op jit(solution)/shard_map/ppermute | solution.py:177
  1046.4 56.6 %collective-permute-start.95 = (bf16[4,48,1536]{2,1,0:T(8,128)(2,1)}, bf16[4,48,1536]{2,1,0:T(8,128)(2,1)}, u32[]{:S(2)}, u32[]{:S(2)}) collective-permute-start(bf16[4,48,1536]{2,1,0:T(8,128)(2,1)} %fusion.111), channel_id=1, source_target_pairs={{0,4},{1,5},{2,6},{3,7},{4,0},{5,1},{6,2},{7,3},{8,12},{9,13},{10,... | collective-permute-start | bytes 1769480 | tf_op jit(solution)/shard_map/ppermute | solution.py:177
  1047.1 64.1 %collective-permute-start.83 = (bf16[4,48,1536]{2,1,0:T(8,128)(2,1)}, bf16[4,48,1536]{2,1,0:T(8,128)(2,1)}, u32[]{:S(2)}, u32[]{:S(2)}) collective-permute-start(bf16[4,48,1536]{2,1,0:T(8,128)(2,1)} %fusion.109), channel_id=1, source_target_pairs={{0,4},{1,5},{2,6},{3,7},{4,0},{5,1},{6,2},{7,3},{8,12},{9,13},{10,... | collective-permute-start | bytes 1769480 | tf_op jit(solution)/shard_map/ppermute | solution.py:177
  1089.3 27.0 %collective-permute-start.78 = (bf16[2,48,1536]{2,1,0:T(8,128)(2,1)}, bf16[2,48,1536]{2,1,0:T(8,128)(2,1)}, u32[]{:S(2)}, u32[]{:S(2)}) collective-permute-start(bf16[2,48,1536]{2,1,0:T(8,128)(2,1)} %fusion.205), channel_id=1, source_target_pairs={{0,8},{1,9},{2,10},{3,11},{4,12},{5,13},{6,14},{7,15},{8,0},{9,1},... | collective-permute-start | bytes 884744 | tf_op jit(solution)/shard_map/ppermute | solution.py:177
  1101.6 17.1 %collective-permute-start.90 = (bf16[2,48,1536]{2,1,0:T(8,128)(2,1)}, bf16[2,48,1536]{2,1,0:T(8,128)(2,1)}, u32[]{:S(2)}, u32[]{:S(2)}) collective-permute-start(bf16[2,48,1536]{2,1,0:T(8,128)(2,1)} %fusion.207), channel_id=1, source_target_pairs={{0,8},{1,9},{2,10},{3,11},{4,12},{5,13},{6,14},{7,15},{8,0},{9,1},... | collective-permute-start | bytes 884744 | tf_op jit(solution)/shard_map/ppermute | solution.py:177
  1110.6 13.0 %collective-permute-start.96 = (bf16[2,48,1536]{2,1,0:T(8,128)(2,1)}, bf16[2,48,1536]{2,1,0:T(8,128)(2,1)}, u32[]{:S(2)}, u32[]{:S(2)}) collective-permute-start(bf16[2,48,1536]{2,1,0:T(8,128)(2,1)} %fusion.208), channel_id=1, source_target_pairs={{0,8},{1,9},{2,10},{3,11},{4,12},{5,13},{6,14},{7,15},{8,0},{9,1},... | collective-permute-start | bytes 884744 | tf_op jit(solution)/shard_map/ppermute | solution.py:177
  1114.7 13.9 %collective-permute-start.84 = (bf16[2,48,1536]{2,1,0:T(8,128)(2,1)S(1)}, bf16[2,48,1536]{2,1,0:T(8,128)(2,1)S(1)}, u32[]{:S(2)}, u32[]{:S(2)}) collective-permute-start(bf16[2,48,1536]{2,1,0:T(8,128)(2,1)S(1)} %fusion.206), channel_id=1, source_target_pairs={{0,8},{1,9},{2,10},{3,11},{4,12},{5,13},{6,14},{7,15},{8,0},{9,1},... | collective-permute-start | bytes 884744 | tf_op jit(solution)/shard_map/ppermute | solution.py:177
  1117.3 21.6 %collective-permute-start.79 = (bf16[1,48,1536]{2,1,0:T(8,128)(2,1)S(1)}, bf16[1,48,1536]{2,1,0:T(8,128)(2,1)S(1)}, u32[]{:S(2)}, u32[]{:S(2)}) collective-permute-start(bf16[1,48,1536]{2,1,0:T(8,128)(2,1)S(1)} %dynamic-slice_convert_fusion.22), channel_id=1, source_target_pairs={{0,16},{1,17},{2,18},{3,19},{4,20},{5,21},{6,22},{7,23},{8,24},{9,... | collective-permute-start | bytes 442376 | tf_op jit(solution)/shard_map/ppermute | solution.py:177
  1119.7 17.4 %collective-permute-start.91 = (bf16[1,48,1536]{2,1,0:T(8,128)(2,1)S(1)}, bf16[1,48,1536]{2,1,0:T(8,128)(2,1)S(1)}, u32[]{:S(2)}, u32[]{:S(2)}) collective-permute-start(bf16[1,48,1536]{2,1,0:T(8,128)(2,1)S(1)} %dynamic-slice_convert_fusion.20), channel_id=1, source_target_pairs={{0,16},{1,17},{2,18},{3,19},{4,20},{5,21},{6,22},{7,23},{8,24},{9,... | collective-permute-start | bytes 442376 | tf_op jit(solution)/shard_map/ppermute | solution.py:177
  1124.7 14.0 %collective-permute-start.97 = (bf16[1,48,1536]{2,1,0:T(8,128)(2,1)S(1)}, bf16[1,48,1536]{2,1,0:T(8,128)(2,1)S(1)}, u32[]{:S(2)}, u32[]{:S(2)}) collective-permute-start(bf16[1,48,1536]{2,1,0:T(8,128)(2,1)S(1)} %dynamic-slice_convert_fusion.19), channel_id=1, source_target_pairs={{0,16},{1,17},{2,18},{3,19},{4,20},{5,21},{6,22},{7,23},{8,24},{9,... | collective-permute-start | bytes 442376 | tf_op jit(solution)/shard_map/ppermute | solution.py:177
  1128.7 11.7 %collective-permute-start.85 = (bf16[1,48,1536]{2,1,0:T(8,128)(2,1)S(1)}, bf16[1,48,1536]{2,1,0:T(8,128)(2,1)S(1)}, u32[]{:S(2)}, u32[]{:S(2)}) collective-permute-start(bf16[1,48,1536]{2,1,0:T(8,128)(2,1)S(1)} %dynamic-slice_convert_fusion.21), channel_id=1, source_target_pairs={{0,16},{1,17},{2,18},{3,19},{4,20},{5,21},{6,22},{7,23},{8,24},{9,... | collective-permute-start | bytes 442376 | tf_op jit(solution)/shard_map/ppermute | solution.py:177
  (287 other events, 2836.4 us)

commit v2 on v1

v2 whole, which is shorter than its diff:
```python
from functools import partial
import math

import jax
import jax.numpy as jnp
from jax import lax
from jax.experimental import pallas as pl
from jax.experimental.pallas import tpu as pltpu
from jax.sharding import PartitionSpec as P

D = 768
FF = 3072
HALF = 384
UNITS = 1536
WORDS = 20
REGIONS = 36
HEAD_DIM = 64
GROUP = 4
STEP = 8
PIECES = 4

NORM_EPSILON = 1e-06
MASK_FILL = -1e30
LOG2_E = 1.4426950408889634
SCALE = HEAD_DIM ** (-0.5)
F32 = jnp.float32
BF16 = jnp.bfloat16


def dot32(left, right, left_dim, right_dim):
    return lax.dot_general(
        left, right, (((left_dim,), (right_dim,)), ((), ())), preferred_element_type=F32
    )


def group_index(shape, axis, per_item):
    place = lax.broadcasted_iota(jnp.int32, shape, axis)
    span = per_item * GROUP
    item = jnp.zeros(shape, jnp.int32)
    for bound in range(per_item, shape[axis], per_item):
        if bound % span == 0:
            item = jnp.where(place >= bound, 0, item)
        else:
            item = item + (place >= bound).astype(jnp.int32)
    return item


def two_heads(block):
    lane = lax.broadcasted_iota(jnp.int32, block.shape, 1)
    zero = jnp.zeros_like(block)
    return jnp.concatenate(
        (jnp.where(lane < HEAD_DIM, block, zero), jnp.where(lane < HEAD_DIM, zero, block)), axis=0
    )


def join_heads(stacked):
    rows = stacked.shape[0] // 2
    lane = lax.broadcasted_iota(jnp.int32, (rows, stacked.shape[1]), 1)
    return jnp.where(lane < HEAD_DIM, stacked[:rows], stacked[rows:])


def key_mask(key_item, query_rows, query_item_rows):
    query_item = group_index((1, 2 * query_rows), 1, query_item_rows)
    return jnp.where(key_item == query_item, 0.0, MASK_FILL).astype(F32)


def probabilities(query_stack, keys, mask):
    scores = dot32(keys, query_stack, 1, 1) * (SCALE * LOG2_E) + mask
    raised = jnp.exp2(scores - jnp.max(scores, axis=0, keepdims=True))
    return raised * (1.0 / jnp.sum(raised, axis=0, keepdims=True))


def head_pairs(half):
    return [half * 3 * HALF + start for start in range(0, HALF, 2 * HEAD_DIM)]


def attend_forward(q_ref, kv_ref, o_ref, q_at, k_at, q_rows, k_rows, mask, halves):
    for half in halves:
        for pair, column in enumerate(head_pairs(half)):
            query_stack = two_heads(q_ref[pl.ds(q_at, q_rows), column : column + 128])
            keys = kv_ref[pl.ds(k_at, k_rows), column + HALF : column + HALF + 128]
            values = kv_ref[pl.ds(k_at, k_rows), column + 2 * HALF : column + 2 * HALF + 128]
            probs = probabilities(query_stack, keys, mask).astype(BF16)
            mixed = dot32(probs, values, 0, 0)
            target = half * HALF + pair * 128
            o_ref[pl.ds(q_at, q_rows), target : target + 128] = join_heads(mixed).astype(BF16)


def attend_backward(
    q_ref, kv_ref, do_ref, dq_ref, dkv_ref, q_at, k_at, q_rows, k_rows, mask, halves
):
    for half in halves:
        for pair, column in enumerate(head_pairs(half)):
            query_stack = two_heads(q_ref[pl.ds(q_at, q_rows), column : column + 128])
            keys = kv_ref[pl.ds(k_at, k_rows), column + HALF : column + HALF + 128]
            values = kv_ref[pl.ds(k_at, k_rows), column + 2 * HALF : column + 2 * HALF + 128]
            target = half * HALF + pair * 128
            grad_stack = two_heads(do_ref[pl.ds(q_at, q_rows), target : target + 128])
            probs = probabilities(query_stack, keys, mask)
            grad_probs = dot32(values, grad_stack, 1, 1)
            centre = jnp.sum(grad_probs * probs, axis=0, keepdims=True)
            grad_scores = (probs * (grad_probs - centre)).astype(BF16)
            dq = join_heads(dot32(grad_scores, keys, 0, 0)) * SCALE
            dk = dot32(grad_scores, query_stack, 1, 0) * SCALE
            dv = dot32(probs.astype(BF16), grad_stack, 1, 0)
            dq_ref[pl.ds(q_at, q_rows), column : column + 128] = dq.astype(BF16)
            dkv_ref[pl.ds(k_at, k_rows), column + HALF : column + HALF + 128] = dk.astype(BF16)
            dkv_ref[pl.ds(k_at, k_rows), column + 2 * HALF : column + 2 * HALF + 128] = dv.astype(
                BF16
            )


def attend_streams(cross, key_ref, body):
    rows = (GROUP * WORDS, GROUP * REGIONS)
    per_item = (WORDS, REGIONS)

    def group(index, carry):
        at = [pl.multiple_of(index * count, 16) for count in rows]
        items = (
            group_index((rows[0], 1), 0, WORDS),
            key_ref[pl.ds(at[1], rows[1]), :],
        )
        for query in range(2):
            key = 1 - query if cross else query
            mask = key_mask(items[key], rows[query], per_item[query])
            body(query, key, at[query], at[key], rows[query], rows[key], mask)
        return carry

    lax.fori_loop(0, STEP // GROUP, group, 0)


def norm_forward(summed, gain, shift):
    centred = summed - jnp.mean(summed, axis=-1, keepdims=True)
    spread = jnp.mean(centred * centred, axis=-1, keepdims=True)
    inv_scale = lax.rsqrt(spread + NORM_EPSILON)
    normed = centred * inv_scale
    return normed * gain + shift, normed, inv_scale


def norm_backward(grad_out, normed, inv_scale, gain):
    grad_normed = grad_out * gain
    mean_first = jnp.mean(grad_normed, axis=-1, keepdims=True)
    mean_second = jnp.mean(grad_normed * normed, axis=-1, keepdims=True)
    total = inv_scale * (grad_normed - mean_first - normed * mean_second)
    sums = [jnp.sum(part, axis=0, keepdims=True) for part in (total, grad_out, grad_out * normed)]
    return total, sums


def add_rows(ref, first, rows):
    for row, value in enumerate(rows):
        ref[first + row : first + row + 1, :] += value


def clear_first(*refs):
    @pl.when(pl.program_id(0) == 0)
    def _():
        for ref in refs:
            ref[...] = jnp.zeros(ref.shape, ref.dtype)


def place_other(piece, parts, base, w_in, w_out, in_at, out_at):
    size_in, size_out = D // PIECES, HALF // PIECES
    for step, part in enumerate(parts):
        at = piece ^ step
        rows_in = pl.ds(pl.multiple_of(at * size_in, 16), size_in)
        rows_out = pl.ds(pl.multiple_of(out_at + at * size_out, 16), size_out)
        for kind in range(3):
            column = in_at + kind * HALF
            first = base + kind * size_in
            w_in[rows_in, column : column + HALF] = part[first : first + size_in, :]
        for side in range(2):
            first = base + 3 * size_in + side * size_out
            w_out[rows_out, side * HALF : (side + 1) * HALF] = part[first : first + size_out, :]


def place_own(own_in, own_out, w_in, w_out):
    for kind in range(3):
        w_in[:, kind * HALF : (kind + 1) * HALF] = own_in[0, kind]
    if own_out is not None:
        w_out[0:HALF, :] = own_out[0]


def first_half_kernel(scal, key_ref, xl, xv, own_in, bias, qkvl, qkvv, ol, ov, w_in):
    @pl.when(pl.program_id(0) == 0)
    def _():
        place_own(own_in, None, w_in, None)

    for x, qkv in ((xl, qkvl), (xv, qkvv)):
        qkv[...] = (dot32(x[...], w_in[...], 1, 0) + bias[:, : 3 * HALF]).astype(BF16)
    qkvs, outs = (qkvl, qkvv), (ol, ov)

    def body(query, key, *rest):
        attend_forward(qkvs[query], qkvs[key], outs[query], *rest, (0,))

    attend_streams(True, key_ref, body)


def block_forward_kernel(cross, *refs):
    refs = list(refs)
    take = lambda count: [refs.pop(0) for _ in range(count)]
    sets = 1 if cross else 2
    scal, key_ref = take(2)
    xs = take(2)
    first = take(4) if cross else None
    own = [take(2) for _ in range(sets)]
    parts = take(PIECES)
    biases = take(sets)
    vecs = take(2)
    qkvs, os, ns, invs, lows = (take(2) for _ in range(5))
    weights = [take(2) for _ in range(sets)]

    @pl.when(pl.program_id(0) == 0)
    def _():
        for index in range(sets):
            place_own(*own[index], *weights[index])
            place_other(scal[0], parts, index * D, *weights[index], 3 * HALF, HALF)

    fulls = []
    for stream in range(2):
        w_in = weights[stream % sets][0]
        bias = biases[stream % sets]
        if cross:
            fulls.append(xs[stream][...].astype(F32))
            low = xs[stream][...]
            qkvs[stream][:, : 3 * HALF] = first[2 * stream][...]
            os[stream][:, :HALF] = first[2 * stream + 1][...]
            qkvs[stream][:, 3 * HALF :] = (
                dot32(low, w_in[:, 3 * HALF :], 1, 0) + bias[:, 3 * HALF :]
            ).astype(BF16)
        else:
            vec = vecs[stream]
            low = (xs[stream][...] * vec[3:4, :] + vec[4:5, :]).astype(BF16)
            qkvs[stream][...] = (dot32(low, w_in[...], 1, 0) + bias[...]).astype(BF16)

    def body(query, key, *rest):
        attend_forward(qkvs[query], qkvs[key], os[query], *rest, (1,) if cross else (0, 1))

    attend_streams(cross, key_ref, body)
    for stream in range(2):
        vec = vecs[stream]
        branch = dot32(os[stream][...], weights[stream % sets][1][...], 1, 0)
        full = fulls[stream] if cross else xs[stream][...] * vec[3:4, :] + vec[4:5, :]
        out, normed, inv_scale = norm_forward(full + branch + vec[0:1, :], vec[2:3, :], vec[1:2, :])
        ns[stream][...] = normed
        invs[stream][...] = inv_scale
        lows[stream][...] = out.astype(BF16)


def block_backward_kernel(cross, *refs):
    refs = list(refs)
    take = lambda count: [refs.pop(0) for _ in range(count)]
    sets = 1 if cross else 2
    scal, key_ref = take(2)
    totals, lows, qkvs = take(2), take(2), take(2)
    own = [take(2) for _ in range(sets)]
    parts = take(PIECES)
    if not cross:
        ns, invs, vecs = take(2), take(2), take(2)
    dqkvs, biases, outs = take(2), take(2), take(2)
    if not cross:
        low_outs, sums = take(2), take(1)
    mixes = take(2)
    weights = [take(2) for _ in range(sets)]

    @pl.when(pl.program_id(0) == 0)
    def _():
        for index in range(sets):
            place_own(*own[index], *weights[index])
            place_other(scal[0], parts, index * D, *weights[index], 3 * HALF, HALF)

    clear_first(*biases, *(() if cross else sums))
    for stream in range(2):
        mixes[stream][...] = dot32(
            lows[stream][...], weights[stream % sets][1][...], 1, 1
        ).astype(BF16)

    def body(query, key, *rest):
        attend_backward(
            qkvs[query], qkvs[key], mixes[query], dqkvs[query], dqkvs[key], *rest, (0, 1)
        )

    attend_streams(cross, key_ref, body)
    for stream in range(2):
        grads = dqkvs[stream][...]
        biases[stream][...] += jnp.sum(grads.astype(F32), axis=0, keepdims=True)
        back = totals[stream][...] + dot32(grads, weights[stream % sets][0][...], 1, 1)
        if cross:
            outs[stream][...] = back
        else:
            total, rows = norm_backward(
                back, ns[stream][...], invs[stream][...], vecs[stream][2:3, :]
            )
            outs[stream][...] = total
            low_outs[stream][...] = total.astype(BF16)
            add_rows(sums[0], 0, rows)


CHUNK = 512


def gelu_parts(hidden):
    below = 0.5 + 0.5 * lax.erf(hidden * (0.5**0.5))
    density = jnp.exp2(hidden * hidden * (-0.5 * LOG2_E)) * (1.0 / math.sqrt(2.0 * math.pi))
    return hidden * below, below + hidden * density


def feed_kernel(
    scal,
    n_ref,
    inv_ref,
    low_ref,
    cot_ref,
    ok_ref,
    own_up,
    own_down,
    part0,
    part1,
    part2,
    part3,
    bias,
    vec,
    out_ref,
    act_ref,
    dhid_ref,
    dbr_ref,
    total_ref,
    low_total_ref,
    sums,
    up_sums,
    other_up,
    other_down,
    slope,
):
    @pl.when(pl.program_id(0) == 0)
    def _():
        size = UNITS // PIECES
        for step, part in enumerate((part0, part1, part2, part3)):
            at = pl.multiple_of((scal[0] ^ step) * size, 128)
            other_up[:, pl.ds(at, size)] = part[0:D, :]
            other_down[pl.ds(at, size), 0:HALF] = part[D : D + size, :]
            other_down[pl.ds(at, size), HALF:D] = part[D + size : D + 2 * size, :]

    clear_first(sums, up_sums)

    def up(start):
        if start < UNITS:
            return own_up[0, :, start : start + CHUNK]
        return other_up[:, start - UNITS : start - UNITS + CHUNK]

    def down(start):
        if start < UNITS:
            return own_down[0, start : start + CHUNK, :]
        return other_down[start - UNITS : start - UNITS + CHUNK, :]

    normed = n_ref[...]
    full = normed * vec[0:1, :] + vec[1:2, :]
    low = low_ref[...]
    branch = 0.0
    for start in range(0, FF, CHUNK):
        span = slice(start, start + CHUNK)
        act, slope_part = gelu_parts(dot32(low, up(start), 1, 0) + bias[:, span])
        act = act.astype(BF16)
        act_ref[:, span] = act
        slope[:, span] = slope_part
        branch = branch + dot32(act, down(start), 1, 0)
    out, out_normed, out_scale = norm_forward(full + branch + vec[2:3, :], vec[4:5, :], vec[3:4, :])
    out_ref[...] = out
    cot = cot_ref[...].astype(F32) * ok_ref[...]
    total, rows = norm_backward(cot, out_normed, out_scale, vec[4:5, :])
    add_rows(sums, 0, rows)
    low_grad = total.astype(BF16)
    dbr_ref[...] = low_grad
    back = total
    for start in range(0, FF, CHUNK):
        span = slice(start, start + CHUNK)
        dhidden = (dot32(low_grad, down(start), 1, 1) * slope[:, span]).astype(BF16)
        dhid_ref[:, span] = dhidden
        up_sums[:, span] += jnp.sum(dhidden.astype(F32), axis=0, keepdims=True)
        back = back + dot32(dhidden, up(start), 1, 1)
    total, rows = norm_backward(back, normed, inv_ref[...], vec[0:1, :])
    add_rows(sums, 3, rows)
    total_ref[...] = total
    low_total_ref[...] = total.astype(BF16)


def grads_kernel(plan, counts, scal, *refs):
    operands, (send, keep, total) = refs[:-3], refs[-3:]
    low_rows = send.shape[2]
    at = 0
    for terms, width in plan:
        value = 0.0
        for left, right in terms:
            value = value + dot32(operands[left][...], operands[right][...], 0, 0)
        total[:, 0:width] = value
        for slot in range(send.shape[1]):
            pair = (scal[1] >> 1) ^ slot
            side = scal[1] & 1
            for ref, which in ((keep, side), (send, 1 - side)):
                first = pl.multiple_of((2 * pair + which) * low_rows, 16)
                ref[0, slot, :, at : at + width] = total[pl.ds(first, low_rows), 0:width].astype(
                    BF16
                )
        at += width


def grads_unit(scal, ndp, plan, operands):
    columns = sum(width for _, width in plan)
    low_rows = D // ndp
    if low_rows % 16 or ndp % 2:
        dp = lax.axis_index("dp")
        order = jnp.arange(ndp, dtype=jnp.int32) ^ dp
        halves = []
        for half in range(2):
            parts = []
            for terms, width in plan:
                parts.append(
                    sum(
                        dot32(
                            operands[a], operands[b][:, half * width : (half + 1) * width], 0, 0
                        ).astype(F32)
                        for a, b in terms
                    )
                )
            whole = jnp.concatenate(parts, axis=1).astype(BF16)
            halves.append(whole.reshape(ndp, low_rows, columns)[order])
        slots = jnp.stack(halves).reshape(2, ndp // 2, 2, low_rows, columns)
        return slots[:, :, 1], slots[:, :, 0]
    width_of = {}
    for terms, width in plan:
        for left, right in terms:
            width_of[right] = width
    specs, flops = [], 0
    for index, operand in enumerate(operands):
        if index in width_of:
            specs.append(pl.BlockSpec((operand.shape[0], width_of[index]), lambda m, s: (0, m)))
            flops += 2 * operand.shape[0] * operand.shape[1] * D
        else:
            specs.append(pl.BlockSpec(operand.shape, lambda m, s: (0, 0)))
    shape = (2, ndp // 2, low_rows, columns)
    out = jax.ShapeDtypeStruct(shape, BF16)
    out_spec = pl.BlockSpec((1, *shape[1:]), lambda m, s: (m, 0, 0, 0))
    return pl.pallas_call(
        partial(grads_kernel, plan, None),
        grid_spec=pltpu.PrefetchScalarGridSpec(
            num_scalar_prefetch=1,
            grid=(2,),
            in_specs=specs,
            out_specs=[out_spec, out_spec],
            scratch_shapes=[pltpu.VMEM((D, max(width for _, width in plan)), F32)],
        ),
        out_shape=[out, out],
        cost_estimate=pl.CostEstimate(
            flops=flops, bytes_accessed=20_000_000, transcendentals=0
        ),
        name="grads",
    )(scal, *operands)


def row_spec(rows, width):
    return pl.BlockSpec((rows, width), lambda i, s: (i, 0))


def full_spec(shape, lead=None):
    if lead is None:
        return pl.BlockSpec(shape, lambda i, s: (0,) * len(shape))
    return pl.BlockSpec((1, *shape[1:]), lambda i, s: (lead,) + (0,) * (len(shape) - 1))


def call(kernel, scal, steps, operands, outs, scratch, flops, name):
    nbytes = sum(a.size * a.dtype.itemsize for a, _ in operands)
    return pl.pallas_call(
        kernel,
        grid_spec=pltpu.PrefetchScalarGridSpec(
            num_scalar_prefetch=1,
            grid=(steps,),
            in_specs=[spec for _, spec in operands],
            out_specs=[spec for *_, spec in outs],
            scratch_shapes=scratch,
        ),
        out_shape=[jax.ShapeDtypeStruct(shape, dtype) for shape, dtype, _ in outs],
        cost_estimate=pl.CostEstimate(
            flops=int(flops), bytes_accessed=2 * nbytes, transcendentals=0
        ),
        name=name,
    )(scal, *[array for array, _ in operands])


class Links:
    def __init__(self):
        self.ndp = lax.axis_size("dp")
        self.bits = self.ndp.bit_length() - 1
        self.dp = lax.axis_index("dp")
        self.mp = lax.axis_index("mp")
        self.piece = self.dp % PIECES

    def across(self, value):
        pairs = [(2 * d + m, 2 * d + 1 - m) for d in range(self.ndp) for m in range(2)]
        return lax.ppermute(value, ("dp", "mp"), pairs)

    def flip(self, value, bit):
        pairs = [
            (2 * d + m, 2 * (d ^ (1 << bit)) + m) for d in range(self.ndp) for m in range(2)
        ]
        return lax.ppermute(value, ("dp", "mp"), pairs)

    def exchange(self, value, axis):
        return self.across(value) if axis == "m" else self.flip(value, axis)

    def other_pieces(self, own_piece):
        first = self.across(own_piece)
        third = self.flip(first, 1)
        second = self.flip(first, 0)
        fourth = self.flip(third, 0)
        return [first, second, third, fourth]

    def own_piece(self, value, axis):
        size = value.shape[axis] // PIECES
        return lax.dynamic_slice_in_dim(value, self.piece * size, size, axis)

    def reduce(self, send, keep, order):
        low, columns = send.shape[2:]
        axes = ["m"] + list(range(self.bits - 1, 0, -1))
        shape = (2,) * len(axes) + (low, columns)
        got = self.flip(send, 0).reshape(shape)
        total = keep.reshape(shape).astype(F32) + got.astype(F32)
        for axis in order:
            place = axes.index(axis)
            axes.pop(place)
            going = lax.index_in_dim(total, 1, place, keepdims=False).astype(BF16)
            staying = lax.index_in_dim(total, 0, place, keepdims=False)
            total = staying + self.exchange(going, axis).astype(F32)
        return total

    def total(self, value):
        value = value + self.across(value)
        for bit in range(self.bits):
            value = value + self.flip(value, bit)
        return value


def per_device(
    lang,
    vision,
    region_count,
    att_in,
    att_in_bias,
    att_out,
    att_row_bias,
    att_gain,
    ffn_up,
    ffn_up_bias,
    ffn_down,
    ffn_row_bias,
    ffn_gain,
    cot_lang,
    cot_vision,
):
    links = Links()
    items = region_count.shape[0] // 2
    steps = items // STEP
    rows = (STEP * WORDS, STEP * REGIONS)
    all_rows = (items * WORDS, items * REGIONS)
    row_total = sum(all_rows)
    scal = jnp.stack((links.piece, links.dp)).astype(jnp.int32)
    counts = lax.dynamic_slice_in_dim(region_count, links.mp * items, items)
    slot = jnp.arange(REGIONS, dtype=jnp.int32)
    region_ok = slot[None, :] < counts[:, None]
    item_index = (jnp.arange(items, dtype=jnp.int32) % GROUP)[:, None]
    region_key = jnp.where(region_ok, item_index, -1).reshape(-1, 1)
    row_ok = (region_ok.reshape(-1, 1).astype(F32), jnp.ones((all_rows[0], 1), F32))
    row_ok = (row_ok[1], row_ok[0])

    def att_piece(block):
        piece_in = links.own_piece(att_in[block], 1).reshape(-1, HALF)
        piece_out = links.own_piece(att_out[block], 0)
        return [piece_in, piece_out[:, :HALF], piece_out[:, HALF:]]

    def ffn_piece(stream):
        piece_up = links.own_piece(ffn_up[stream], 1)
        piece_down = links.own_piece(ffn_down[stream], 0)
        return [piece_up, piece_down[:, :HALF], piece_down[:, HALF:]]

    small_own = jnp.concatenate((att_in_bias.reshape(-1), ffn_up_bias.reshape(-1)))
    cross_parts = links.other_pieces(jnp.concatenate(att_piece(0)))
    small_other = links.across(small_own)
    self_parts = links.other_pieces(jnp.concatenate(att_piece(1) + att_piece(2)))
    ffn_parts = [None, None]
    for stream in (1, 0):
        ffn_parts[stream] = links.other_pieces(jnp.concatenate(ffn_piece(stream)))
    bias_other = small_other[: 6 * HALF].reshape(3, 2, HALF)
    up_bias_other = small_other[6 * HALF :].reshape(2, UNITS)

    def bias_row(block):
        none = jnp.zeros((HALF,), BF16)
        own, other = att_in_bias[block], bias_other[block]
        return jnp.concatenate((own[0], none, own[1], other[0], none, other[1]))[None].astype(F32)

    own_row = jnp.concatenate((att_in_bias[0, 0], jnp.zeros((HALF,), BF16), att_in_bias[0, 1]))
    own_row = own_row[None].astype(F32)
    row_bias = att_row_bias.astype(F32)
    gain = att_gain.astype(F32)
    ffn_bias = ffn_row_bias.astype(F32)
    feed_gain = ffn_gain.astype(F32)
    none = jnp.zeros((D,), F32)

    def vectors(*rows8):
        return jnp.stack(list(rows8) + [none] * (8 - len(rows8)))

    key_operand = (region_key, row_spec(rows[1], 1))

    def own_weights(block):
        return [(att_in, full_spec(att_in.shape, block)), (att_out, full_spec(att_out.shape, block))]

    def streams(arrays):
        return [(a, row_spec(rows[s], a.shape[1])) for s, a in enumerate(arrays)]

    def stream_outs(width, dtype):
        return [((all_rows[s], width), dtype, row_spec(rows[s], width)) for s in range(2)]

    def whole(arrays):
        return [(a, full_spec(a.shape)) for a in arrays]

    def weight_scratch(sets):
        return [pltpu.VMEM((D, 6 * HALF), BF16), pltpu.VMEM((D, D), BF16)] * sets

    first = call(
        first_half_kernel,
        scal,
        steps,
        [key_operand] + streams((lang, vision)) + own_weights(0)[:1] + whole([own_row]),
        stream_outs(3 * HALF, BF16) + stream_outs(HALF, BF16),
        [pltpu.VMEM((D, 3 * HALF), BF16)],
        2 * row_total * D * 3 * HALF * 3,
        "cross_first",
    )
    first = (first[0], first[2], first[1], first[3])
    cross_vec = vectors(row_bias[0, 0], row_bias[0, 1], gain[0])
    forward_outs = (
        stream_outs(6 * HALF, BF16)
        + stream_outs(D, BF16)
        + stream_outs(D, F32)
        + stream_outs(1, F32)
        + stream_outs(D, BF16)
    )
    cross_out = call(
        partial(block_forward_kernel, True),
        scal,
        steps,
        [key_operand]
        + streams((lang, vision))
        + [(a, row_spec(rows[i // 2], a.shape[1])) for i, a in enumerate(first)]
        + own_weights(0)
        + whole(cross_parts)
        + whole([bias_row(0), cross_vec, cross_vec]),
        forward_outs,
        weight_scratch(1),
        2 * row_total * D * 5 * HALF * 3,
        "cross_forward",
    )
    qkv_a, o_a, n_a, inv_a, low_a = (cross_out[2 * i : 2 * i + 2] for i in range(5))
    self_vecs = [
        vectors(row_bias[b, 0], row_bias[b, 1], gain[b], gain[0], row_bias[0, 1]) for b in (1, 2)
    ]
    self_out = call(
        partial(block_forward_kernel, False),
        scal,
        steps,
        [key_operand]
        + streams(n_a)
        + own_weights(1)
        + own_weights(2)
        + whole(self_parts)
        + whole([bias_row(1), bias_row(2)] + self_vecs),
        forward_outs,
        weight_scratch(2),
        2 * row_total * D * 8 * HALF * 3,
        "self_forward",
    )
    qkv_b, o_b, n_b, inv_b, low_b = (self_out[2 * i : 2 * i + 2] for i in range(5))

    cots = (cot_lang, cot_vision)
    fed = [None, None]
    reduced_ffn = [None, None]
    for stream in (1, 0):
        bias = jnp.concatenate((ffn_up_bias[stream], up_bias_other[stream]))[None].astype(F32)
        vec = vectors(
            gain[1 + stream],
            row_bias[1 + stream, 1],
            ffn_bias[stream, 0],
            ffn_bias[stream, 1],
            feed_gain[stream],
        )
        tall = rows[stream]

        def spec(width, tall=tall):
            return row_spec(tall, width)

        count = all_rows[stream]
        fed[stream] = call(
            feed_kernel,
            scal,
            steps,
            [
                (n_b[stream], spec(D)),
                (inv_b[stream], spec(1)),
                (low_b[stream], spec(D)),
                (cots[stream], spec(D)),
                (row_ok[stream], spec(1)),
                (ffn_up, full_spec(ffn_up.shape, stream)),
                (ffn_down, full_spec(ffn_down.shape, stream)),
            ]
            + whole(ffn_parts[stream])
            + whole([bias, vec]),
            [
                ((count, D), F32, spec(D)),
                ((count, FF), BF16, spec(FF)),
                ((count, FF), BF16, spec(FF)),
                ((count, D), BF16, spec(D)),
                ((count, D), F32, spec(D)),
                ((count, D), BF16, spec(D)),
                ((8, D), F32, full_spec((8, D))),
                ((1, FF), F32, full_spec((1, FF))),
            ],
            [
                pltpu.VMEM((D, UNITS), BF16),
                pltpu.VMEM((UNITS, D), BF16),
                pltpu.VMEM((tall, FF), F32),
            ],
            2 * count * D * FF * 8,
            "feed",
        )
        act, dhid, dbr = fed[stream][1:4]
        send, keep = grads_unit(
            scal,
            links.ndp,
            [([(0, 1)], UNITS), ([(2, 3)], UNITS)],
            [low_b[stream], dhid, dbr, act],
        )
        rest = list(range(2, links.bits))
        order = ["m", 1] + rest if stream else [1, "m"] + rest
        reduced_ffn[stream] = links.reduce(send, keep, order)

    total_b = [fed[s][4] for s in range(2)]
    low_total_b = [fed[s][5] for s in range(2)]
    flops = 2 * row_total * D * 8 * HALF * 4
    grad_vec = vectors(none, none, gain[0])
    back = call(
        partial(block_backward_kernel, False),
        scal,
        steps,
        [key_operand]
        + streams(total_b)
        + streams(low_total_b)
        + streams(qkv_b)
        + own_weights(1)
        + own_weights(2)
        + whole(self_parts)
        + streams(n_a)
        + streams(inv_a)
        + whole([grad_vec, grad_vec]),
        stream_outs(6 * HALF, BF16)
        + [((1, 6 * HALF), F32, full_spec((1, 6 * HALF)))] * 2
        + stream_outs(D, F32)
        + stream_outs(D, BF16)
        + [((8, D), F32, full_spec((8, D)))],
        [pltpu.VMEM((rows[0], D), BF16), pltpu.VMEM((rows[1], D), BF16)] + weight_scratch(2),
        flops,
        "self_backward",
    )
    dqkv_b, in_sums_b, total_a, low_total_a, sums_a = (
        back[0:2],
        back[2:4],
        back[4:6],
        back[6:8],
        back[8],
    )
    send, keep = grads_unit(
        scal,
        links.ndp,
        [
            ([(0, 1)], 3 * HALF),
            ([(2, 3)], HALF),
            ([(4, 5)], 3 * HALF),
            ([(6, 7)], HALF),
        ],
        [
            low_a[0],
            dqkv_b[0],
            low_total_b[0],
            o_b[0],
            low_a[1],
            dqkv_b[1],
            low_total_b[1],
            o_b[1],
        ],
    )
    reduced_self = links.reduce(
        send, keep, [2, "m", 1] + list(range(3, links.bits)) if links.bits > 2 else ["m", 1]
    )

    back = call(
        partial(block_backward_kernel, True),
        scal,
        steps,
        [key_operand]
        + streams(total_a)
        + streams(low_total_a)
        + streams(qkv_a)
        + own_weights(0)
        + whole(cross_parts),
        stream_outs(6 * HALF, BF16)
        + [((1, 6 * HALF), F32, full_spec((1, 6 * HALF)))] * 2
        + stream_outs(D, F32),
        [pltpu.VMEM((rows[0], D), BF16), pltpu.VMEM((rows[1], D), BF16)] + weight_scratch(1),
        flops,
        "cross_backward",
    )
    dqkv_a, in_sums_a, grad_rows = back[0:2], back[2:4], back[4:6]
    send, keep = grads_unit(
        scal,
        links.ndp,
        [([(0, 1), (4, 5)], 3 * HALF), ([(2, 3), (6, 7)], HALF)],
        [
            lang,
            dqkv_a[0],
            low_total_a[0],
            o_a[0],
            vision,
            dqkv_a[1],
            low_total_a[1],
            o_a[1],
        ],
    )
    reduced_cross = links.reduce(send, keep, ["m"] + list(range(1, links.bits)))

    ins = [reduced_cross, reduced_self[:, : 4 * HALF], reduced_self[:, 4 * HALF :]]
    low_rows = D // links.ndp
    att_in_grad = jnp.stack(
        [v[:, : 3 * HALF].reshape(low_rows, 3, HALF).transpose(1, 0, 2) for v in ins]
    )
    att_out_grad = jnp.stack([v[:, 3 * HALF :].T for v in ins])
    up_grad = jnp.stack([v[:, :UNITS] for v in reduced_ffn])
    down_grad = jnp.stack([v[:, UNITS:].T for v in reduced_ffn])

    def in_order(value, width):
        lead = value.shape[:-1]
        split = value.reshape(*lead, 2, width)
        swapped = split[..., ::-1, :]
        return jnp.where(links.mp == 0, split, swapped).reshape(value.shape)

    in_sums = jnp.stack([in_sums_a[0] + in_sums_a[1], in_sums_b[0], in_sums_b[1]])
    in_sums = in_sums.reshape(3, 2, 3, HALF)[:, :, ::2].transpose(0, 2, 1, 3).reshape(3, 2, D)
    up_sums = jnp.concatenate([fed[s][7] for s in range(2)])
    parts = (
        in_order(in_sums, HALF),
        in_order(up_sums, UNITS),
        jnp.stack((sums_a[0:2], fed[0][6][3:5], fed[1][6][3:5])),
        jnp.stack((sums_a[2], fed[0][6][5], fed[1][6][5])),
        jnp.stack([fed[s][6][0:2] for s in range(2)]),
        jnp.stack([fed[s][6][2] for s in range(2)]),
    )
    flat = links.total(jnp.concatenate([part.reshape(-1) for part in parts]))
    summed, at = [], 0
    for part in parts:
        summed.append(flat[at : at + part.size].reshape(part.shape))
        at += part.size
    return (
        fed[0][0],
        fed[1][0],
        grad_rows[0],
        grad_rows[1],
        att_in_grad,
        summed[0],
        att_out_grad,
        summed[2],
        summed[3],
        up_grad,
        summed[1],
        down_grad,
        summed[4],
        summed[5],
    )


def solution(mesh):
    rows = P(("dp", "mp"), None)
    return jax.shard_map(
        per_device,
        mesh=mesh,
        in_specs=(
            rows,
            rows,
            P("dp"),
            P(None, None, None, "mp"),
            P(None, None, "mp"),
            P(None, "mp", None),
            P(),
            P(),
            P(None, None, "mp"),
            P(None, "mp"),
            P(None, "mp", None),
            P(),
            P(),
            rows,
            rows,
        ),
        out_specs=(
            rows,
            rows,
            rows,
            rows,
            P(None, None, "dp", "mp"),
            P(),
            P(None, "mp", "dp"),
            P(),
            P(),
            P(None, "dp", "mp"),
            P(),
            P(None, "mp", "dp"),
            P(),
            P(),
        ),
        check_vma=False,
    )
```

time: 1150 us -> 626 us (0.54)
  matrix products: 315 us -> 0 us
  local copies, waits for them, and re-layouts: 284 us -> 54.5 us
  Pallas kernels: 123 us -> 274 us
  other arithmetic: 108 us -> 45.4 us
  starting transfers between devices: 88.9 us -> 34.6 us
    dot_general x120 -> x0, matrix products: 315 us -> none  [dot32(): lax.dot_general(left, right, (((left_dim,), (right_dim,)), ((), ())), pre...]
    pallas_call x8 -> x11, Pallas kernels: 123 us -> 274 us  [the longest x7 214 us: call(): pl.pallas_call(kernel, grid_spec=pltpu.PrefetchScalarGridSpec(num_scalar_...]
    convert_element_type x63 -> x17, local copies, waits for them, and re-layouts: 77.2 us -> 7.03 us  [the longest x16 6.08 us: reduce(): going = lax.index_in_dim(total, 1, place, keepdims=False).astype(BF16)]
    rev x8 -> x1, local copies, waits for them, and re-layouts: 55.4 us -> 0.35 us  [in_order(): swapped = split[..., ::-1, :]]
    ppermute x78 -> x32, starting transfers between devices: 66.8 us -> 21.7 us  [flip(): return lax.ppermute(value, ('dp', 'mp'), pairs)]
    reshape x13 -> x4, local copies, waits for them, and re-layouts: 34.3 us -> 0.31 us  [the longest x3 0.27 us: per_device(): v[:, :3 * HALF].reshape(low_rows, 3, HALF).transpose(1, 0, 2)]
    concatenate x8, local copies, waits for them, and re-layouts: 32.3 us -> 0.69 us  [the longest x1 0.64 us: per_device(): jnp.concatenate(att_piece(1) + att_piece(2))]
    convert_element_type x27 -> x7, other arithmetic: 32.1 us -> 3.79 us  [the longest x3 1.88 us: bias_row(): jnp.concatenate((own[0], none, own[1], other[0], none, other[1]))[None]]
  transfers between devices with their start and end apart: 98 -> 42, of which waited for: 38 -> 18; matrix products, arithmetic and copies ran while one was open for 42% -> 11% of each run, Pallas kernels for 3% -> 22%
where the time goes in v2:
time: 626 us; the launch traced here: 622 us
  Pallas kernels  274 us (44%)
  waiting for transfers between devices  211 us (34%)
  local copies, waits for them, and re-layouts  54.5 us (9%)
  other arithmetic  45.4 us (7%)
  starting transfers between devices  34.6 us (6%)
    pallas_call x7, Pallas kernels, call(): pl.pallas_call(kernel, grid_spec=pltpu.PrefetchScalarGridSpec(num_scalar_...  214 us
    ppermute x32, waiting for transfers between devices, flip(): return lax.ppermute(value, ('dp', 'mp'), pairs)  112 us
    ppermute x10, waiting for transfers between devices, across(): return lax.ppermute(value, ('dp', 'mp'), pairs)  99.8 us
    pallas_call x4, Pallas kernels, grads_unit(): pl.pallas_call(partial(grads_kernel, plan, None), grid_spec=pltpu.Prefetc...  59.4 us
    ppermute x32, starting transfers between devices, flip(): return lax.ppermute(value, ('dp', 'mp'), pairs)  21.7 us
    add x4, other arithmetic, reduce(): total = keep.reshape(shape).astype(F32) + got.astype(F32)  19.6 us
    unnamed x73, local copies, waits for them, and re-layouts  14.2 us
    ppermute x10, starting transfers between devices, across(): return lax.ppermute(value, ('dp', 'mp'), pairs)  12.9 us
  transfers between devices with their start and end apart: 42, of which 18 were waited for; matrix products, arithmetic and copies ran while one was open for 11% of the time, Pallas kernels for 22%

profile of v2, /device:TPU:0, one launch (start us, length us, event | category | flops | bytes accessed | tf_op | source)
XLA Modules:
  0.0 622.0 jit_solution(2941377824110625336)
XLA Ops:
  0.7 2.7 fusion.33
  3.3 4.4 fusion.30
  7.7 1.9 constant_dynamic-slice_fusion
  12.7 1.8 constant_dynamic-update-slice_fusion.6
  15.8 3.0 collective-permute-start.5
  21.3 2.0 collective-permute-start.4
  23.3 4.1 fusion.32
  28.6 2.7 fusion.31
  31.9 2.1 collective-permute-start.13
  36.5 15.8 %cross_first.1 = (bf16[480,1152]{1,0:T(8,128)(2,1)}, bf16[864,1152]{1,0:T(8,128)(2,1)}, bf16[480,384]{1,0:T(8,128)(2,1)}, bf16[864,384]{1,0:T(8,128)(2,1)}) custom-call(s32[2]{0:T(128)} %pad_add_fusion.scal.refs_0_, s32[864,1]{1,0:T(8,128)} %select_n.78.key_ref.refs_1_, bf16[480,768]{1,0:T(8,128)(2,1)} %refs_0_.1, bf16[864,768]{1,0:T(8,128)(2,1)} %refs_4_.3, ...), custom_call_target="tpu_custom_call" | custom-call | flops 7134511104 | bytes 14761728 | tf_op jit(solution)/shard_map/cross_first/pallas_call | solution.py:471
  57.2 1.6 collective-permute-done.4
  60.5 2.0 collective-permute-start.2
  63.2 13.7 %collective-permute-done.2.refs_12_ = bf16[768,384]{1,0:T(8,128)(2,1)S(1)} collective-permute-done((bf16[768,384]{1,0:T(8,128)(2,1)}, bf16[768,384]{1,0:T(8,128)(2,1)S(1)}, u32[]{:S(2)}, u32[]{:S(2)}) %collective-permute-start.2) | collective-permute-done | bytes 589856 | tf_op jit(solution)/shard_map/ppermute | solution.py:504
  79.3 4.8 collective-permute-done.9.part0
  84.1 2.0 collective-permute-start.11
  86.1 22.4 %collective-permute-done.13.part0 = bf16[1536,384]{1,0:T(8,128)(2,1)} collective-permute-done((bf16[1536,384]{1,0:T(8,128)(2,1)S(1)}, bf16[1536,384]{1,0:T(8,128)(2,1)}, u32[]{:S(2)}, u32[]{:S(2)}) %collective-permute-start.13) | collective-permute-done | bytes 1179680 | tf_op jit(solution)/shard_map/ppermute | solution.py:498
  108.5 1.7 collective-permute-start.15
  112.2 20.8 %cross_forward.1 = (bf16[480,2304]{1,0:T(8,128)(2,1)}, bf16[864,2304]{1,0:T(8,128)(2,1)}, bf16[480,768]{1,0:T(8,128)(2,1)}, bf16[864,768]{1,0:T(8,128)(2,1)}, f3...) custom-call(s32[2]{0:T(128)} %pad_add_fusion.scal.refs_0_, ...), custom_call_target="tpu_custom_call" | custom-call | flops 11890851840 | bytes 31384320 | tf_op jit(solution)/shard_map/cross_forward/pallas_call | solution.py:471
  133.6 16.6 %collective-permute-done.15.part2 = bf16[1536,384]{1,0:T(8,128)(2,1)S(1)} collective-permute-done((bf16[1536,384]{1,0:T(8,128)(2,1)}, bf16[1536,384]{1,0:T(8,128)(2,1)S(1)}, u32[]{:S(2)}, u32[]{:S(2)}) %collective-permute-start.15) | collective-permute-done | bytes 1179680 | tf_op jit(solution)/shard_map/ppermute | solution.py:504
  151.3 30.2 %self_forward.1 = (bf16[480,2304]{1,0:T(8,128)(2,1)}, bf16[864,2304]{1,0:T(8,128)(2,1)}, bf16[480,768]{1,0:T(8,128)(2,1)}, bf16[864,768]{1,0:T(8,128)(2,1)}, f32...) custom-call(s32[2]{0:T(128)} %pad_add_fusion.scal.refs_0_, ...), custom_call_target="tpu_custom_call" | custom-call | flops 19025362944 | bytes 46148352 | tf_op jit(solution)/shard_map/self_forward/pallas_call | solution.py:471
  182.2 26.3 %feed.2 = (f32[480,768]{1,0:T(8,128)}, bf16[480,3072]{1,0:T(8,128)(2,1)}, bf16[480,3072]{1,0:T(8,128)(2,1)}, bf16[480,768]{1,0:T(8,128)(2,1)}, f32[480,768]{1,0:...) custom-call(s32[2]{0:T(128)} %pad_add_fusion.scal.refs_0_, ...), custom_call_target="tpu_custom_call" | custom-call | flops 18119393280 | bytes 34291200 | tf_op jit(solution)/shard_map/feed/pallas_call | solution.py:471
  208.6 32.2 %feed.3 = (f32[864,768]{1,0:T(8,128)}, bf16[864,3072]{1,0:T(8,128)(2,1)}, bf16[864,3072]{1,0:T(8,128)(2,1)}, bf16[864,768]{1,0:T(8,128)(2,1)}, f32[864,768]{1,0:...) custom-call(s32[2]{0:T(128)} %pad_add_fusion.scal.refs_0_, ...), custom_call_target="tpu_custom_call" | custom-call | flops 32614907904 | bytes 39015936 | tf_op jit(solution)/shard_map/feed/pallas_call | solution.py:471
  240.8 47.9 %self_backward.1 = (bf16[480,2304]{1,0:T(8,128)(2,1)}, bf16[864,2304]{1,0:T(8,128)(2,1)}, f32[1,2304]{1,0:T(1,128)}, f32[1,2304]{1,0:T(1,128)}, f32[480,768]{1,0...) custom-call(s32[2]{0:T(128)} %pad_add_fusion.scal.refs_0_, ...), custom_call_target="tpu_custom_call" | custom-call | flops 25367150592 | bytes 70894848 | tf_op jit(solution)/shard_map/self_backward/pallas_call | solution.py:471
  288.8 41.0 %cross_backward.1 = (bf16[480,2304]{1,0:T(8,128)(2,1)}, bf16[864,2304]{1,0:T(8,128)(2,1)}, f32[1,2304]{1,0:T(1,128)}, f32[1,2304]{1,0:T(1,128)}, f32[480,768]{1,0:T(8,128)}, /*index=5*/f32[864,768]{1,0:T(8,128)}) custom-call(s32[2]{0:T(128)} %pad_add_fusion.scal.refs_0_, s32[864,1]{1,0:T(8,128)} %select_n.78.key_ref.refs_1_, ...), custom_call_target="tpu_custom_call" | custom-call | flops 25367150592 | bytes 43653888 | tf_op jit(solution)/shard_map/cross_backward/pallas_call | solution.py:471
  329.8 14.8 %grads.4 = (bf16[2,8,48,1536]{3,2,1,0:T(8,128)(2,1)}, bf16[2,8,48,1536]{3,2,1,0:T(8,128)(2,1)}) custom-call(s32[2]{0:T(128)} %pad_add_fusion.scal.refs_0_, bf16[480,768]{1,0:T(8,128)(2,1)} %refs_0_.1, bf16[480,2304]{1,0:T(8,128)(2,1)} %get-tuple-element.107.refs_1_, bf16[480,768]{1,0:T(8,128)(2,1)} %get-tuple-element.101.refs_4_.refs_2_, ...), custom_call_target="tpu_custom_call" | custom-call | flops 6341787648 | bytes 20000000 | tf_op jit(solution)/shard_map/grads/pallas_call | solution.py:442
  348.8 1.3 constant_dynamic-update-slice_fusion.20
  350.8 2.4 convert_add_fusion.3
  353.4 1.9 copy-done.1
  355.4 1.5 collective-permute-start.18
  357.7 27.5 %collective-permute-done.27 = f32[22272]{0:T(1024)S(1)} collective-permute-done((f32[22272]{0:T(1024)S(1)}, f32[22272]{0:T(1024)S(1)}, u32[]{:S(2)}, u32[]{:S(2)}) %collective-permute-start.27) | collective-permute-done | bytes 89120 | tf_op jit(solution)/shard_map/ppermute | solution.py:498
  385.3 1.3 collective-permute-done.28
  386.6 1.5 collective-permute-start.29
  388.1 11.2 %grads.6 = (bf16[2,8,48,3072]{3,2,1,0:T(8,128)(2,1)}, bf16[2,8,48,3072]{3,2,1,0:T(8,128)(2,1)}) custom-call(s32[2]{0:T(128)} %pad_add_fusion.scal.refs_0_, bf16[480,768]{1,0:T(8,128)(2,1)} %get-tuple-element.85.low_ref.refs_0_, bf16[480,3072]{1,0:T(8,128)(2,1)} %get-tuple-element.130.refs_1_, bf16[480,768]{1,0:T(8,128)(2,1)} %get-tuple-element.131.refs_2_, ...), custom_call_target="tpu_custom_call" | custom-call | flops 4529848320 | bytes 20000000 | tf_op jit(solution)/shard_map/grads/pallas_call | solution.py:442
  399.9 1.6 collective-permute-start.30
  402.7 16.9 %grads.7 = (bf16[2,8,48,3072]{3,2,1,0:T(8,128)(2,1)}, bf16[2,8,48,3072]{3,2,1,0:T(8,128)(2,1)}) custom-call(s32[2]{0:T(128)} %pad_add_fusion.scal.refs_0_, bf16[864,768]{1,0:T(8,128)(2,1)} %get-tuple-element.89.low_ref.refs_0_, bf16[864,3072]{1,0:T(8,128)(2,1)} %get-tuple-element.135.refs_1_, bf16[864,768]{1,0:T(8,128)(2,1)} %get-tuple-element.136.refs_2_, ...), custom_call_target="tpu_custom_call" | custom-call | flops 8153726976 | bytes 20000000 | tf_op jit(solution)/shard_map/grads/pallas_call | solution.py:442
  419.8 1.6 add.140
  421.3 2.5 collective-permute-start.31
  423.9 1.2 fusion.13
  425.1 1.6 collective-permute-start.20
  426.8 16.5 %grads.5 = (bf16[2,8,48,3072]{3,2,1,0:T(8,128)(2,1)}, bf16[2,8,48,3072]{3,2,1,0:T(8,128)(2,1)}) custom-call(s32[2]{0:T(128)} %pad_add_fusion.scal.refs_0_, bf16[480,768]{1,0:T(8,128)(2,1)} %get-tuple-element.113.refs_0_, bf16[480,2304]{1,0:T(8,128)(2,1)} %get-tuple-element.114.refs_1_, bf16[480,768]{1,0:T(8,128)(2,1)} %get-tuple-element.93.refs_4_.refs_2_, ...), custom_call_target="tpu_custom_call" | custom-call | flops 6341787648 | bytes 20000000 | tf_op jit(solution)/shard_map/grads/pallas_call | solution.py:442
  448.6 6.2 collective-permute-done.21
  454.9 5.7 convert_add_fusion.1
  460.6 1.8 fusion.3
  462.5 1.5 collective-permute-start.33
  464.0 5.7 convert_add_fusion
  470.1 3.4 copy-done
  473.4 1.6 copy.53
  475.0 1.5 collective-permute-start.38
  476.5 5.7 convert_add_fusion.2
  482.2 1.8 fusion.2
  484.0 32.0 %collective-permute-done.33 = bf16[2,2,2,48,3072]{4,3,1,2,0:T(8,128)(2,1)} collective-permute-done((bf16[2,2,2,48,3072]{4,3,1,2,0:T(8,128)(2,1)}, bf16[2,2,2,48,3072]{4,3,1,2,0:T(8,128)(2,1)}, u32[]{:S(2)}, u32[]{:S(2)}) %collective-permute-start.33) | collective-permute-done | bytes 2359328 | tf_op jit(solution)/shard_map/ppermute | solution.py:504
  516.0 2.8 fusion
  519.0 1.6 collective-permute-start.34
  520.5 8.9 %collective-permute-done.38 = bf16[2,2,2,48,3072]{4,3,0,1,2:T(8,128)(2,1)} collective-permute-done((bf16[2,2,2,48,3072]{4,3,0,1,2:T(8,128)(2,1)}, bf16[2,2,2,48,3072]{4,3,0,1,2:T(8,128)(2,1)}, u32[]{:S(2)}, u32[]{:S(2)}) %collective-permute-start.38) | collective-permute-done | bytes 2359328 | tf_op jit(solution)/shard_map/ppermute | solution.py:498
  529.4 2.6 copy_add_fusion
  532.8 4.2 collective-permute-done.23
  537.0 2.6 fusion.1
  540.3 14.2 %collective-permute-done.34 = bf16[2,2,48,3072]{3,2,0,1:T(8,128)(2,1)S(1)} collective-permute-done((bf16[2,2,48,3072]{3,2,0,1:T(8,128)(2,1)S(1)}, bf16[2,2,48,3072]{3,2,0,1:T(8,128)(2,1)S(1)}, u32[]{:S(2)}, u32[]{:S(2)}) %collective-permute-start.34) | collective-permute-done | bytes 1179680 | tf_op jit(solution)/shard_map/ppermute | solution.py:498
  555.1 2.8 collective-permute-done.39
  558.4 20.3 %collective-permute-done.24 = bf16[2,2,48,3072]{3,2,0,1:T(8,128)(2,1)S(1)} collective-permute-done((bf16[2,2,48,3072]{3,2,0,1:T(8,128)(2,1)S(1)}, bf16[2,2,48,3072]{3,2,0,1:T(8,128)(2,1)S(1)}, u32[]{:S(2)}, u32[]{:S(2)}) %collective-permute-start.24) | collective-permute-done | bytes 1179680 | tf_op jit(solution)/shard_map/ppermute | solution.py:498
  580.9 2.2 collective-permute-start.41
  583.1 10.2 %collective-permute-done.25 = bf16[2,48,3072]{2,1,0:T(8,128)(2,1)S(1)} collective-permute-done((bf16[2,48,3072]{2,1,0:T(8,128)(2,1)S(1)}, bf16[2,48,3072]{2,1,0:T(8,128)(2,1)S(1)}, u32[]{:S(2)}, u32[]{:S(2)}) %collective-permute-start.25) | collective-permute-done | bytes 589856 | tf_op jit(solution)/shard_map/ppermute | solution.py:504
  593.6 11.4 %collective-permute-done.36 = bf16[48,3072]{1,0:T(8,128)(2,1)S(1)} collective-permute-done((bf16[48,3072]{1,0:T(8,128)(2,1)S(1)}, bf16[48,3072]{1,0:T(8,128)(2,1)S(1)}, u32[]{:S(2)}, u32[]{:S(2)}) %collective-permute-start.36) | collective-permute-done | bytes 294944 | tf_op jit(solution)/shard_map/ppermute | solution.py:504
  605.1 12.4 %collective-permute-done.26 = bf16[48,3072]{1,0:T(8,128)(2,1)S(1)} collective-permute-done((bf16[48,3072]{1,0:T(8,128)(2,1)S(1)}, bf16[48,3072]{1,0:T(8,128)(2,1)S(1)}, u32[]{:S(2)}, u32[]{:S(2)}) %collective-permute-start.26) | collective-permute-done | bytes 294944 | tf_op jit(solution)/shard_map/ppermute | solution.py:504
  (266 shorter events, 47.4 us)
Async XLA Ops:
  10.4 10.3 %copy-start.5 = (bf16[3,2,384]{2,1,0:T(2,128)(2,1)S(1)}, bf16[3,2,384]{2,1,0:T(2,128)(2,1)}, u32[]{:S(2)}) copy-start(bf16[3,2,384]{2,1,0:T(2,128)(2,1)} %param.19) | copy-start | bytes 13828
  10.4 10.3 %copy-start.6 = (bf16[2,1536]{1,0:T(2,128)(2,1)S(1)}, bf16[2,1536]{1,0:T(2,128)(2,1)}, u32[]{:S(2)}) copy-start(bf16[2,1536]{1,0:T(2,128)(2,1)} %param.24) | copy-start | bytes 18436
  15.8 46.7 %collective-permute-start.5 = (bf16[1536,384]{1,0:T(8,128)(2,1)}, bf16[1536,384]{1,0:T(8,128)(2,1)}, u32[]{:S(2)}, u32[]{:S(2)}) collective-permute-start(bf16[1536,384]{1,0:T(8,128)(2,1)} %slice_dynamic-update-slice_fusion), channel_id=1, source_target_pairs={{0,1},{1,0},{2,3},{3,2},{4,5},{5,4},{6,7},{7,6},{8,9},{9,8},{10,11... | collective-permute-start | bytes 3538952 | tf_op jit(solution)/shard_map/ppermute | solution.py:498
  20.7 39.8 %collective-permute-start = (bf16[768,384]{1,0:T(8,128)(2,1)}, bf16[768,384]{1,0:T(8,128)(2,1)}, u32[]{:S(2)}, u32[]{:S(2)}) collective-permute-start(bf16[768,384]{1,0:T(8,128)(2,1)} %pad_maximum_fusion.3), channel_id=1, source_target_pairs={{0,1},{1,0},{2,3},{3,2},{4,5},{5,4},{6,7},{7,6},{8,9},{9,8},{10,11... | collective-permute-start | bytes 1769480 | tf_op jit(solution)/shard_map/ppermute | solution.py:498
  21.3 37.5 %collective-permute-start.4 = (bf16[5376]{0:T(1024)(128)(2,1)}, bf16[5376]{0:T(1024)(128)(2,1)}, u32[]{:S(2)}, u32[]{:S(2)}) collective-permute-start(bf16[5376]{0:T(1024)(128)(2,1)} %pad_maximum_fusion.11), channel_id=1, source_target_pairs={{0,1},{1,0},{2,3},{3,2},{4,5},{5,4},{6,7},{7,6},{8,9},{9,8},{10,11... | collective-permute-start | bytes 32264 | tf_op jit(solution)/shard_map/ppermute | solution.py:498
  31.5 52.6 %collective-permute-start.9 = (bf16[1536,384]{1,0:T(8,128)(2,1)S(1)}, bf16[1536,384]{1,0:T(8,128)(2,1)}, u32[]{:S(2)}, u32[]{:S(2)}) collective-permute-start(bf16[1536,384]{1,0:T(8,128)(2,1)S(1)} %pad_maximum_fusion), channel_id=1, source_target_pairs={{0,1},{1,0},{2,3},{3,2},{4,5},{5,4},{6,7},{7,6},{8,9},{9,8},{10,11... | collective-permute-start | bytes 3538952 | tf_op jit(solution)/shard_map/ppermute | solution.py:498
  31.6 4.2 copy-start.10
  31.7 4.2 copy-start.13
  31.9 76.6 %collective-permute-start.13 = (bf16[1536,384]{1,0:T(8,128)(2,1)S(1)}, bf16[1536,384]{1,0:T(8,128)(2,1)}, u32[]{:S(2)}, u32[]{:S(2)}) collective-permute-start(bf16[1536,384]{1,0:T(8,128)(2,1)S(1)} %pad_maximum_fusion.1), channel_id=1, source_target_pairs={{0,1},{1,0},{2,3},{3,2},{4,5},{5,4},{6,7},{7,6},{8,9},{9,8},{10,11... | collective-permute-start | bytes 3538952 | tf_op jit(solution)/shard_map/ppermute | solution.py:498
  36.5 15.8 %copy-start.14 = (bf16[3,2,768]{2,1,0:T(2,128)(2,1)S(1)}, bf16[3,2,768]{2,1,0:T(2,128)(2,1)}, u32[]{:S(2)}) copy-start(bf16[3,2,768]{2,1,0:T(2,128)(2,1)} %param.21) | copy-start | bytes 27652
  36.5 15.9 %copy-start.19 = (bf16[2,2,768]{2,1,0:T(2,128)(2,1)S(1)}, bf16[2,2,768]{2,1,0:T(2,128)(2,1)}, u32[]{:S(2)}) copy-start(bf16[2,2,768]{2,1,0:T(2,128)(2,1)} %param.26) | copy-start | bytes 18436
  60.5 16.4 %collective-permute-start.2 = (bf16[768,384]{1,0:T(8,128)(2,1)}, bf16[768,384]{1,0:T(8,128)(2,1)S(1)}, u32[]{:S(2)}, u32[]{:S(2)}) collective-permute-start(bf16[768,384]{1,0:T(8,128)(2,1)} %collective-permute-done.refs_10_), channel_id=1, source_target_pairs={{0,4},{1,5},{2,6},{3,7},{4,0},{5,1},{6,2},{7,3},{8,12},{9,13},{10,... | collective-permute-start | bytes 1769480 | tf_op jit(solution)/shard_map/ppermute | solution.py:504
  62.5 47.7 %collective-permute-start.7 = (bf16[1536,384]{1,0:T(8,128)(2,1)}, bf16[1536,384]{1,0:T(8,128)(2,1)}, u32[]{:S(2)}, u32[]{:S(2)}) collective-permute-start(bf16[1536,384]{1,0:T(8,128)(2,1)} %collective-permute-done.5.refs_8_.refs_12_), channel_id=1, source_target_pairs={{0,4},{1,5},{2,6},{3,7},{4,0},{5,1},{6,2},{7,3},{8,12},{9,13},{10,... | collective-permute-start | bytes 3538952 | tf_op jit(solution)/shard_map/ppermute | solution.py:504
  63.2 15.6 %collective-permute-start.1 = (bf16[768,384]{1,0:T(8,128)(2,1)}, bf16[768,384]{1,0:T(8,128)(2,1)S(1)}, u32[]{:S(2)}, u32[]{:S(2)}) collective-permute-start(bf16[768,384]{1,0:T(8,128)(2,1)} %collective-permute-done.refs_10_), channel_id=1, source_target_pairs={{0,2},{1,3},{2,0},{3,1},{4,6},{5,7},{6,4},{7,5},{8,10},{9,11},{10,... | collective-permute-start | bytes 1769480 | tf_op jit(solution)/shard_map/ppermute | solution.py:504
  76.9 33.9 %copy-start.22 = (bf16[768,384]{1,0:T(8,128)(2,1)}, bf16[768,384]{1,0:T(8,128)(2,1)S(1)}, u32[]{:S(2)}) copy-start(bf16[768,384]{1,0:T(8,128)(2,1)S(1)} %collective-permute-done.2.refs_12_) | copy-start | bytes 1769476
  76.9 33.9 %collective-permute-start.3 = (bf16[768,384]{1,0:T(8,128)(2,1)S(1)}, bf16[768,384]{1,0:T(8,128)(2,1)S(1)}, u32[]{:S(2)}, u32[]{:S(2)}) collective-permute-start(bf16[768,384]{1,0:T(8,128)(2,1)S(1)} %collective-permute-done.2.refs_12_), channel_id=1, source_target_pairs={{0,2},{1,3},{2,0},{3,1},{4,6},{5,7},{6,4},{7,5},{8,10},{9,11},{10,... | collective-permute-start | bytes 1769480 | tf_op jit(solution)/shard_map/ppermute | solution.py:504
  78.8 7.3 %copy-start.23 = (bf16[768,384]{1,0:T(8,128)(2,1)}, bf16[768,384]{1,0:T(8,128)(2,1)S(1)}, u32[]{:S(2)}) copy-start(bf16[768,384]{1,0:T(8,128)(2,1)S(1)} %collective-permute-done.1.refs_11_) | copy-start | bytes 1769476
  78.8 54.2 %collective-permute-start.6 = (bf16[1536,384]{1,0:T(8,128)(2,1)}, bf16[1536,384]{1,0:T(8,128)(2,1)}, u32[]{:S(2)}, u32[]{:S(2)}) collective-permute-start(bf16[1536,384]{1,0:T(8,128)(2,1)} %collective-permute-done.5.refs_8_.refs_12_), channel_id=1, source_target_pairs={{0,2},{1,3},{2,0},{3,1},{4,6},{5,7},{6,4},{7,5},{8,10},{9,11},{10,... | collective-permute-start | bytes 3538952 | tf_op jit(solution)/shard_map/ppermute | solution.py:504
  84.1 49.0 %collective-permute-start.11 = (bf16[1536,384]{1,0:T(8,128)(2,1)}, bf16[1536,384]{1,0:T(8,128)(2,1)}, u32[]{:S(2)}, u32[]{:S(2)}) collective-permute-start(bf16[1536,384]{1,0:T(8,128)(2,1)} %collective-permute-done.9.part0), channel_id=1, source_target_pairs={{0,4},{1,5},{2,6},{3,7},{4,0},{5,1},{6,2},{7,3},{8,12},{9,13},{10,... | collective-permute-start | bytes 3538952 | tf_op jit(solution)/shard_map/ppermute | solution.py:504
  108.5 41.7 %collective-permute-start.15 = (bf16[1536,384]{1,0:T(8,128)(2,1)}, bf16[1536,384]{1,0:T(8,128)(2,1)S(1)}, u32[]{:S(2)}, u32[]{:S(2)}) collective-permute-start(bf16[1536,384]{1,0:T(8,128)(2,1)} %collective-permute-done.13.part0), channel_id=1, source_target_pairs={{0,4},{1,5},{2,6},{3,7},{4,0},{5,1},{6,2},{7,3},{8,12},{9,13},{10,... | collective-permute-start | bytes 3538952 | tf_op jit(solution)/shard_map/ppermute | solution.py:504
  110.2 40.0 %collective-permute-start.8 = (bf16[1536,384]{1,0:T(8,128)(2,1)}, bf16[1536,384]{1,0:T(8,128)(2,1)S(1)}, u32[]{:S(2)}, u32[]{:S(2)}) collective-permute-start(bf16[1536,384]{1,0:T(8,128)(2,1)} %collective-permute-done.7.refs_10_.refs_14_), channel_id=1, source_target_pairs={{0,2},{1,3},{2,0},{3,1},{4,6},{5,7},{6,4},{7,5},{8,10},{9,11},{10,... | collective-permute-start | bytes 3538952 | tf_op jit(solution)/shard_map/ppermute | solution.py:504
  111.7 69.8 %collective-permute-start.10 = (bf16[1536,384]{1,0:T(8,128)(2,1)}, bf16[1536,384]{1,0:T(8,128)(2,1)}, u32[]{:S(2)}, u32[]{:S(2)}) collective-permute-start(bf16[1536,384]{1,0:T(8,128)(2,1)} %collective-permute-done.9.part0), channel_id=1, source_target_pairs={{0,2},{1,3},{2,0},{3,1},{4,6},{5,7},{6,4},{7,5},{8,10},{9,11},{10,... | collective-permute-start | bytes 3538952 | tf_op jit(solution)/shard_map/ppermute | solution.py:504
  133.0 75.6 %collective-permute-start.14 = (bf16[1536,384]{1,0:T(8,128)(2,1)}, bf16[1536,384]{1,0:T(8,128)(2,1)}, u32[]{:S(2)}, u32[]{:S(2)}) collective-permute-start(bf16[1536,384]{1,0:T(8,128)(2,1)} %collective-permute-done.13.part0), channel_id=1, source_target_pairs={{0,2},{1,3},{2,0},{3,1},{4,6},{5,7},{6,4},{7,5},{8,10},{9,11},{10,... | collective-permute-start | bytes 3538952 | tf_op jit(solution)/shard_map/ppermute | solution.py:504
  133.1 48.4 %collective-permute-start.12 = (bf16[1536,384]{1,0:T(8,128)(2,1)}, bf16[1536,384]{1,0:T(8,128)(2,1)}, u32[]{:S(2)}, u32[]{:S(2)}) collective-permute-start(bf16[1536,384]{1,0:T(8,128)(2,1)} %collective-permute-done.11.part2), channel_id=1, source_target_pairs={{0,2},{1,3},{2,0},{3,1},{4,6},{5,7},{6,4},{7,5},{8,10},{9,11},{10,... | collective-permute-start | bytes 3538952 | tf_op jit(solution)/shard_map/ppermute | solution.py:504
  150.2 31.3 %copy-start.21 = (bf16[1536,384]{1,0:T(8,128)(2,1)}, bf16[1536,384]{1,0:T(8,128)(2,1)S(1)}, u32[]{:S(2)}) copy-start(bf16[1536,384]{1,0:T(8,128)(2,1)S(1)} %collective-permute-done.15.part2) | copy-start | bytes 3538948
  150.2 58.4 %collective-permute-start.16 = (bf16[1536,384]{1,0:T(8,128)(2,1)S(1)}, bf16[1536,384]{1,0:T(8,128)(2,1)}, u32[]{:S(2)}, u32[]{:S(2)}) collective-permute-start(bf16[1536,384]{1,0:T(8,128)(2,1)S(1)} %collective-permute-done.15.part2), channel_id=1, source_target_pairs={{0,2},{1,3},{2,0},{3,1},{4,6},{5,7},{6,4},{7,5},{8,10},{9,11},{10,... | collective-permute-start | bytes 3538952 | tf_op jit(solution)/shard_map/ppermute | solution.py:504
  329.8 16.1 %copy-start.11 = (f32[1,3072]{1,0:T(1,128)S(1)}, f32[1,3072]{1,0:T(1,128)}, u32[]{:S(2)}) copy-start(f32[1,3072]{1,0:T(1,128)} %get-tuple-element.125) | copy-start | bytes 36868
  329.8 16.1 %copy-start.12 = (f32[1,3072]{1,0:T(1,128)S(1)}, f32[1,3072]{1,0:T(1,128)}, u32[]{:S(2)}) copy-start(f32[1,3072]{1,0:T(1,128)} %get-tuple-element.126) | copy-start | bytes 36868
  329.8 16.5 %copy-start.17 = (f32[1,2304]{1,0:T(1,128)S(1)}, f32[1,2304]{1,0:T(1,128)}, u32[]{:S(2)}) copy-start(f32[1,2304]{1,0:T(1,128)} %get-tuple-element.121) | copy-start | bytes 27652
  329.8 16.5 %copy-start.18 = (f32[1,2304]{1,0:T(1,128)S(1)}, f32[1,2304]{1,0:T(1,128)}, u32[]{:S(2)}) copy-start(f32[1,2304]{1,0:T(1,128)} %get-tuple-element.122) | copy-start | bytes 27652
  329.8 16.6 %copy-start.16 = (f32[1,2304]{1,0:T(1,128)S(1)}, f32[1,2304]{1,0:T(1,128)}, u32[]{:S(2)}) copy-start(f32[1,2304]{1,0:T(1,128)} %get-tuple-element.123) | copy-start | bytes 27652
  329.8 16.6 %copy-start.15 = (f32[1,2304]{1,0:T(1,128)S(1)}, f32[1,2304]{1,0:T(1,128)}, u32[]{:S(2)}) copy-start(f32[1,2304]{1,0:T(1,128)} %get-tuple-element.124) | copy-start | bytes 27652
  329.8 16.9 %copy-start.9 = (f32[8,768]{1,0:T(8,128)S(1)}, f32[8,768]{1,0:T(8,128)}, u32[]{:S(2)}) copy-start(f32[8,768]{1,0:T(8,128)} %get-tuple-element.129) | copy-start | bytes 73732
  329.8 16.9 %copy-start.8 = (f32[8,768]{1,0:T(8,128)S(1)}, f32[8,768]{1,0:T(8,128)}, u32[]{:S(2)}) copy-start(f32[8,768]{1,0:T(8,128)} %get-tuple-element.128) | copy-start | bytes 73732
  344.7 6.1 collective-permute-start.17
  353.2 3.7 copy-start.4
  353.2 3.7 copy-start.2
  353.2 3.8 copy-start.3
  355.4 46.2 %collective-permute-start.18 = (bf16[2,2,2,48,1536]{4,3,0,1,2:T(8,128)(2,1)S(1)}, bf16[2,2,2,48,1536]{4,3,0,1,2:T(8,128)(2,1)S(1)}, u32[]{:S(2)}, u32[]{:S(2)}) collective-permute-start(bf16[2,2,2,48,1536]{4,3,0,1,2:T(8,128)(2,1)S(1)} %copy.46), channel_id=1, source_target_pairs={{0,1},{1,0},{2,3},{3,2},{4,5},{5,4},{6,7},{7,6},{8,9},{9,8},{10,11... | collective-permute-start | bytes 3538952 | tf_op jit(solution)/shard_map/ppermute | solution.py:498
  357.0 28.2 %collective-permute-start.27 = (f32[22272]{0:T(1024)S(1)}, f32[22272]{0:T(1024)S(1)}, u32[]{:S(2)}, u32[]{:S(2)}) collective-permute-start(f32[22272]{0:T(1024)S(1)} %constant_dynamic-update-slice_fusion.21), channel_id=1, source_target_pairs={{0,1},{1,0},{2,3},{3,2},{4,5},{5,4},{6,7},{7,6},{8,9},{9,8},{10,11... | collective-permute-start | bytes 267272 | tf_op jit(solution)/shard_map/ppermute | solution.py:498
  385.2 1.4 collective-permute-start.28
  386.6 12.7 %collective-permute-start.29 = (f32[22272]{0:T(1024)S(1)}, f32[22272]{0:T(1024)S(1)}, u32[]{:S(2)}, u32[]{:S(2)}) collective-permute-start(f32[22272]{0:T(1024)S(1)} %add.138), channel_id=1, source_target_pairs={{0,4},{1,5},{2,6},{3,7},{4,0},{5,1},{6,2},{7,3},{8,12},{9,13},{10,... | collective-permute-start | bytes 267272 | tf_op jit(solution)/shard_map/ppermute | solution.py:504
  399.3 55.6 %collective-permute-start.32 = (bf16[2,8,48,3072]{3,2,1,0:T(8,128)(2,1)}, bf16[2,8,48,3072]{3,2,1,0:T(8,128)(2,1)}, u32[]{:S(2)}, u32[]{:S(2)}) collective-permute-start(bf16[2,8,48,3072]{3,2,1,0:T(8,128)(2,1)} %get-tuple-element.134), channel_id=1, source_target_pairs={{0,2},{1,3},{2,0},{3,1},{4,6},{5,7},{6,4},{7,5},{8,10},{9,11},{10,... | collective-permute-start | bytes 14155784 | tf_op jit(solution)/shard_map/ppermute | solution.py:504
  399.9 19.8 %collective-permute-start.30 = (f32[22272]{0:T(1024)}, f32[22272]{0:T(1024)}, u32[]{:S(2)}, u32[]{:S(2)}) collective-permute-start(f32[22272]{0:T(1024)} %add.139), channel_id=1, source_target_pairs={{0,8},{1,9},{2,10},{3,11},{4,12},{5,13},{6,14},{7,15},{8,0},{9,1},... | collective-permute-start | bytes 267272 | tf_op jit(solution)/shard_map/ppermute | solution.py:504
  402.0 21.9 %collective-permute-start.19 = (bf16[2,2,48,1536]{3,2,0,1:T(8,128)(2,1)S(1)}, bf16[2,2,48,1536]{3,2,0,1:T(8,128)(2,1)}, u32[]{:S(2)}, u32[]{:S(2)}) collective-permute-start(bf16[2,2,48,1536]{3,2,0,1:T(8,128)(2,1)S(1)} %fusion.14), channel_id=1, source_target_pairs={{0,4},{1,5},{2,6},{3,7},{4,0},{5,1},{6,2},{7,3},{8,12},{9,13},{10,... | collective-permute-start | bytes 1769480 | tf_op jit(solution)/shard_map/ppermute | solution.py:504
  419.5 44.4 %collective-permute-start.37 = (bf16[2,8,48,3072]{3,2,1,0:T(8,128)(2,1)}, bf16[2,8,48,3072]{3,2,1,0:T(8,128)(2,1)}, u32[]{:S(2)}, u32[]{:S(2)}) collective-permute-start(bf16[2,8,48,3072]{3,2,1,0:T(8,128)(2,1)} %get-tuple-element.139), channel_id=1, source_target_pairs={{0,2},{1,3},{2,0},{3,1},{4,6},{5,7},{6,4},{7,5},{8,10},{9,11},{10,... | collective-permute-start | bytes 14155784 | tf_op jit(solution)/shard_map/ppermute | solution.py:504
  421.3 22.0 %collective-permute-start.31 = (f32[22272]{0:T(1024)}, f32[22272]{0:T(1024)}, u32[]{:S(2)}, u32[]{:S(2)}) collective-permute-start(f32[22272]{0:T(1024)} %add.140), channel_id=1, source_target_pairs={{0,16},{1,17},{2,18},{3,19},{4,20},{5,21},{6,22},{7,23},{8,24},{9,... | collective-permute-start | bytes 267272 | tf_op jit(solution)/shard_map/ppermute | solution.py:504
  425.1 19.2 %collective-permute-start.20 = (bf16[2,48,1536]{2,1,0:T(8,128)(2,1)S(1)}, bf16[2,48,1536]{2,1,0:T(8,128)(2,1)S(1)}, u32[]{:S(2)}, u32[]{:S(2)}) collective-permute-start(bf16[2,48,1536]{2,1,0:T(8,128)(2,1)S(1)} %fusion.22), channel_id=1, source_target_pairs={{0,8},{1,9},{2,10},{3,11},{4,12},{5,13},{6,14},{7,15},{8,0},{9,1},... | collective-permute-start | bytes 884744 | tf_op jit(solution)/shard_map/ppermute | solution.py:504
  443.3 33.2 %collective-permute-start.22 = (bf16[2,8,48,3072]{3,2,1,0:T(8,128)(2,1)}, bf16[2,8,48,3072]{3,2,1,0:T(8,128)(2,1)}, u32[]{:S(2)}, u32[]{:S(2)}) collective-permute-start(bf16[2,8,48,3072]{3,2,1,0:T(8,128)(2,1)} %get-tuple-element.120), channel_id=1, source_target_pairs={{0,2},{1,3},{2,0},{3,1},{4,6},{5,7},{6,4},{7,5},{8,10},{9,11},{10,... | collective-permute-start | bytes 14155784 | tf_op jit(solution)/shard_map/ppermute | solution.py:504
  444.5 10.2 %collective-permute-start.21 = (bf16[48,1536]{1,0:T(8,128)(2,1)S(1)}, bf16[48,1536]{1,0:T(8,128)(2,1)S(1)}, u32[]{:S(2)}, u32[]{:S(2)}) collective-permute-start(bf16[48,1536]{1,0:T(8,128)(2,1)S(1)} %fusion.27), channel_id=1, source_target_pairs={{0,16},{1,17},{2,18},{3,19},{4,20},{5,21},{6,22},{7,23},{8,24},{9,... | collective-permute-start | bytes 442376 | tf_op jit(solution)/shard_map/ppermute | solution.py:504
  462.5 53.5 %collective-permute-start.33 = (bf16[2,2,2,48,3072]{4,3,1,2,0:T(8,128)(2,1)}, bf16[2,2,2,48,3072]{4,3,1,2,0:T(8,128)(2,1)}, u32[]{:S(2)}, u32[]{:S(2)}) collective-permute-start(bf16[2,2,2,48,3072]{4,3,1,2,0:T(8,128)(2,1)} %fusion.3), channel_id=1, source_target_pairs={{0,4},{1,5},{2,6},{3,7},{4,0},{5,1},{6,2},{7,3},{8,12},{9,13},{10,... | collective-permute-start | bytes 7077896 | tf_op jit(solution)/shard_map/ppermute | solution.py:504
  469.7 3.7 copy-start
  475.0 54.4 %collective-permute-start.38 = (bf16[2,2,2,48,3072]{4,3,0,1,2:T(8,128)(2,1)}, bf16[2,2,2,48,3072]{4,3,0,1,2:T(8,128)(2,1)}, u32[]{:S(2)}, u32[]{:S(2)}) collective-permute-start(bf16[2,2,2,48,3072]{4,3,0,1,2:T(8,128)(2,1)} %copy.53), channel_id=1, source_target_pairs={{0,1},{1,0},{2,3},{3,2},{4,5},{5,4},{6,7},{7,6},{8,9},{9,8},{10,11... | collective-permute-start | bytes 7077896 | tf_op jit(solution)/shard_map/ppermute | solution.py:498
  484.0 53.0 %collective-permute-start.23 = (bf16[2,2,2,48,3072]{4,3,1,2,0:T(8,128)(2,1)}, bf16[2,2,2,48,3072]{4,3,1,2,0:T(8,128)(2,1)}, u32[]{:S(2)}, u32[]{:S(2)}) collective-permute-start(bf16[2,2,2,48,3072]{4,3,1,2,0:T(8,128)(2,1)} %fusion.2), channel_id=1, source_target_pairs={{0,8},{1,9},{2,10},{3,11},{4,12},{5,13},{6,14},{7,15},{8,0},{9,1},... | collective-permute-start | bytes 7077896 | tf_op jit(solution)/shard_map/ppermute | solution.py:504
  516.0 13.4 %slice-start = ((f32[2,8,48,3072]{3,2,1,0:T(8,128)}), f32[1,8,48,3072]{3,2,1,0:T(8,128)S(1)}, s32[]{:S(2)}) async-start(f32[2,8,48,3072]{3,2,1,0:T(8,128)} %copy-done), calls=%async_computation | async-start | bytes 9437184 | tf_op jit(solution)/shard_map/slice | solution.py:530
  519.0 35.6 %collective-permute-start.34 = (bf16[2,2,48,3072]{3,2,0,1:T(8,128)(2,1)S(1)}, bf16[2,2,48,3072]{3,2,0,1:T(8,128)(2,1)S(1)}, u32[]{:S(2)}, u32[]{:S(2)}) collective-permute-start(bf16[2,2,48,3072]{3,2,0,1:T(8,128)(2,1)S(1)} %fusion.8), channel_id=1, source_target_pairs={{0,1},{1,0},{2,3},{3,2},{4,5},{5,4},{6,7},{7,6},{8,9},{9,8},{10,11... | collective-permute-start | bytes 3538952 | tf_op jit(solution)/shard_map/ppermute | solution.py:498
  532.2 25.7 %collective-permute-start.39 = (bf16[2,2,48,3072]{3,2,0,1:T(8,128)(2,1)S(1)}, bf16[2,2,48,3072]{3,2,0,1:T(8,128)(2,1)S(1)}, u32[]{:S(2)}, u32[]{:S(2)}) collective-permute-start(bf16[2,2,48,3072]{3,2,0,1:T(8,128)(2,1)S(1)} %fusion.9), channel_id=1, source_target_pairs={{0,4},{1,5},{2,6},{3,7},{4,0},{5,1},{6,2},{7,3},{8,12},{9,13},{10,... | collective-permute-start | bytes 3538952 | tf_op jit(solution)/shard_map/ppermute | solution.py:504
  539.8 38.9 %collective-permute-start.24 = (bf16[2,2,48,3072]{3,2,0,1:T(8,128)(2,1)S(1)}, bf16[2,2,48,3072]{3,2,0,1:T(8,128)(2,1)S(1)}, u32[]{:S(2)}, u32[]{:S(2)}) collective-permute-start(bf16[2,2,48,3072]{3,2,0,1:T(8,128)(2,1)S(1)} %fusion.7), channel_id=1, source_target_pairs={{0,1},{1,0},{2,3},{3,2},{4,5},{5,4},{6,7},{7,6},{8,9},{9,8},{10,11... | collective-permute-start | bytes 3538952 | tf_op jit(solution)/shard_map/ppermute | solution.py:498
  555.0 24.7 %collective-permute-start.35 = (bf16[2,48,3072]{2,1,0:T(8,128)(2,1)S(1)}, bf16[2,48,3072]{2,1,0:T(8,128)(2,1)S(1)}, u32[]{:S(2)}, u32[]{:S(2)}) collective-permute-start(bf16[2,48,3072]{2,1,0:T(8,128)(2,1)S(1)} %fusion.16), channel_id=1, source_target_pairs={{0,8},{1,9},{2,10},{3,11},{4,12},{5,13},{6,14},{7,15},{8,0},{9,1},... | collective-permute-start | bytes 1769480 | tf_op jit(solution)/shard_map/ppermute | solution.py:504
  558.3 22.4 %collective-permute-start.40 = (bf16[2,48,3072]{2,1,0:T(8,128)(2,1)S(1)}, bf16[2,48,3072]{2,1,0:T(8,128)(2,1)S(1)}, u32[]{:S(2)}, u32[]{:S(2)}) collective-permute-start(bf16[2,48,3072]{2,1,0:T(8,128)(2,1)S(1)} %fusion.17), channel_id=1, source_target_pairs={{0,8},{1,9},{2,10},{3,11},{4,12},{5,13},{6,14},{7,15},{8,0},{9,1},... | collective-permute-start | bytes 1769480 | tf_op jit(solution)/shard_map/ppermute | solution.py:504
  579.1 14.2 %collective-permute-start.25 = (bf16[2,48,3072]{2,1,0:T(8,128)(2,1)S(1)}, bf16[2,48,3072]{2,1,0:T(8,128)(2,1)S(1)}, u32[]{:S(2)}, u32[]{:S(2)}) collective-permute-start(bf16[2,48,3072]{2,1,0:T(8,128)(2,1)S(1)} %fusion.15), channel_id=1, source_target_pairs={{0,4},{1,5},{2,6},{3,7},{4,0},{5,1},{6,2},{7,3},{8,12},{9,13},{10,... | collective-permute-start | bytes 1769480 | tf_op jit(solution)/shard_map/ppermute | solution.py:504
  579.9 25.2 %collective-permute-start.36 = (bf16[48,3072]{1,0:T(8,128)(2,1)S(1)}, bf16[48,3072]{1,0:T(8,128)(2,1)S(1)}, u32[]{:S(2)}, u32[]{:S(2)}) collective-permute-start(bf16[48,3072]{1,0:T(8,128)(2,1)S(1)} %fusion.24), channel_id=1, source_target_pairs={{0,16},{1,17},{2,18},{3,19},{4,20},{5,21},{6,22},{7,23},{8,24},{9,... | collective-permute-start | bytes 884744 | tf_op jit(solution)/shard_map/ppermute | solution.py:504
  580.9 36.8 %collective-permute-start.41 = (bf16[48,3072]{1,0:T(8,128)(2,1)S(1)}, bf16[48,3072]{1,0:T(8,128)(2,1)S(1)}, u32[]{:S(2)}, u32[]{:S(2)}) collective-permute-start(bf16[48,3072]{1,0:T(8,128)(2,1)S(1)} %fusion.25), channel_id=1, source_target_pairs={{0,16},{1,17},{2,18},{3,19},{4,20},{5,21},{6,22},{7,23},{8,24},{9,... | collective-permute-start | bytes 884744 | tf_op jit(solution)/shard_map/ppermute | solution.py:504
  593.5 24.0 %collective-permute-start.26 = (bf16[48,3072]{1,0:T(8,128)(2,1)S(1)}, bf16[48,3072]{1,0:T(8,128)(2,1)S(1)}, u32[]{:S(2)}, u32[]{:S(2)}) collective-permute-start(bf16[48,3072]{1,0:T(8,128)(2,1)S(1)} %fusion.23), channel_id=1, source_target_pairs={{0,16},{1,17},{2,18},{3,19},{4,20},{5,21},{6,22},{7,23},{8,24},{9,... | collective-permute-start | bytes 884744 | tf_op jit(solution)/shard_map/ppermute | solution.py:504
  (6 other events, 11.9 us)
